TPU v7x, 256 devices: a whole 4x4x8 slice. The times are simulated.
256 devices in a mesh: slab: 32 (over z_hi, x, y), pencil: 8 (over z_lo, core).
Axes of the slice: x: 4, y: 4, z: 8 (z_hi: 2, z_lo: 4; z = z_hi * 4 + z_lo), core: 2. Of those that a mesh axis runs over, the one named last changes fastest.
Arguments:
- adjoint_vort: float32 [3, 64, 512, 512], P(None, 'slab', 'pencil'), may hold values from -6 to 6
- omega_ckpt: float32 [2, 3, 64, 512, 512], P(None, None, 'slab', 'pencil'), may hold values from -6 to 6
- cell_shift: int32 [2, 64, 512, 512], P(None, 'slab', 'pencil'), may hold values from -2 to 2
- move_count: int32 [2, 32, 8, 2], P(None, 'slab', 'pencil'), may hold values from 16 to 128, as said below
- move_blocks: int32 [2, 32, 8, 2, 128], P(None, 'slab', 'pencil'), may hold values from 0 to 255, as said below
Outputs:
- adjoint_out: float32 [3, 64, 512, 512], P(None, 'slab', 'pencil')
Inputs may be any that keep to these rules, and one draw needn't show every extreme that they name: `move_count`: in every substep and direction some device has 128 live entries and some device 128 // 8. `move_blocks`: for each substep and device, the 256 entries are the plane-block numbers 0 to 255, each once.
All inputs are finite; a program needn't handle non-finite values.
Results may differ from a plain program's by a relative error of at most 0.00025.
Values sent between devices are 32-bit elements; how exact they have to be, the bound alone decides.
No kernel may reach another device: no remote copies, remote signals or barrier semaphores. Data moves between devices by JAX's collectives and lax.ppermute only.
A program may use at most 64 MiB of HBM per device.

v0:
```python
import math

import jax
import jax.numpy as jnp
from jax import lax
from jax.sharding import PartitionSpec as P

NY = 512
BL = 128


time_step = 0.25
highest = lax.Precision.HIGHEST


def shifted(value, axis, by):
    count = lax.axis_size(axis)
    return lax.ppermute(value, axis, [(i, (i + by) % count) for i in range(count)])


def padded_2(cells, sides, width):
    for axis, dim in sides:
        count = lax.axis_size(axis)
        head = lax.slice_in_dim(cells, 0, width, axis=dim)
        tail = lax.slice_in_dim(cells, cells.shape[dim] - width, cells.shape[dim], axis=dim)
        cells = jnp.concatenate(
            [
                lax.ppermute(tail, axis, [(i, (i + 1) % count) for i in range(count)]),
                cells,
                lax.ppermute(head, axis, [((i + 1) % count, i) for i in range(count)]),
            ],
            axis=dim,
        )
    return cells


def cross_product(first_vec, second_vec):
    return jnp.stack(
        [
            first_vec[1] * second_vec[2] - first_vec[2] * second_vec[1],
            first_vec[2] * second_vec[0] - first_vec[0] * second_vec[2],
            first_vec[0] * second_vec[1] - first_vec[1] * second_vec[0],
        ],
        0,
    )


def phase_table(length):
    wave_index = jnp.arange(length, dtype=jnp.int32)
    products = wave_index[:, None] * wave_index[None, :] % length
    return products.astype(jnp.float32) * (2.0 * math.pi / length)


def cas_plain(length):
    phases = phase_table(length)
    return jnp.cos(phases) + jnp.sin(phases)


def cas_slope(length):
    phases = phase_table(length)
    angle_step = jnp.arange(length, dtype=jnp.int32).astype(jnp.float32) * (2.0 * math.pi / length)
    return jnp.sin(angle_step)[:, None] * (jnp.cos(phases) - jnp.sin(phases)) / length


def inverse_factor(wave_y, wave_z, length_y, length_z):
    sine_y = jnp.sin(math.pi * wave_y.astype(jnp.float32) / length_y)
    sine_z = jnp.sin(math.pi * wave_z.astype(jnp.float32) / length_z)
    symbol = 4.0 * sine_y * sine_y + 4.0 * sine_z * sine_z
    nonzero = wave_y + wave_z > 0
    return jnp.where(nonzero, 1.0 / jnp.where(nonzero, symbol, 1.0), 0.0)


def shifted_deposit(values, shifts):
    total = jnp.zeros(values.shape, jnp.float32)
    for amount in (-2, -1, 0, 1, 2):
        picked = jnp.where(shifts == amount, values, 0.0)
        total = total + jnp.roll(picked, amount, axis=-1)
    return total


def velocity(source):
    planes = source.shape[1]
    local_rows = source.shape[2]
    depth_cells = source.shape[3]
    width_cells = NY
    groups = lax.axis_size("pencil")
    forward_z = cas_plain(depth_cells)
    forward_y = cas_plain(width_cells)
    plain_z = forward_z / depth_cells
    slope_z = cas_slope(depth_cells)
    plain_y = forward_y / width_cells
    slope_y = cas_slope(width_cells)
    kz_block = depth_cells // groups
    along_z = jnp.einsum("cxyz,zk->xcky", source, forward_z, precision=highest)
    along_z = along_z.reshape(planes, 3, groups, kz_block * local_rows)
    received = lax.all_to_all(along_z, "pencil", split_axis=2, concat_axis=2, tiled=True)
    item_count = received.shape[0]
    received_blocks = received.reshape(item_count, 3, groups, kz_block, local_rows)
    spectrum = jnp.einsum(
        "ncqkr,qrm->nckm",
        received_blocks,
        forward_y.reshape(groups, local_rows, width_cells),
        precision=highest,
    )
    wave_z = lax.axis_index("pencil") * kz_block + jnp.arange(kz_block, dtype=jnp.int32)
    wave_y = jnp.arange(width_cells, dtype=jnp.int32)
    stream = spectrum * inverse_factor(wave_y[None, :], wave_z[:, None], width_cells, depth_cells)
    plain_rows = plain_y.reshape(width_cells, groups, local_rows)
    slope_rows = slope_y.reshape(width_cells, groups, local_rows)
    pieces = [
        jnp.einsum("nkm,mqr->nqkr", stream[:, 2], slope_rows, precision=highest),
        jnp.einsum("nkm,mqr->nqkr", stream[:, 1], plain_rows, precision=highest),
        jnp.einsum("nkm,mqr->nqkr", stream[:, 0], plain_rows, precision=highest),
        jnp.einsum("nkm,mqr->nqkr", stream[:, 0], slope_rows, precision=highest),
    ]
    outgoing = jnp.stack(pieces, 1).reshape(item_count, 4, groups, kz_block * local_rows)
    returned = lax.all_to_all(outgoing, "pencil", split_axis=2, concat_axis=2, tiled=True)
    returned = returned.reshape(planes, 4, depth_cells, local_rows)
    pattern = "xky,kz->xyz"
    pieces = [returned[:, member] for member in range(4)]
    first_part = jnp.einsum(pattern, pieces[0], plain_z, precision=highest) - jnp.einsum(
        pattern, pieces[1], slope_z, precision=highest
    )
    second = jnp.einsum(pattern, pieces[2], slope_z, precision=highest)
    third_part = -jnp.einsum(pattern, pieces[3], plain_z, precision=highest)
    return jnp.stack([first_part, second, third_part], 0)


def shards(adjoint_vort, omega_ckpt, cell_shift, move_count, move_blocks):
    planes = adjoint_vort.shape[1]
    local_rows = adjoint_vort.shape[2]
    depth_cells = adjoint_vort.shape[3]
    per_row = depth_cells // BL
    plane_blocks = local_rows * per_row
    all_blocks = planes * plane_blocks
    capacity = move_blocks.shape[-1]
    block_id = jnp.arange(all_blocks, dtype=jnp.int32)
    slot_id = jnp.arange(capacity, dtype=jnp.int32)

    def cell_mask(block_mask):
        spread = jnp.broadcast_to(
            block_mask.reshape(planes, local_rows, per_row, 1), (planes, local_rows, per_row, BL)
        )
        return spread.reshape(planes, local_rows, depth_cells)

    adjoint = adjoint_vort
    for substep in range(omega_ckpt.shape[0]):
        shifts = cell_shift[substep]
        payload = jnp.concatenate([adjoint, omega_ckpt[substep]], 0)
        chosen = move_blocks[substep, 0, 0]
        alive_slot = slot_id[None, :] < move_count[substep, 0, 0][:, None]
        right_ids = (planes - 1) * plane_blocks + chosen[0]
        left_ids = chosen[1]
        right_hit = jnp.any(
            (block_id[:, None] == right_ids[None, :]) & alive_slot[0][None, :], axis=1
        )
        left_hit = jnp.any(
            (block_id[:, None] == left_ids[None, :]) & alive_slot[1][None, :], axis=1
        )
        right_cells = cell_mask(right_hit)
        left_cells = cell_mask(left_hit)
        staying = jnp.where(right_cells | left_cells, 0.0, payload)
        deposit = shifted_deposit(staying, shifts)
        right_plane = shifted_deposit(
            jnp.where(right_cells[planes - 1], payload[:, planes - 1], 0.0), shifts[planes - 1]
        )
        left_plane = shifted_deposit(jnp.where(left_cells[0], payload[:, 0], 0.0), shifts[0])
        from_left = shifted(right_plane, "slab", 1)
        from_right = shifted(left_plane, "slab", -1)
        deposit = deposit.at[:, 0].add(from_left)
        deposit = deposit.at[:, planes - 1].add(from_right)
        remeshed = deposit[:3]
        vortex = deposit[3:]
        velocity_field = velocity(remeshed)
        padded = padded_2(velocity_field, (("slab", 1),), 1)
        slope_x = (padded[:, 2:] - padded[:, :-2]) * 0.5
        adjoint = remeshed + time_step * (
            cross_product(vortex, velocity_field) + vortex[0] * slope_x
        )
    return adjoint


def solution(mesh):
    return jax.shard_map(
        shards,
        mesh=mesh,
        in_specs=(
            P(None, "slab", "pencil", None),
            P(None, None, "slab", "pencil", None),
            P(None, "slab", "pencil", None),
            P(None, "slab", "pencil", None),
            P(None, "slab", "pencil", None, None),
        ),
        out_specs=P(None, "slab", "pencil", None),
        check_vma=False,
    )
```

profile of v0, /device:TPU:1, one launch (start us, length us, event | category | flops | bytes accessed | tf_op | source)
XLA Modules:
  0.0 428.0 jit_solution(17264373664423243174)
XLA Ops:
  13.7 10.5 %collective-permute-start.1 = (f32[6,64,512]{2,1,0:T(8,128)}, f32[6,64,512]{2,1,0:T(8,128)}, u32[]{:S(2)}, u32[]{:S(2)}) collective-permute-start(f32[6,64,512]{2,1,0:T(8,128)} %fusion.85), channel_id=1, source_target_pairs={{0,248},{8,0},{16,8},{24,16},{32,24},{40,32},{48,40},{56,48},{64,5... | collective-permute-start | bytes 2359304 | tf_op jit(solution)/shard_map/ppermute | solution.py:18
  28.9 15.5 %collective-permute-done = f32[6,64,512]{2,1,0:T(8,128)} collective-permute-done((f32[6,64,512]{2,1,0:T(8,128)}, f32[6,64,512]{2,1,0:T(8,128)}, u32[]{:S(2)}, u32[]{:S(2)}) %collective-permute-start) | collective-permute-done | bytes 786464 | tf_op jit(solution)/shard_map/ppermute | solution.py:18
  47.2 6.2 %convolution_bitcast_fusion.3 = f32[2,3,512,64]{2,3,0,1:T(8,128)S(1)} fusion(f32[6,2,64,512]{3,2,1,0:T(8,128)S(1)} %fusion.78), kind=kOutput, calls=%fused_computation.29 | convolution fusion | flops 1211891712 | bytes 1572864 | tf_op jit(solution)/shard_map/cxyz,zk->xcky/dot_general | solution.py:94
  58.4 16.5 %all-to-all-start = ((f32[2,3,8,4096]{3,0,1,2:T(2,128)}), f32[2,3,8,4096]{3,0,1,2:T(2,128)S(1)}, u32[]{:S(2)}, u32[]{:S(2)}) async-start(f32[2,3,8,4096]{3,0,1,2:T(2,128)} %copy.119), calls=%async_computation | async-start | bytes 1572864 | tf_op jit(solution)/shard_map/all_to_all | solution.py:96
  75.3 19.7 %all-to-all-done = f32[2,3,8,4096]{3,0,1,2:T(2,128)S(1)} async-done(((f32[2,3,8,4096]{3,0,1,2:T(2,128)}), f32[2,3,8,4096]{3,0,1,2:T(2,128)S(1)}, u32[]{:S(2)}, u32[]{:S(2)}) %all-to-all-start) | async-done | bytes 786464 | tf_op jit(solution)/shard_map/all_to_all | solution.py:96
  99.2 7.2 %fusion.7 = f32[2,3,64,512]{3,2,1,0:T(8,128)S(1)} fusion(f32[2,3,8,64,64]{4,3,2,1,0:T(8,128)} %reshape.635, s32[8,64]{1,0:T(8,128)S(1)} %multiply_add_fusion, f32[64,512]{1,0:T(8,128)S(1)} %divide_select_fusion), kind=kOutput, calls=%fused_computation.30 | convolution fusion | flops 1212088320 | bytes 1705984 | tf_op jit(solution)/shard_map/ncqkr,qrm->nckm/dot_general | solution.py:99
  112.6 6.3 %convolution_bitcast_fusion.10 = f32[2,8,64,64]{2,3,0,1:T(8,128)} fusion(s32[8,64]{1,0:T(8,128)S(1)} %multiply_add_fusion, f32[2,3,64,512]{3,2,1,0:T(8,128)S(1)} %fusion.7), kind=kOutput, calls=%fused_computation.38 | convolution fusion | flops 406847488 | bytes 528384 | tf_op jit(solution)/shard_map/nkm,mqr->nqkr/dot_general | solution.py:112
  124.1 6.4 %convolution_bitcast_fusion.11 = f32[2,8,64,64]{2,3,0,1:T(8,128)} fusion(s32[8,64]{1,0:T(8,128)S(1)} %multiply_add_fusion, f32[512]{0:T(512)S(1)} %multiply_sine_fusion, f32[2,3,64,512]{3,2,1,0:T(8,128)S(1)} %fusion.7), kind=kOutput, calls=%fused_computation.39 | convolution fusion | flops 407109632 | bytes 530432 | tf_op jit(solution)/shard_map/nkm,mqr->nqkr/dot_general | solution.py:111
  146.5 23.8 %all-to-all-done.1 = f32[2,4,8,4096]{3,0,1,2:T(2,128)} async-done(((f32[2,4,8,4096]{3,0,1,2:T(2,128)}), f32[2,4,8,4096]{3,0,1,2:T(2,128)}, u32[]{:S(2)}, u32[]{:S(2)}) %all-to-all-start.1) | async-done | bytes 1048608 | tf_op jit(solution)/shard_map/all_to_all | solution.py:117
  174.3 7.0 %convolution_negate_fusion.1 = f32[2,64,512]{2,1,0:T(8,128)S(1)} fusion(f32[2,4,512,64]{3,2,1,0:T(8,128)} %reshape.636), kind=kOutput, calls=%fused_computation.47 | convolution fusion | flops 406913024 | bytes 786432 | tf_op jit(solution)/shard_map/xky,kz->xyz/dot_general | solution.py:125
  186.7 6.2 %fusion.31 = f32[2,64,512]{2,1,0:T(8,128)S(1)} fusion(f32[2,4,512,64]{3,2,1,0:T(8,128)S(1)} %copy-done.3), kind=kOutput, calls=%fused_computation.72 | convolution fusion | flops 406847488 | bytes 786432 | tf_op jit(solution)/shard_map/xky,kz->xyz/dot_general | solution.py:121
  198.5 10.7 %collective-permute-start.2 = (f32[3,1,64,512]{3,2,1,0:T(8,128)S(1)}, f32[3,1,64,512]{3,2,1,0:T(8,128)S(1)}, u32[]{:S(2)}, u32[]{:S(2)}) collective-permute-start(f32[3,1,64,512]{3,2,1,0:T(8,128)S(1)} %get-tuple-element.89), channel_id=1, source_target_pairs={{8,0},{16,8},{24,16},{32,24},{40,32},{48,40},{56,48},{64,56},{72,6... | collective-permute-start | bytes 1179656 | tf_op jit(solution)/shard_map/ppermute | solution.py:30
  210.4 15.6 %collective-permute-done.3 = f32[3,1,64,512]{3,2,1,0:T(8,128)S(1)} collective-permute-done((f32[3,1,64,512]{3,2,1,0:T(8,128)S(1)}, f32[3,1,64,512]{3,2,1,0:T(8,128)S(1)}, u32[]{:S(2)}, u32[]{:S(2)}) %collective-permute-start.3) | collective-permute-done | bytes 393248 | tf_op jit(solution)/shard_map/ppermute | solution.py:28
  232.4 9.9 %collective-permute-start.5 = (f32[6,64,512]{2,1,0:T(8,128)S(1)}, f32[6,64,512]{2,1,0:T(8,128)S(1)}, u32[]{:S(2)}, u32[]{:S(2)}) collective-permute-start(f32[6,64,512]{2,1,0:T(8,128)S(1)} %fusion.91), channel_id=1, source_target_pairs={{0,248},{8,0},{16,8},{24,16},{32,24},{40,32},{48,40},{56,48},{64,5... | collective-permute-start | bytes 2359304 | tf_op jit(solution)/shard_map/ppermute | solution.py:18
  245.5 25.7 %collective-permute-done.4 = f32[6,64,512]{2,1,0:T(8,128)S(1)} collective-permute-done((f32[6,64,512]{2,1,0:T(8,128)S(1)}, f32[6,64,512]{2,1,0:T(8,128)S(1)}, u32[]{:S(2)}, u32[]{:S(2)}) %collective-permute-start.4) | collective-permute-done | bytes 786464 | tf_op jit(solution)/shard_map/ppermute | solution.py:18
  273.6 6.2 %convolution_bitcast_fusion.1 = f32[2,3,512,64]{2,3,0,1:T(8,128)S(1)} fusion(f32[6,2,64,512]{3,2,0,1:T(8,128)S(1)} %fusion.69), kind=kOutput, calls=%fused_computation.27 | convolution fusion | flops 1211891712 | bytes 1572864 | tf_op jit(solution)/shard_map/cxyz,zk->xcky/dot_general | solution.py:94
  283.9 24.0 %all_to_all.20 = f32[2,3,8,4096]{3,0,1,2:T(2,128)S(1)} all-to-all(f32[2,3,8,4096]{3,0,1,2:T(2,128)S(1)} %copy.136), channel_id=1, replica_groups=mesh['slab'=32,'pencil'=8] {'pencil'}, dimensions={2} | all-to-all | bytes 1572864 | tf_op jit(solution)/shard_map/all_to_all | solution.py:96
  310.2 7.2 %fusion.8 = f32[2,3,64,512]{3,2,1,0:T(8,128)S(1)} fusion(f32[2,3,8,64,64]{4,3,2,1,0:T(8,128)} %reshape.640, s32[8,64]{1,0:T(8,128)S(1)} %multiply_add_fusion, f32[64,512]{1,0:T(8,128)S(1)} %copy-done.19), kind=kOutput, calls=%fused_computation.31 | convolution fusion | flops 1212088320 | bytes 1705984 | tf_op jit(solution)/shard_map/ncqkr,qrm->nckm/dot_general | solution.py:99
  317.5 6.6 %convolution_bitcast_fusion.4 = f32[2,8,64,64]{2,3,0,1:T(8,128)} fusion(s32[8,64]{1,0:T(8,128)S(1)} %multiply_add_fusion, f32[512]{0:T(512)S(1)} %multiply_sine_fusion, f32[2,3,64,512]{3,2,1,0:T(8,128)S(1)} %fusion.8), kind=kOutput, calls=%fused_computation.32 | convolution fusion | flops 407109632 | bytes 530432 | tf_op jit(solution)/shard_map/nkm,mqr->nqkr/dot_general | solution.py:114
  329.3 6.3 %convolution_bitcast_fusion.6 = f32[2,8,64,64]{2,3,0,1:T(8,128)} fusion(s32[8,64]{1,0:T(8,128)S(1)} %multiply_add_fusion, f32[2,3,64,512]{3,2,1,0:T(8,128)S(1)} %fusion.8), kind=kOutput, calls=%fused_computation.34 | convolution fusion | flops 406847488 | bytes 528384 | tf_op jit(solution)/shard_map/nkm,mqr->nqkr/dot_general | solution.py:112
  345.3 29.2 %all_to_all.21 = f32[2,4,8,4096]{3,0,1,2:T(2,128)S(1)} all-to-all(f32[2,4,8,4096]{3,0,1,2:T(2,128)S(1)} %copy.142), channel_id=1, replica_groups=mesh['slab'=32,'pencil'=8] {'pencil'}, dimensions={2} | all-to-all | bytes 2097152 | tf_op jit(solution)/shard_map/all_to_all | solution.py:117
  377.3 7.0 %convolution_negate_fusion = f32[2,64,512]{2,1,0:T(8,128)S(1)} fusion(f32[2,4,512,64]{3,2,1,0:T(8,128)} %reshape.641), kind=kOutput, calls=%fused_computation.46 | convolution fusion | flops 406913024 | bytes 786432 | tf_op jit(solution)/shard_map/xky,kz->xyz/dot_general | solution.py:125
  401.4 10.4 %collective-permute-start.6 = (f32[3,1,64,512]{3,2,1,0:T(8,128)S(1)}, f32[3,1,64,512]{3,2,1,0:T(8,128)S(1)}, u32[]{:S(2)}, u32[]{:S(2)}) collective-permute-start(f32[3,1,64,512]{3,2,1,0:T(8,128)S(1)} %get-tuple-element.84), channel_id=1, source_target_pairs={{8,0},{16,8},{24,16},{32,24},{40,32},{48,40},{56,48},{64,56},{72,6... | collective-permute-start | bytes 1179656 | tf_op jit(solution)/shard_map/ppermute | solution.py:30
  412.0 14.4 %collective-permute-done.7 = f32[3,1,64,512]{3,2,1,0:T(8,128)S(1)} collective-permute-done((f32[3,1,64,512]{3,2,1,0:T(8,128)S(1)}, f32[3,1,64,512]{3,2,1,0:T(8,128)S(1)}, u32[]{:S(2)}, u32[]{:S(2)}) %collective-permute-start.7) | collective-permute-done | bytes 393248 | tf_op jit(solution)/shard_map/ppermute | solution.py:28
  (196 shorter events, 128.1 us)
Async XLA Ops:
  3.0 1.0 copy-start.1
  3.0 2.9 copy-start
  8.9 35.5 %collective-permute-start = (f32[6,64,512]{2,1,0:T(8,128)}, f32[6,64,512]{2,1,0:T(8,128)}, u32[]{:S(2)}, u32[]{:S(2)}) collective-permute-start(f32[6,64,512]{2,1,0:T(8,128)} %fusion.82), channel_id=1, source_target_pairs={{0,8},{8,16},{16,24},{24,32},{32,40},{40,48},{48,56},{56,64},{64,7... | collective-permute-start | bytes 2359304 | tf_op jit(solution)/shard_map/ppermute | solution.py:18
  13.7 32.3 %collective-permute-start.1 = (f32[6,64,512]{2,1,0:T(8,128)}, f32[6,64,512]{2,1,0:T(8,128)}, u32[]{:S(2)}, u32[]{:S(2)}) collective-permute-start(f32[6,64,512]{2,1,0:T(8,128)} %fusion.85), channel_id=1, source_target_pairs={{0,248},{8,0},{16,8},{24,16},{32,24},{40,32},{48,40},{56,48},{64,5... | collective-permute-start | bytes 2359304 | tf_op jit(solution)/shard_map/ppermute | solution.py:18
  58.4 36.5 %all-to-all-start = ((f32[2,3,8,4096]{3,0,1,2:T(2,128)}), f32[2,3,8,4096]{3,0,1,2:T(2,128)S(1)}, u32[]{:S(2)}, u32[]{:S(2)}) async-start(f32[2,3,8,4096]{3,0,1,2:T(2,128)} %copy.119), calls=%async_computation | async-start | bytes 1572864 | tf_op jit(solution)/shard_map/all_to_all | solution.py:96
  75.2 24.0 %copy-start.18 = (f32[64,512]{1,0:T(8,128)}, f32[64,512]{1,0:T(8,128)S(1)}, u32[]{:S(2)}) copy-start(f32[64,512]{1,0:T(8,128)S(1)} %divide_select_fusion) | copy-start | bytes 393220
  139.5 30.8 %all-to-all-start.1 = ((f32[2,4,8,4096]{3,0,1,2:T(2,128)}), f32[2,4,8,4096]{3,0,1,2:T(2,128)}, u32[]{:S(2)}, u32[]{:S(2)}) async-start(f32[2,4,8,4096]{3,0,1,2:T(2,128)} %copy.125), calls=%async_computation.1 | async-start | bytes 2097152 | tf_op jit(solution)/shard_map/all_to_all | solution.py:117
  174.3 7.0 %copy-start.3 = (f32[2,4,512,64]{3,2,1,0:T(8,128)S(1)}, f32[2,4,512,64]{3,2,1,0:T(8,128)}, u32[]{:S(2)}) copy-start(f32[2,4,512,64]{3,2,1,0:T(8,128)} %reshape.636) | copy-start | bytes 3145732
  198.5 27.6 %collective-permute-start.3 = (f32[3,1,64,512]{3,2,1,0:T(8,128)S(1)}, f32[3,1,64,512]{3,2,1,0:T(8,128)S(1)}, u32[]{:S(2)}, u32[]{:S(2)}) collective-permute-start(f32[3,1,64,512]{3,2,1,0:T(8,128)S(1)} %get-tuple-element.90), channel_id=1, source_target_pairs={{0,8},{8,16},{16,24},{24,32},{32,40},{40,48},{48,56},{56,64},{64,7... | collective-permute-start | bytes 1179656 | tf_op jit(solution)/shard_map/ppermute | solution.py:28
  198.5 27.5 %collective-permute-start.2 = (f32[3,1,64,512]{3,2,1,0:T(8,128)S(1)}, f32[3,1,64,512]{3,2,1,0:T(8,128)S(1)}, u32[]{:S(2)}, u32[]{:S(2)}) collective-permute-start(f32[3,1,64,512]{3,2,1,0:T(8,128)S(1)} %get-tuple-element.89), channel_id=1, source_target_pairs={{8,0},{16,8},{24,16},{32,24},{40,32},{48,40},{56,48},{64,56},{72,6... | collective-permute-start | bytes 1179656 | tf_op jit(solution)/shard_map/ppermute | solution.py:30
  226.0 0.8 copy-start.5
  226.0 0.9 copy-start.6
  226.0 0.9 copy-start.7
  226.0 0.9 copy-start.8
  227.0 0.8 copy-start.16
  229.0 0.8 copy-start.12
  229.0 0.8 copy-start.17
  229.8 41.5 %collective-permute-start.4 = (f32[6,64,512]{2,1,0:T(8,128)S(1)}, f32[6,64,512]{2,1,0:T(8,128)S(1)}, u32[]{:S(2)}, u32[]{:S(2)}) collective-permute-start(f32[6,64,512]{2,1,0:T(8,128)S(1)} %fusion.88), channel_id=1, source_target_pairs={{0,8},{8,16},{16,24},{24,32},{32,40},{40,48},{48,56},{56,64},{64,7... | collective-permute-start | bytes 2359304 | tf_op jit(solution)/shard_map/ppermute | solution.py:18
  232.4 40.9 %collective-permute-start.5 = (f32[6,64,512]{2,1,0:T(8,128)S(1)}, f32[6,64,512]{2,1,0:T(8,128)S(1)}, u32[]{:S(2)}, u32[]{:S(2)}) collective-permute-start(f32[6,64,512]{2,1,0:T(8,128)S(1)} %fusion.91), channel_id=1, source_target_pairs={{0,248},{8,0},{16,8},{24,16},{32,24},{40,32},{48,40},{56,48},{64,5... | collective-permute-start | bytes 2359304 | tf_op jit(solution)/shard_map/ppermute | solution.py:18
  243.3 0.8 copy-start.4
  308.0 2.3 copy-start.19
  377.3 7.0 %copy-start.2 = (f32[2,4,512,64]{3,2,1,0:T(8,128)S(1)}, f32[2,4,512,64]{3,2,1,0:T(8,128)}, u32[]{:S(2)}) copy-start(f32[2,4,512,64]{3,2,1,0:T(8,128)} %reshape.641) | copy-start | bytes 3145732
  401.3 25.1 %collective-permute-start.7 = (f32[3,1,64,512]{3,2,1,0:T(8,128)S(1)}, f32[3,1,64,512]{3,2,1,0:T(8,128)S(1)}, u32[]{:S(2)}, u32[]{:S(2)}) collective-permute-start(f32[3,1,64,512]{3,2,1,0:T(8,128)S(1)} %get-tuple-element.85), channel_id=1, source_target_pairs={{0,8},{8,16},{16,24},{24,32},{32,40},{40,48},{48,56},{56,64},{64,7... | collective-permute-start | bytes 1179656 | tf_op jit(solution)/shard_map/ppermute | solution.py:28
  401.4 25.0 %collective-permute-start.6 = (f32[3,1,64,512]{3,2,1,0:T(8,128)S(1)}, f32[3,1,64,512]{3,2,1,0:T(8,128)S(1)}, u32[]{:S(2)}, u32[]{:S(2)}) collective-permute-start(f32[3,1,64,512]{3,2,1,0:T(8,128)S(1)} %get-tuple-element.84), channel_id=1, source_target_pairs={{8,0},{16,8},{24,16},{32,24},{40,32},{48,40},{56,48},{64,56},{72,6... | collective-permute-start | bytes 1179656 | tf_op jit(solution)/shard_map/ppermute | solution.py:30
  (6 other events, 4.6 us)
where the time goes:
time: 436 us; the launch traced here: 428 us
  matrix products  122 us (28%)
  waiting for transfers between devices  117 us (27%)
  starting transfers between devices  65.5 us (15%)
  blocking collectives  53.2 us (12%)
  local copies, waits for them, and re-layouts  48.7 us (11%)
  other arithmetic  20.8 us (5%)
    ppermute x4, waiting for transfers between devices, shifted(): lax.ppermute(value, axis, [(i, (i + by) % count) for i in range(count)])  43.1 us
    ppermute x2, waiting for transfers between devices, padded_2(): lax.ppermute(tail, axis, [(i, (i + 1) % count) for i in range(count)])  30 us
    all_to_all x1, blocking collectives, velocity(): lax.all_to_all(outgoing, 'pencil', split_axis=2, concat_axis=2, tiled=True)  29.2 us
    all_to_all x1, blocking collectives, velocity(): lax.all_to_all(along_z, 'pencil', split_axis=2, concat_axis=2, tiled=True)  24 us
    all_to_all x1, waiting for transfers between devices, velocity(): lax.all_to_all(outgoing, 'pencil', split_axis=2, concat_axis=2, tiled=True)  23.8 us
    ppermute x4, starting transfers between devices, shifted(): lax.ppermute(value, axis, [(i, (i + by) % count) for i in range(count)])  22.6 us
    ppermute x2, starting transfers between devices, padded_2(): lax.ppermute(head, axis, [((i + 1) % count, i) for i in range(count)])  21.2 us
    all_to_all x1, waiting for transfers between devices, velocity(): lax.all_to_all(along_z, 'pencil', split_axis=2, concat_axis=2, tiled=True)  19.7 us
  transfers between devices with their start and end apart: 10, of which 7 were waited for; matrix products, arithmetic and copies ran while one was open for 4% of the time, Pallas kernels for 0%

commit v1 on v0

v1 whole, which is shorter than its diff:
```python
import math

import jax
import jax.numpy as jnp
import numpy as np
from jax import lax
from jax.experimental import pallas as pl
from jax.experimental.pallas import tpu as pltpu
from jax.sharding import PartitionSpec as P

N = 512
H = 256
ROWS = 64
GROUPS = 8
BL = 128
TIME_STEP = 0.25
VMEM_LIMIT = 40 * 1024 * 1024


def lane_wave():
    m = np.arange(128)
    return np.concatenate([2 * m, np.where(m == 0, 256, 2 * m), 2 * m + 1, 2 * m + 1])


def tables():
    wave = lane_wave()
    z = np.arange(H)
    angle = 2 * np.pi * (wave[:, None] * z[None, :] % N) / N
    is_sin = np.zeros(N, bool)
    is_sin[129:256] = True
    is_sin[384:] = True
    basis = np.where(is_sin[:, None], np.sin(angle), np.cos(angle))
    forward = np.stack([basis[:H].T, basis[H:].T])
    lam = 4 * np.sin(np.pi * wave / N) ** 2
    r = 1 + lam / 2 - np.sqrt(lam + lam * lam / 4)
    norm = np.where((wave == 0) | (wave == 256), 1.0, 2.0) / N
    inverse = basis * (norm * r)[:, None]
    inverse = np.stack([inverse[:H], inverse[H:]])
    sigma = np.sin(2 * np.pi * wave / N)
    sigma[128] = 0.0
    sigma[0] = 0.0
    swap = sigma.copy()
    swap[128:256] *= -1
    swap[384:] *= -1
    rpow = r[None, :] ** (np.arange(ROWS)[:, None] + 1)

    rs = np.where(wave == 0, 0.5, r)
    rho = rs**ROWS
    wrap = 1 / (1 - rho**GROUPS)
    step = np.arange(GROUPS)
    up = np.where(step == 0, GROUPS, GROUPS - step)
    down = np.where(step == 0, GROUPS, step)
    cuu = rho[None, :] ** (up[:, None] - 1) * wrap
    cww = rho[None, :] ** (down[:, None] - 1) * wrap
    kappa = rs * (1 - rs ** (2 * ROWS)) / (1 - rs**2)
    cwu = np.zeros((GROUPS, N))
    for a in range(GROUPS):
        for b in range(GROUPS):
            cwu[(a + b) % GROUPS] += kappa * cww[a] * cuu[b]
    tri = ROWS * (ROWS + 1) // 2
    pyr = sum(tri - y * (y + 1) // 2 for y in range(ROWS))
    left, right = [], []
    row, rhs = np.zeros(17), np.zeros(24)
    row[16] = N
    rhs[:8] = 1
    left.append(row)
    right.append(rhs)
    for m in range(8):
        row, rhs = np.zeros(17), np.zeros(24)
        row[(m + 1) % 8] += 1
        row[m] -= 1
        row[16] = ROWS
        rhs[m] = 1
        left.append(row)
        right.append(rhs)
        row, rhs = np.zeros(17), np.zeros(24)
        row[8 + (m - 1) % 8] += 1
        row[8 + m] -= 1
        row[m] -= ROWS
        row[16] = tri
        rhs[8 + m] = 1
        left.append(row)
        right.append(rhs)
    row, rhs = np.zeros(17), np.zeros(24)
    row[:8] = ROWS
    row[16] = -8 * tri
    rhs[8:16] = -1
    left.append(row)
    right.append(rhs)
    row, rhs = np.zeros(17), np.zeros(24)
    row[:8] = tri
    row[8:16] = ROWS
    row[16] = -8 * pyr
    rhs[16:] = -1
    left.append(row)
    right.append(rhs)
    answer = np.linalg.lstsq(np.array(left), np.array(right), rcond=None)[0]
    cuu[:, 0] = answer[0, :8]
    cww[:, 0] = answer[8, 8:16]
    cwu[:, 0] = answer[8, :8]
    zero_u = answer[0, 8]
    zero_z = answer[8, 16]
    return {
        "forward": forward,
        "inverse": inverse,
        "swap": swap,
        "rpow": rpow,
        "r": r,
        "cuu": cuu,
        "cww": cww,
        "cwu": cwu,
        "zero_u": float(zero_u),
        "zero_z": float(zero_z),
    }


def halves(matrix):
    full = np.asarray(matrix, np.float32)
    high = full.astype(jnp.bfloat16)
    low = (full - high.astype(np.float32)).astype(jnp.bfloat16)
    return jnp.asarray(np.stack([high, low]))


def split(x):
    high = x.astype(jnp.bfloat16)
    return high, (x - high.astype(jnp.float32)).astype(jnp.bfloat16)


def dot3(x, matrix_ref, block):
    high, low = split(x)
    first = matrix_ref[0, block]
    second = matrix_ref[1, block]
    out = jnp.dot(high, first, preferred_element_type=jnp.float32)
    out = out + jnp.dot(low, first, preferred_element_type=jnp.float32)
    return out + jnp.dot(high, second, preferred_element_type=jnp.float32)


def code_kernel(count_ref, blocks_ref, shift_ref, out_ref):
    slot = lax.broadcasted_iota(jnp.int32, (1, BL), 1)
    row_id = lax.broadcasted_iota(jnp.int32, (ROWS, BL), 0)
    lane_block = lax.broadcasted_iota(jnp.int32, (N, BL), 0) // BL
    for s in range(2):
        for plane in range(2):
            direction = 1 - plane
            ids = blocks_ref[pl.ds(s * 2 + direction, 1), :]
            alive = slot < count_ref[s * 2 + direction]
            ids = jnp.where(alive, ids, -8)
            rows = jnp.where(jnp.broadcast_to(ids >> 2, (ROWS, BL)) == row_id, 1.0, 0.0)
            lanes = jnp.where(jnp.broadcast_to(ids & 3, (N, BL)) == lane_block, 1.0, 0.0)
            moved = lax.dot_general(
                rows.astype(jnp.bfloat16),
                lanes.astype(jnp.bfloat16),
                (((1,), (1,)), ((), ())),
                preferred_element_type=jnp.float32,
            )
            out_ref[s, plane] = shift_ref[s, plane] + 8 * moved.astype(jnp.int32)


def codes_of(count, blocks, shifts):
    return pl.pallas_call(
        code_kernel,
        out_shape=jax.ShapeDtypeStruct((2, 2, ROWS, N), jnp.int32),
        in_specs=[
            pl.BlockSpec(memory_space=pltpu.SMEM),
            pl.BlockSpec(memory_space=pltpu.VMEM),
            pl.BlockSpec(memory_space=pltpu.VMEM),
        ],
        out_specs=pl.BlockSpec(memory_space=pltpu.VMEM),
        compiler_params=pltpu.CompilerParams(vmem_limit_bytes=VMEM_LIMIT),
        name="codes",
    )(count, blocks, shifts)


def deposit(own, own_code, other, other_code):
    total = None
    for amount in (0, 1, 2, -1, -2):
        picked = jnp.where(own_code == amount, own, 0.0) + jnp.where(
            other_code == amount + 8, other, 0.0
        )
        if amount:
            picked = pltpu.roll(picked, amount % N, 1)
        total = picked if total is None else total + picked
    return total


def omega_kernel(own_ref, below_ref, above_ref, code_ref, cbelow_ref, cabove_ref, out_ref):
    for plane, other_ref, cother_ref in ((0, below_ref, cbelow_ref), (1, above_ref, cabove_ref)):

        @pl.loop(0, ROWS // 8)
        def _(step, plane=plane, other_ref=other_ref, cother_ref=cother_ref):
            rows = pl.ds(pl.multiple_of(step * 8, 8), 8)
            own_code = code_ref[plane, rows, :]
            other_code = cother_ref[rows, :]
            for c in range(3):
                out_ref[c, plane, rows, :] = deposit(
                    own_ref[c, plane, rows, :], own_code, other_ref[c, rows, :], other_code
                )


def omega_of(own, below, above, code, cbelow, cabove):
    return pl.pallas_call(
        omega_kernel,
        out_shape=jax.ShapeDtypeStruct((3, 2, ROWS, N), jnp.float32),
        in_specs=[pl.BlockSpec(memory_space=pltpu.VMEM)] * 6,
        out_specs=pl.BlockSpec(memory_space=pltpu.VMEM),
        compiler_params=pltpu.CompilerParams(vmem_limit_bytes=VMEM_LIMIT),
        cost_estimate=pl.CostEstimate(flops=30_000_000, bytes_accessed=6_000_000, transcendentals=0),
        name="omega",
    )(own, below, above, code, cbelow, cabove)


SUBLANE = (0, 4, 12)


def first_kernel(
    own_ref, below_ref, above_ref, code_ref, cbelow_ref, cabove_ref, forward_ref, r_ref,
    lam_ref, u_ref, ends_ref, x_ref, h_ref,
):
    for plane, other, other_ref, cother_ref in (
        (0, 0, below_ref, cbelow_ref),
        (1, 3, above_ref, cabove_ref),
    ):

        @pl.loop(0, ROWS // 8)
        def _(step, plane=plane, other=other, other_ref=other_ref, cother_ref=cother_ref):
            start = pl.multiple_of(step * 8, 8)
            rows = pl.ds(start, 8)
            own_code = code_ref[plane, rows, :]
            other_code = cother_ref[rows, :]
            for c in range(3):
                own = own_ref[c, plane, rows, :]
                far = other_ref[c, rows, :]
                here = deposit(own, own_code, far, other_code)
                there = deposit(far, other_code, own, own_code)
                lam_ref[c, plane, rows, :] = here
                for place, value in ((plane + 1, here), (other, there)):
                    base = (c * 4 + place) * ROWS
                    at = pl.ds(pl.multiple_of(base + start, 8), 8)
                    x_ref[at, :H] = value[:, :H] + value[:, H:]
                    x_ref[at, H:] = value[:, :H] - value[:, H:]

    for block in range(2):
        lanes = pl.ds(block * H, H)
        out = dot3(x_ref[:, lanes], forward_ref, block)
        for c in range(3):
            for place in range(4):
                base = (c * 4 + place) * ROWS
                for part in range(2):
                    h_ref[block * 2 + part, pl.ds(SUBLANE[c] + place, ROWS, stride=16), :] = out[
                        base : base + ROWS, part * BL : (part + 1) * BL
                    ]

    r = [jnp.broadcast_to(r_ref[:, q * BL : (q + 1) * BL], (16, BL)) for q in range(4)]
    zero = jnp.zeros((16, BL), jnp.float32)

    def ahead(y, carry):
        at = pl.ds(pl.multiple_of(y * 16, 16), 16)
        new = []
        for q in range(4):
            value = h_ref[q, at, :] + r[q] * carry[q]
            u_ref[q, at, :] = value
            new.append(value)
        return tuple(new)

    u_end = lax.fori_loop(0, ROWS, ahead, (zero,) * 4, unroll=8)

    def back(i, carry):
        y = ROWS - 1 - i
        at = pl.ds(pl.multiple_of(y * 16, 16), 16)
        new = [u_ref[q, at, :] + r[q] * carry[q] for q in range(4)]
        return (*new, carry[4] + new[0])

    w_end = lax.fori_loop(0, ROWS, back, (zero,) * 5, unroll=8)
    for q in range(4):
        lanes = pl.ds(q * BL, BL)
        ends_ref[0:8, lanes] = u_end[q][0:8]
        ends_ref[8:12, lanes] = u_end[q][12:16]
        ends_ref[12:20, lanes] = w_end[q][0:8]
        ends_ref[20:24, lanes] = w_end[q][12:16]
    lane = lax.broadcasted_iota(jnp.int32, (16, BL), 1)
    sub = lax.broadcasted_iota(jnp.int32, (16, BL), 0)
    sums = jnp.broadcast_to(w_end[4][:, 0:1], (16, BL))
    ends_ref[24:25, :] = jnp.zeros((1, N), jnp.float32)
    used = (lane == sub) & ((sub < 8) | (sub >= 12))
    ends_ref[24:25, 0:BL] = jnp.sum(jnp.where(used, sums, 0.0), axis=0, keepdims=True)


def first_of(own, below, above, code, cbelow, cabove, forward, r):
    return pl.pallas_call(
        first_kernel,
        out_shape=(
            jax.ShapeDtypeStruct((3, 2, ROWS, N), jnp.float32),
            jax.ShapeDtypeStruct((4, ROWS * 16, BL), jnp.float32),
            jax.ShapeDtypeStruct((25, N), jnp.float32),
        ),
        in_specs=[pl.BlockSpec(memory_space=pltpu.VMEM)] * 8,
        out_specs=(pl.BlockSpec(memory_space=pltpu.VMEM),) * 3,
        scratch_shapes=[
            pltpu.VMEM((12 * ROWS, N), jnp.float32),
            pltpu.VMEM((4, ROWS * 16, BL), jnp.float32),
        ],
        compiler_params=pltpu.CompilerParams(vmem_limit_bytes=VMEM_LIMIT),
        cost_estimate=pl.CostEstimate(flops=3_000_000_000, bytes_accessed=8_000_000, transcendentals=0),
        name="first",
    )(own, below, above, code, cbelow, cabove, forward, r)


def second_kernel(
    zero_u, zero_z,
    me_ref, ends_ref, u_ref, lam_ref, omega_ref, cuu_ref, cww_ref, cwu_ref, rpow_ref, r_ref,
    swap_ref, inverse_ref, out_ref, y_ref, field_ref,
):
    me = me_ref[0]
    u_in = [[jnp.zeros((8, BL), jnp.float32)] * 2 for _ in range(4)]
    w_in = [[jnp.zeros((8, BL), jnp.float32)] * 2 for _ in range(4)]
    u_sum = [jnp.zeros((8, BL), jnp.float32)] * 2
    w_sum = [jnp.zeros((8, BL), jnp.float32)] * 2
    z_row = jnp.zeros((1, BL), jnp.float32)
    for step in range(GROUPS):
        who = (me + step) & (GROUPS - 1)
        for q in range(4):
            lanes = pl.ds(q * BL, BL)
            uu = cuu_ref[step : step + 1, lanes]
            ww = cww_ref[step : step + 1, lanes]
            wu = cwu_ref[step : step + 1, lanes]
            for g in range(2):
                u = ends_ref[who, 4 * g : 4 * g + 8, lanes]
                w = ends_ref[who, 12 + 4 * g : 20 + 4 * g, lanes]
                u_in[q][g] = u_in[q][g] + uu * u
                w_in[q][g] = w_in[q][g] + (ww * w + wu * u)
                if q == 0:
                    u_sum[g] = u_sum[g] + u
                    w_sum[g] = w_sum[g] + w
        z_row = z_row + ends_ref[step, 24:25, 0:BL]
    lane = lax.broadcasted_iota(jnp.int32, (8, BL), 1)
    sub = lax.broadcasted_iota(jnp.int32, (8, BL), 0)
    first_lane = lane == 0
    mean = []
    for g in range(2):
        u_in[0][g] = u_in[0][g] + jnp.where(first_lane, zero_u * w_sum[g], 0.0)
        mean.append(jnp.where(first_lane, u_sum[g] * (1.0 / N), 0.0))
        mine = jnp.where(lane == sub + 8 * g, jnp.broadcast_to(z_row, (8, BL)), 0.0)
        z_total = jnp.broadcast_to(jnp.sum(mine, axis=1, keepdims=True), (8, BL))
        w_in[0][g] = w_in[0][g] + jnp.where(first_lane, zero_z * z_total, 0.0)

    r = [jnp.broadcast_to(r_ref[:, q * BL : (q + 1) * BL], (8, BL)) for q in range(4)]
    swap = [jnp.broadcast_to(swap_ref[:, q * BL : (q + 1) * BL], (8, BL)) for q in range(4)]
    upper = sub < 4

    def emit(y, after, here, before):
        at = pl.ds(pl.multiple_of(y * 8, 8), 8)
        at_b = pl.ds(pl.multiple_of(ROWS * 8 + y * 8, 8), 8)
        for q in range(4):
            slope0 = 0.5 * (after[2 * q] - before[2 * q])
            slope1 = 0.5 * (after[2 * q + 1] - before[2 * q + 1])
            turned = swap[q] * here[2 * (q ^ 1)]
            lanes = pl.ds(q * BL, BL)
            y_ref[at, lanes] = jnp.where(upper, here[2 * q], slope1 - turned)
            y_ref[at_b, lanes] = slope0

    def back(i, carry):
        y = ROWS - 1 - i
        after, here = carry[:8], carry[8:]
        new = []
        for q in range(4):
            power = rpow_ref[y, :, q * BL : (q + 1) * BL]
            for g in range(2):
                at = pl.ds(pl.multiple_of(y * 16 + 8 * g, 8), 8)
                value = u_ref[q, at, :] + power * u_in[q][g]
                if q == 0:
                    value = value - (y + 1).astype(jnp.float32) * mean[g]
                new.append(value + r[q] * here[2 * q + g])
        emit(y + 1, after, here, new)
        return (*here, *new)

    edge = tuple(w_in[q][g] for q in range(4) for g in range(2))
    new = []
    for q in range(4):
        power = rpow_ref[ROWS - 1, :, q * BL : (q + 1) * BL]
        for g in range(2):
            value = u_ref[q, (ROWS - 1) * 16 + 8 * g : (ROWS - 1) * 16 + 8 * g + 8, :]
            value = value + power * u_in[q][g]
            if q == 0:
                value = value - float(ROWS) * mean[g]
            new.append(value + r[q] * edge[2 * q + g])
    carry = lax.fori_loop(1, ROWS, back, (*edge, *new), unroll=3)
    after, here = carry[:8], carry[8:]
    before = [u_in[q][g] + r[q] * here[2 * q + g] for q in range(4) for g in range(2)]
    emit(jnp.int32(0), after, here, before)

    even = dot3(y_ref[:, :H], inverse_ref, 0)
    odd = dot3(y_ref[:, H:], inverse_ref, 1)
    for part in range(2):
        lanes = slice(part * BL, (part + 1) * BL)
        field_ref[part] = even[:, lanes] + odd[:, lanes]
        field_ref[2 + part] = even[:, lanes] - odd[:, lanes]

    @pl.loop(0, ROWS // 8)
    def _(step):
        start = pl.multiple_of(step * 8, 8)
        rows = pl.ds(start, 8)

        def load(base):
            parts = [
                field_ref[q, pl.ds(start * 8 + base, 8, stride=8), :]
                for q in range(4)
            ]
            return jnp.concatenate(parts, axis=1)

        g = []
        for place in range(4):
            psi = load(place)
            gx = load(4 + place)
            gz = -load(ROWS * 8 + place)
            gy = 0.5 * (pltpu.roll(psi, N - 1, 1) - pltpu.roll(psi, 1, 1))
            g.append((gx, gy, gz))
        for plane in range(2):
            here = g[plane + 1]
            w = [omega_ref[c, plane, rows, :] for c in range(3)]
            cross = (
                w[1] * here[2] - w[2] * here[1],
                w[2] * here[0] - w[0] * here[2],
                w[0] * here[1] - w[1] * here[0],
            )
            for c in range(3):
                slope = 0.5 * (g[plane + 2][c] - g[plane][c])
                out_ref[c, plane, rows, :] = lam_ref[c, plane, rows, :] + TIME_STEP * (
                    cross[c] + w[0] * slope
                )


def second_of(t, me, ends, u, lam, omega, cuu, cww, cwu, rpow, r, swap, inverse):
    def body(*refs):
        second_kernel(t["zero_u"], t["zero_z"], *refs)

    return pl.pallas_call(
        body,
        out_shape=jax.ShapeDtypeStruct((3, 2, ROWS, N), jnp.float32),
        in_specs=[pl.BlockSpec(memory_space=pltpu.SMEM)]
        + [pl.BlockSpec(memory_space=pltpu.VMEM)] * 11,
        out_specs=pl.BlockSpec(memory_space=pltpu.VMEM),
        scratch_shapes=[
            pltpu.VMEM((ROWS * 16, N), jnp.float32),
            pltpu.VMEM((4, ROWS * 16, BL), jnp.float32),
        ],
        compiler_params=pltpu.CompilerParams(vmem_limit_bytes=VMEM_LIMIT),
        cost_estimate=pl.CostEstimate(flops=4_000_000_000, bytes_accessed=8_000_000, transcendentals=0),
        name="second",
    )(me, ends, u, lam, omega, cuu, cww, cwu, rpow, r, swap, inverse)


def shifted(value, axis, by):
    count = lax.axis_size(axis)
    return lax.ppermute(value, axis, [(i, (i + by) % count) for i in range(count)])


def neighbours(lower_plane, upper_plane):
    return shifted(upper_plane, "slab", 1), shifted(lower_plane, "slab", -1)


def shards(adjoint_vort, omega_ckpt, cell_shift, move_count, move_blocks):
    t = tables()
    forward, inverse = halves(t["forward"]), halves(t["inverse"])
    f32 = {k: jnp.asarray(t[k], jnp.float32) for k in ("cuu", "cww", "cwu", "rpow")}
    r = jnp.asarray(t["r"], jnp.float32)[None]
    swap = jnp.asarray(t["swap"], jnp.float32)[None]
    me = lax.axis_index("pencil").astype(jnp.int32)[None]

    lam = adjoint_vort
    code = codes_of(move_count.reshape(4), move_blocks.reshape(4, BL), cell_shift)
    below, above = neighbours(lam[:, 0], lam[:, 1])
    far_code = [neighbours(code[s, 0], code[s, 1]) for s in range(2)]
    omega = []
    for s in range(2):
        far = neighbours(omega_ckpt[s, :, 0], omega_ckpt[s, :, 1])
        omega.append(omega_of(omega_ckpt[s], *far, code[s], *far_code[s]))
    for s in range(2):
        if s:
            below, above = neighbours(lam[:, 0], lam[:, 1])
        lam_r, u, ends = first_of(lam, below, above, code[s], *far_code[s], forward, r)
        gathered = lax.all_to_all(
            jnp.broadcast_to(ends[None], (GROUPS, 25, N)), "pencil", 0, 0, tiled=True
        )
        lam = second_of(
            t, me, gathered, u, lam_r, omega[s], f32["cuu"], f32["cww"], f32["cwu"],
            f32["rpow"][:, None], r, swap, inverse,
        )
    return lam


def solution(mesh):
    return jax.shard_map(
        shards,
        mesh=mesh,
        in_specs=(
            P(None, "slab", "pencil", None),
            P(None, None, "slab", "pencil", None),
            P(None, "slab", "pencil", None),
            P(None, "slab", "pencil", None),
            P(None, "slab", "pencil", None, None),
        ),
        out_specs=P(None, "slab", "pencil", None),
        check_vma=False,
    )
```

time: 436 us -> 184 us (0.42); the launches traced: 428 us -> 184 us
  matrix products: 122 us -> 0 us
  blocking collectives: 53.2 us -> 0 us
  local copies, waits for them, and re-layouts: 48.7 us -> 21.9 us
  waiting for transfers between devices: 117 us -> 90.5 us
  Pallas kernels: 0 us -> 20.9 us
  other arithmetic: 20.8 us -> 0.66 us
  starting transfers between devices: 65.5 us -> 49.6 us
    dot_general x20 -> x0, matrix products: 122 us -> none  [the longest x2 14.5 us: velocity(): jnp.einsum('ncqkr,qrm->nckm', received_blocks, forward_y.reshape(groups,...]
    all_to_all x2 -> x0, blocking collectives: 53.2 us -> none  [the longest x1 29.2 us: velocity(): lax.all_to_all(outgoing, 'pencil', split_axis=2, concat_axis=2, tiled=True)]
    ppermute x4 -> x12, waiting for transfers between devices: 43.1 us -> 86.1 us  [shifted(): lax.ppermute(value, axis, [(i, (i + by) % count) for i in range(count)])]
    all_to_all x2, waiting for transfers between devices: 43.5 us -> 4.45 us  [shards(): lax.all_to_all(jnp.broadcast_to(ends[None], (GROUPS, 25, N)), 'pencil', 0...]
    ppermute x4 -> x0, waiting for transfers between devices: 30 us -> none  [the longest x2 30 us: padded_2(): lax.ppermute(tail, axis, [(i, (i + 1) % count) for i in range(count)])]
    ppermute x4 -> x0, starting transfers between devices: 21.3 us -> none  [the longest x2 21.2 us: padded_2(): lax.ppermute(head, axis, [((i + 1) % count, i) for i in range(count)])]
    pallas_call x0 -> x7, Pallas kernels: none -> 20.9 us  [the longest x2 9.41 us: first_of(): pl.pallas_call(first_kernel, out_shape=(jax.ShapeDtypeStruct((3, 2, ROWS,...]
    ppermute x4 -> x12, starting transfers between devices: 22.6 us -> 41.6 us  [shifted(): lax.ppermute(value, axis, [(i, (i + by) % count) for i in range(count)])]
  transfers between devices with their start and end apart: 10 -> 14, of which waited for: 7 -> 9; matrix products, arithmetic and copies ran while one was open for 4% -> 3% of each run, Pallas kernels for 0% -> 3%
where the time goes in v1:
time: 184 us
  waiting for transfers between devices  90.5 us (49%)
  starting transfers between devices  49.6 us (27%)
  local copies, waits for them, and re-layouts  21.9 us (12%)
  Pallas kernels  20.9 us (11%)
    ppermute x12, waiting for transfers between devices, shifted(): lax.ppermute(value, axis, [(i, (i + by) % count) for i in range(count)])  86.1 us
    ppermute x12, starting transfers between devices, shifted(): lax.ppermute(value, axis, [(i, (i + by) % count) for i in range(count)])  41.6 us
    unnamed x71, local copies, waits for them, and re-layouts  15.2 us
    pallas_call x2, Pallas kernels, first_of(): pl.pallas_call(first_kernel, out_shape=(jax.ShapeDtypeStruct((3, 2, ROWS,...  9.41 us
    all_to_all x2, starting transfers between devices, shards(): lax.all_to_all(jnp.broadcast_to(ends[None], (GROUPS, 25, N)), 'pencil', 0...  7.97 us
    pallas_call x2, Pallas kernels, second_of(): pl.pallas_call(body, out_shape=jax.ShapeDtypeStruct((3, 2, ROWS, N), jnp....  6.74 us
    all_to_all x2, waiting for transfers between devices, shards(): lax.all_to_all(jnp.broadcast_to(ends[None], (GROUPS, 25, N)), 'pencil', 0...  4.45 us
    pallas_call x2, Pallas kernels, omega_of(): pl.pallas_call(omega_kernel, out_shape=jax.ShapeDtypeStruct((3, 2, ROWS,...  3.91 us
  transfers between devices with their start and end apart: 14, of which 9 were waited for; matrix products, arithmetic and copies ran while one was open for 3% of the time, Pallas kernels for 3%

profile of v1, /device:TPU:1, one launch (start us, length us, event | category | flops | bytes accessed | tf_op | source)
XLA Modules:
  0.0 183.7 jit_solution(1032183884348844616)
XLA Ops:
  1.2 12.4 %collective-permute-start.1 = (f32[3,64,512]{2,1,0:T(8,128)S(1)}, f32[3,64,512]{2,1,0:T(8,128)S(1)}, u32[]{:S(2)}, u32[]{:S(2)}) collective-permute-start(f32[3,64,512]{2,1,0:T(8,128)S(1)} %get-tuple-element.25), channel_id=1, source_target_pairs={{0,248},{8,0},{16,8},{24,16},{32,24},{40,32},{48,40},{56,48},{64,5... | collective-permute-start | bytes 1179656 | tf_op jit(solution)/shard_map/ppermute | solution.py:454
  16.6 9.6 %collective-permute-start.3 = (s32[64,512]{1,0:T(8,128)S(1)}, s32[64,512]{1,0:T(8,128)S(1)}, u32[]{:S(2)}, u32[]{:S(2)}) collective-permute-start(s32[64,512]{1,0:T(8,128)S(1)} %get-tuple-element.29), channel_id=1, source_target_pairs={{0,248},{8,0},{16,8},{24,16},{32,24},{40,32},{48,40},{56,48},{64,5... | collective-permute-start | bytes 393224 | tf_op jit(solution)/shard_map/ppermute | solution.py:454
  26.2 10.2 %collective-permute-done.3.cabove_ref = s32[64,512]{1,0:T(8,128)S(1)} collective-permute-done((s32[64,512]{1,0:T(8,128)S(1)}, s32[64,512]{1,0:T(8,128)S(1)}, u32[]{:S(2)}, u32[]{:S(2)}) %collective-permute-start.3) | collective-permute-done | bytes 131104 | tf_op jit(solution)/shard_map/ppermute | solution.py:454
  36.4 10.4 %collective-permute-done.2.cbelow_ref = s32[64,512]{1,0:T(8,128)S(1)} collective-permute-done((s32[64,512]{1,0:T(8,128)S(1)}, s32[64,512]{1,0:T(8,128)S(1)}, u32[]{:S(2)}, u32[]{:S(2)}) %collective-permute-start.2) | collective-permute-done | bytes 131104 | tf_op jit(solution)/shard_map/ppermute | solution.py:454
  46.8 4.7 %first.2 = (f32[3,2,64,512]{3,2,1,0:T(8,128)S(1)}, f32[4,1024,128]{2,1,0:T(8,128)S(1)}, f32[25,512]{1,0:T(8,128)S(1)}) custom-call(f32[3,2,64,512]{3,2,1,0:T(8,128)S(1)} %copy-done, f32[3,64,512]{2,1,0:T(8,128)S(1)} %collective-permute-done.below_ref, f32[3,64,512]{2,1,0:T(8,128)S(1)} %collective-permute-done.1.above_ref, ...), custom_call_target="tpu_custom_call" | custom-call | flops 3000000000 | bytes 8000000 | tf_op jit(solution)/shard_map/first/pallas_call | solution.py:289
  54.6 4.1 %all-to-all-start = ((f32[8,25,512]{2,1,0:T(8,128)}), f32[8,25,512]{2,1,0:T(8,128)S(1)}, u32[]{:S(2)}, u32[]{:S(2)}) async-start(f32[8,25,512]{2,1,0:T(8,128)} %broadcast_in_dim.27), calls=%async_computation | async-start | bytes 1048576 | tf_op jit(solution)/shard_map/all_to_all | solution.py:481
  59.9 1.5 collective-permute-start.4
  61.4 1.5 slice_bitcast_fusion
  62.9 21.7 %collective-permute-done.5.above_ref = f32[3,64,512]{2,1,0:T(8,128)S(1)} collective-permute-done((f32[3,64,512]{2,1,0:T(8,128)}, f32[3,64,512]{2,1,0:T(8,128)S(1)}, u32[]{:S(2)}, u32[]{:S(2)}) %collective-permute-start.5) | collective-permute-done | bytes 393248 | tf_op jit(solution)/shard_map/ppermute | solution.py:454
  84.6 2.4 %collective-permute-done.4.below_ref = f32[3,64,512]{2,1,0:T(8,128)S(1)} collective-permute-done((f32[3,64,512]{2,1,0:T(8,128)}, f32[3,64,512]{2,1,0:T(8,128)S(1)}, u32[]{:S(2)}, u32[]{:S(2)}) %collective-permute-start.4) | collective-permute-done | bytes 393248 | tf_op jit(solution)/shard_map/ppermute | solution.py:454
  87.0 1.9 %omega.2.refs_4_ = f32[3,2,64,512]{3,2,1,0:T(8,128)S(1)} custom-call(f32[3,2,64,512]{3,2,1,0:T(8,128)S(1)} %get-tuple-element.22.own_ref, f32[3,64,512]{2,1,0:T(8,128)S(1)} %collective-permute-done.4.below_ref, f32[3,64,512]{2,1,0:T(8,128)S(1)} %collective-permute-done.5.above_ref, s32[2,64,512]{2,1,0:T(8,128)S(1)} %get-tuple-element.32.code_ref, ...), custom_call_target="tpu_custom_call" | custom-call | flops 30000000 | bytes 6000000 | tf_op jit(solution)/shard_map/omega/pallas_call | solution.py:201
  94.7 1.6 copy-done.22
  97.4 2.9 %second.2.own_ref = f32[3,2,64,512]{3,2,1,0:T(8,128)S(1)} custom-call(s32[1]{0:T(128)} %bitcast.refs_0_, f32[8,25,512]{2,1,0:T(8,128)S(1)} %all-to-all-done.refs_1_, f32[4,1024,128]{2,1,0:T(8,128)S(1)} %copy-done.22, f32[3,2,64,512]{3,2,1,0:T(8,128)S(1)} %copy-done.26, f32[3,2,64,512]{3,2,1,0:T(8,128)S(1)} %omega.2.refs_4_, f32[8,512]{1,0:T(8,128)S(1)} %copy-done.14, ...), custom_call_target="tpu_custom_call" | custom-call | flops 4000000000 | bytes 8000000 | tf_op jit(solution)/shard_map/second/pallas_call | solution.py:436
  100.5 6.9 %collective-permute-start.7 = (f32[3,64,512]{2,1,0:T(8,128)S(1)}, f32[3,64,512]{2,1,0:T(8,128)S(1)}, u32[]{:S(2)}, u32[]{:S(2)}) collective-permute-start(f32[3,64,512]{2,1,0:T(8,128)S(1)} %get-tuple-element.23), channel_id=1, source_target_pairs={{0,248},{8,0},{16,8},{24,16},{32,24},{40,32},{48,40},{56,48},{64,5... | collective-permute-start | bytes 1179656 | tf_op jit(solution)/shard_map/ppermute | solution.py:454
  107.4 9.6 %collective-permute-start.9 = (s32[64,512]{1,0:T(8,128)S(1)}, s32[64,512]{1,0:T(8,128)S(1)}, u32[]{:S(2)}, u32[]{:S(2)}) collective-permute-start(s32[64,512]{1,0:T(8,128)S(1)} %copy-done.33), channel_id=1, source_target_pairs={{0,248},{8,0},{16,8},{24,16},{32,24},{40,32},{48,40},{56,48},{64,5... | collective-permute-start | bytes 393224 | tf_op jit(solution)/shard_map/ppermute | solution.py:454
  117.0 6.8 %collective-permute-done.9.cabove_ref = s32[64,512]{1,0:T(8,128)S(1)} collective-permute-done((s32[64,512]{1,0:T(8,128)S(1)}, s32[64,512]{1,0:T(8,128)S(1)}, u32[]{:S(2)}, u32[]{:S(2)}) %collective-permute-start.9) | collective-permute-done | bytes 131104 | tf_op jit(solution)/shard_map/ppermute | solution.py:454
  123.9 10.3 %collective-permute-done.8.cbelow_ref = s32[64,512]{1,0:T(8,128)S(1)} collective-permute-done((s32[64,512]{1,0:T(8,128)S(1)}, s32[64,512]{1,0:T(8,128)S(1)}, u32[]{:S(2)}, u32[]{:S(2)}) %collective-permute-start.8) | collective-permute-done | bytes 131104 | tf_op jit(solution)/shard_map/ppermute | solution.py:454
  134.2 4.7 %first.3 = (f32[3,2,64,512]{3,2,1,0:T(8,128)S(1)}, f32[4,1024,128]{2,1,0:T(8,128)S(1)}, f32[25,512]{1,0:T(8,128)S(1)}) custom-call(f32[3,2,64,512]{3,2,1,0:T(8,128)S(1)} %second.2.own_ref, f32[3,64,512]{2,1,0:T(8,128)S(1)} %collective-permute-done.6.below_ref, f32[3,64,512]{2,1,0:T(8,128)S(1)} %collective-permute-done.7.above_ref, ...), custom_call_target="tpu_custom_call" | custom-call | flops 3000000000 | bytes 8000000 | tf_op jit(solution)/shard_map/first/pallas_call | solution.py:289
  142.0 3.9 %all-to-all-start.1 = ((f32[8,25,512]{2,1,0:T(8,128)}), f32[8,25,512]{2,1,0:T(8,128)S(1)}, u32[]{:S(2)}, u32[]{:S(2)}) async-start(f32[8,25,512]{2,1,0:T(8,128)} %broadcast_in_dim.30), calls=%async_computation.1 | async-start | bytes 1048576 | tf_op jit(solution)/shard_map/all_to_all | solution.py:481
  147.5 24.3 %collective-permute-done.11.above_ref = f32[3,64,512]{2,1,0:T(8,128)S(1)} collective-permute-done((f32[3,64,512]{2,1,0:T(8,128)S(1)}, f32[3,64,512]{2,1,0:T(8,128)S(1)}, u32[]{:S(2)}, u32[]{:S(2)}) %collective-permute-start.11) | collective-permute-done | bytes 393248 | tf_op jit(solution)/shard_map/ppermute | solution.py:454
  171.8 2.0 %omega.3.refs_4_ = f32[3,2,64,512]{3,2,1,0:T(8,128)S(1)} custom-call(f32[3,2,64,512]{3,2,1,0:T(8,128)S(1)} %get-tuple-element.21.own_ref, f32[3,64,512]{2,1,0:T(8,128)S(1)} %collective-permute-done.10.below_ref, f32[3,64,512]{2,1,0:T(8,128)S(1)} %collective-permute-done.11.above_ref, s32[2,64,512]{2,1,0:T(8,128)S(1)} %get-tuple-element.31.code_ref, ...), custom_call_target="tpu_custom_call" | custom-call | flops 30000000 | bytes 6000000 | tf_op jit(solution)/shard_map/omega/pallas_call | solution.py:201
  173.7 3.4 %all-to-all-done.1.refs_1_ = f32[8,25,512]{2,1,0:T(8,128)S(1)} async-done(((f32[8,25,512]{2,1,0:T(8,128)}), f32[8,25,512]{2,1,0:T(8,128)S(1)}, u32[]{:S(2)}, u32[]{:S(2)}) %all-to-all-start.1) | async-done | bytes 409632 | tf_op jit(solution)/shard_map/all_to_all | solution.py:481
  177.2 1.6 copy-done.24
  179.9 3.8 %second.3 = f32[3,2,64,512]{3,2,1,0:T(8,128)} custom-call(s32[1]{0:T(128)} %bitcast.refs_0_, f32[8,25,512]{2,1,0:T(8,128)S(1)} %all-to-all-done.1.refs_1_, f32[4,1024,128]{2,1,0:T(8,128)S(1)} %copy-done.24, f32[3,2,64,512]{3,2,1,0:T(8,128)S(1)} %copy-done.28, f32[3,2,64,512]{3,2,1,0:T(8,128)S(1)} %omega.3.refs_4_, f32[8,512]{1,0:T(8,128)S(1)} %copy-done.15, ...), custom_call_target="tpu_custom_call" | custom-call | flops 4000000000 | bytes 8000000 | tf_op jit(solution)/shard_map/second/pallas_call | solution.py:436
  (92 shorter events, 21.3 us)
Async XLA Ops:
  1.2 45.6 %collective-permute-start.1 = (f32[3,64,512]{2,1,0:T(8,128)S(1)}, f32[3,64,512]{2,1,0:T(8,128)S(1)}, u32[]{:S(2)}, u32[]{:S(2)}) collective-permute-start(f32[3,64,512]{2,1,0:T(8,128)S(1)} %get-tuple-element.25), channel_id=1, source_target_pairs={{0,248},{8,0},{16,8},{24,16},{32,24},{40,32},{48,40},{56,48},{64,5... | collective-permute-start | bytes 1179656 | tf_op jit(solution)/shard_map/ppermute | solution.py:454
  13.7 33.1 %collective-permute-start = (f32[3,64,512]{2,1,0:T(8,128)S(1)}, f32[3,64,512]{2,1,0:T(8,128)S(1)}, u32[]{:S(2)}, u32[]{:S(2)}) collective-permute-start(f32[3,64,512]{2,1,0:T(8,128)S(1)} %get-tuple-element.26), channel_id=1, source_target_pairs={{0,8},{8,16},{16,24},{24,32},{32,40},{40,48},{48,56},{56,64},{64,7... | collective-permute-start | bytes 1179656 | tf_op jit(solution)/shard_map/ppermute | solution.py:454
  15.0 31.8 %copy-start = (f32[3,2,64,512]{3,2,1,0:T(8,128)S(1)}, f32[3,2,64,512]{3,2,1,0:T(8,128)}, u32[]{:S(2)}) copy-start(f32[3,2,64,512]{3,2,1,0:T(8,128)} %own_ref.1) | copy-start | bytes 2359300
  15.0 31.9 %copy-start.7 = (bf16[2,2,256,256]{3,2,1,0:T(8,128)(2,1)S(1)}, bf16[2,2,256,256]{3,2,1,0:T(8,128)(2,1)}, u32[]{:S(2)}) copy-start(bf16[2,2,256,256]{3,2,1,0:T(8,128)(2,1)} %constant.20.clone.forward_ref) | copy-start | bytes 1572868
  15.0 31.9 %copy-start.16 = (f32[1,512]{1,0:T(1,128)S(1)}, f32[1,512]{1,0:T(1,128)}, u32[]{:S(2)}) copy-start(f32[1,512]{1,0:T(1,128)} %constant.33.r_ref.refs_9_) | copy-start | bytes 6148
  16.6 19.9 %collective-permute-start.3 = (s32[64,512]{1,0:T(8,128)S(1)}, s32[64,512]{1,0:T(8,128)S(1)}, u32[]{:S(2)}, u32[]{:S(2)}) collective-permute-start(s32[64,512]{1,0:T(8,128)S(1)} %get-tuple-element.29), channel_id=1, source_target_pairs={{0,248},{8,0},{16,8},{24,16},{32,24},{40,32},{48,40},{56,48},{64,5... | collective-permute-start | bytes 393224 | tf_op jit(solution)/shard_map/ppermute | solution.py:454
  26.2 20.6 %collective-permute-start.2 = (s32[64,512]{1,0:T(8,128)S(1)}, s32[64,512]{1,0:T(8,128)S(1)}, u32[]{:S(2)}, u32[]{:S(2)}) collective-permute-start(s32[64,512]{1,0:T(8,128)S(1)} %get-tuple-element.30), channel_id=1, source_target_pairs={{0,8},{8,16},{16,24},{24,32},{32,40},{40,48},{48,56},{56,64},{64,7... | collective-permute-start | bytes 393224 | tf_op jit(solution)/shard_map/ppermute | solution.py:454
  54.6 35.3 %all-to-all-start = ((f32[8,25,512]{2,1,0:T(8,128)}), f32[8,25,512]{2,1,0:T(8,128)S(1)}, u32[]{:S(2)}, u32[]{:S(2)}) async-start(f32[8,25,512]{2,1,0:T(8,128)} %broadcast_in_dim.27), calls=%async_computation | async-start | bytes 1048576 | tf_op jit(solution)/shard_map/all_to_all | solution.py:481
  59.9 24.7 %collective-permute-start.5 = (f32[3,64,512]{2,1,0:T(8,128)}, f32[3,64,512]{2,1,0:T(8,128)S(1)}, u32[]{:S(2)}, u32[]{:S(2)}) collective-permute-start(f32[3,64,512]{2,1,0:T(8,128)} %get-tuple-element.19), channel_id=1, source_target_pairs={{0,248},{8,0},{16,8},{24,16},{32,24},{40,32},{48,40},{56,48},{64,5... | collective-permute-start | bytes 1179656 | tf_op jit(solution)/shard_map/ppermute | solution.py:454
  59.9 27.1 %collective-permute-start.4 = (f32[3,64,512]{2,1,0:T(8,128)}, f32[3,64,512]{2,1,0:T(8,128)S(1)}, u32[]{:S(2)}, u32[]{:S(2)}) collective-permute-start(f32[3,64,512]{2,1,0:T(8,128)} %get-tuple-element.20), channel_id=1, source_target_pairs={{0,8},{8,16},{16,24},{24,32},{32,40},{40,48},{48,56},{56,64},{64,7... | collective-permute-start | bytes 1179656 | tf_op jit(solution)/shard_map/ppermute | solution.py:454
  100.4 33.8 %copy-start.8 = (bf16[2,2,256,256]{3,2,1,0:T(8,128)(2,1)S(1)}, bf16[2,2,256,256]{3,2,1,0:T(8,128)(2,1)}, u32[]{:S(2)}) copy-start(bf16[2,2,256,256]{3,2,1,0:T(8,128)(2,1)} %constant.20.clone.forward_ref) | copy-start | bytes 1572868
  100.4 33.8 %copy-start.18 = (f32[1,512]{1,0:T(1,128)S(1)}, f32[1,512]{1,0:T(1,128)}, u32[]{:S(2)}) copy-start(f32[1,512]{1,0:T(1,128)} %constant.33.r_ref.refs_9_) | copy-start | bytes 6148
  100.5 33.7 %collective-permute-start.7 = (f32[3,64,512]{2,1,0:T(8,128)S(1)}, f32[3,64,512]{2,1,0:T(8,128)S(1)}, u32[]{:S(2)}, u32[]{:S(2)}) collective-permute-start(f32[3,64,512]{2,1,0:T(8,128)S(1)} %get-tuple-element.23), channel_id=1, source_target_pairs={{0,248},{8,0},{16,8},{24,16},{32,24},{40,32},{48,40},{56,48},{64,5... | collective-permute-start | bytes 1179656 | tf_op jit(solution)/shard_map/ppermute | solution.py:454
  107.4 26.8 %collective-permute-start.6 = (f32[3,64,512]{2,1,0:T(8,128)S(1)}, f32[3,64,512]{2,1,0:T(8,128)S(1)}, u32[]{:S(2)}, u32[]{:S(2)}) collective-permute-start(f32[3,64,512]{2,1,0:T(8,128)S(1)} %get-tuple-element.24), channel_id=1, source_target_pairs={{0,8},{8,16},{16,24},{24,32},{32,40},{40,48},{48,56},{56,64},{64,7... | collective-permute-start | bytes 1179656 | tf_op jit(solution)/shard_map/ppermute | solution.py:454
  107.4 16.4 %collective-permute-start.9 = (s32[64,512]{1,0:T(8,128)S(1)}, s32[64,512]{1,0:T(8,128)S(1)}, u32[]{:S(2)}, u32[]{:S(2)}) collective-permute-start(s32[64,512]{1,0:T(8,128)S(1)} %copy-done.33), channel_id=1, source_target_pairs={{0,248},{8,0},{16,8},{24,16},{32,24},{40,32},{48,40},{56,48},{64,5... | collective-permute-start | bytes 393224 | tf_op jit(solution)/shard_map/ppermute | solution.py:454
  117.0 17.2 %collective-permute-start.8 = (s32[64,512]{1,0:T(8,128)S(1)}, s32[64,512]{1,0:T(8,128)S(1)}, u32[]{:S(2)}, u32[]{:S(2)}) collective-permute-start(s32[64,512]{1,0:T(8,128)S(1)} %copy-done.32), channel_id=1, source_target_pairs={{0,8},{8,16},{16,24},{24,32},{32,40},{40,48},{48,56},{56,64},{64,7... | collective-permute-start | bytes 393224 | tf_op jit(solution)/shard_map/ppermute | solution.py:454
  142.0 35.2 %all-to-all-start.1 = ((f32[8,25,512]{2,1,0:T(8,128)}), f32[8,25,512]{2,1,0:T(8,128)S(1)}, u32[]{:S(2)}, u32[]{:S(2)}) async-start(f32[8,25,512]{2,1,0:T(8,128)} %broadcast_in_dim.30), calls=%async_computation.1 | async-start | bytes 1048576 | tf_op jit(solution)/shard_map/all_to_all | solution.py:481
  145.9 31.2 %copy-start.6 = (bf16[2,2,256,256]{3,2,1,0:T(8,128)(2,1)S(1)}, bf16[2,2,256,256]{3,2,1,0:T(8,128)(2,1)}, u32[]{:S(2)}) copy-start(bf16[2,2,256,256]{3,2,1,0:T(8,128)(2,1)} %constant.21.clone.refs_11_) | copy-start | bytes 1572868
  145.9 31.2 %copy-start.10 = (f32[64,1,512]{2,1,0:T(1,128)S(1)}, f32[64,1,512]{2,1,0:T(1,128)}, u32[]{:S(2)}) copy-start(f32[64,1,512]{2,1,0:T(1,128)} %constant.34.refs_8_) | copy-start | bytes 393220
  145.9 31.2 %copy-start.13 = (f32[8,512]{1,0:T(8,128)S(1)}, f32[8,512]{1,0:T(8,128)}, u32[]{:S(2)}) copy-start(f32[8,512]{1,0:T(8,128)} %constant.23.clone.refs_6_) | copy-start | bytes 49156
  145.9 31.2 %copy-start.15 = (f32[8,512]{1,0:T(8,128)S(1)}, f32[8,512]{1,0:T(8,128)}, u32[]{:S(2)}) copy-start(f32[8,512]{1,0:T(8,128)} %constant.22.clone.refs_5_) | copy-start | bytes 49156
  146.0 31.2 %copy-start.20 = (f32[1,512]{1,0:T(1,128)S(1)}, f32[1,512]{1,0:T(1,128)}, u32[]{:S(2)}) copy-start(f32[1,512]{1,0:T(1,128)} %constant.35.refs_10_) | copy-start | bytes 6148
  146.0 25.8 %collective-permute-start.11 = (f32[3,64,512]{2,1,0:T(8,128)S(1)}, f32[3,64,512]{2,1,0:T(8,128)S(1)}, u32[]{:S(2)}, u32[]{:S(2)}) collective-permute-start(f32[3,64,512]{2,1,0:T(8,128)S(1)} %copy-done.31), channel_id=1, source_target_pairs={{0,248},{8,0},{16,8},{24,16},{32,24},{40,32},{48,40},{56,48},{64,5... | collective-permute-start | bytes 1179656 | tf_op jit(solution)/shard_map/ppermute | solution.py:454
  146.1 25.7 %collective-permute-start.10 = (f32[3,64,512]{2,1,0:T(8,128)S(1)}, f32[3,64,512]{2,1,0:T(8,128)S(1)}, u32[]{:S(2)}, u32[]{:S(2)}) collective-permute-start(f32[3,64,512]{2,1,0:T(8,128)S(1)} %copy-done.30), channel_id=1, source_target_pairs={{0,8},{8,16},{16,24},{24,32},{32,40},{40,48},{48,56},{56,64},{64,7... | collective-permute-start | bytes 1179656 | tf_op jit(solution)/shard_map/ppermute | solution.py:454
  (25 other events, 154.6 us)

commit v2 on v1

--- a/solution.py
+++ b/solution.py
@@ -14,7 +14,12 @@
 GROUPS = 8
 BL = 128
 TIME_STEP = 0.25
-VMEM_LIMIT = 40 * 1024 * 1024
+VMEM_LIMIT = 16 * 1024 * 1024
+CUU_ROW = ROWS
+CWW_ROW = CUU_ROW + GROUPS
+CWU_ROW = CWW_ROW + GROUPS
+R_ROW = CWU_ROW + GROUPS
+SWAP_ROW = R_ROW + 1
 
 
 def lane_wave():
@@ -135,16 +140,18 @@
     return out + jnp.dot(high, second, preferred_element_type=jnp.float32)
 
 
-def code_kernel(count_ref, blocks_ref, shift_ref, out_ref):
+def live_ids(count_ref, blocks_ref, s, direction):
     slot = lax.broadcasted_iota(jnp.int32, (1, BL), 1)
+    ids = blocks_ref[s, 0, 0, direction : direction + 1, :]
+    return jnp.where(slot < count_ref[s, 0, 0, direction], ids, -8)
+
+
+def code_kernel(count_ref, blocks_ref, shift_ref, *out_refs):
     row_id = lax.broadcasted_iota(jnp.int32, (ROWS, BL), 0)
     lane_block = lax.broadcasted_iota(jnp.int32, (N, BL), 0) // BL
     for s in range(2):
         for plane in range(2):
-            direction = 1 - plane
-            ids = blocks_ref[pl.ds(s * 2 + direction, 1), :]
-            alive = slot < count_ref[s * 2 + direction]
-            ids = jnp.where(alive, ids, -8)
+            ids = live_ids(count_ref, blocks_ref, s, 1 - plane)
             rows = jnp.where(jnp.broadcast_to(ids >> 2, (ROWS, BL)) == row_id, 1.0, 0.0)
             lanes = jnp.where(jnp.broadcast_to(ids & 3, (N, BL)) == lane_block, 1.0, 0.0)
             moved = lax.dot_general(
@@ -153,22 +160,72 @@
                 (((1,), (1,)), ((), ())),
                 preferred_element_type=jnp.float32,
             )
-            out_ref[s, plane] = shift_ref[s, plane] + 8 * moved.astype(jnp.int32)
+            out_refs[2 * s + plane][...] = shift_ref[s, plane] + 8 * moved.astype(jnp.int32)
 
 
 def codes_of(count, blocks, shifts):
     return pl.pallas_call(
         code_kernel,
-        out_shape=jax.ShapeDtypeStruct((2, 2, ROWS, N), jnp.int32),
+        out_shape=(jax.ShapeDtypeStruct((ROWS, N), jnp.int32),) * 4,
         in_specs=[
             pl.BlockSpec(memory_space=pltpu.SMEM),
             pl.BlockSpec(memory_space=pltpu.VMEM),
             pl.BlockSpec(memory_space=pltpu.VMEM),
         ],
-        out_specs=pl.BlockSpec(memory_space=pltpu.VMEM),
+        out_specs=(pl.BlockSpec(memory_space=pltpu.VMEM),) * 4,
         compiler_params=pltpu.CompilerParams(vmem_limit_bytes=VMEM_LIMIT),
+        cost_estimate=pl.CostEstimate(flops=40_000_000, bytes_accessed=1_000_000, transcendentals=0),
         name="codes",
     )(count, blocks, shifts)
+
+
+def parts_of(x):
+    high = x.astype(jnp.bfloat16)
+    rest = x - high.astype(jnp.float32)
+    middle = rest.astype(jnp.bfloat16)
+    return high, middle, (rest - middle.astype(jnp.float32)).astype(jnp.bfloat16)
+
+
+def chosen_rows(ids, q):
+    row_id = lax.broadcasted_iota(jnp.int32, (ROWS, BL), 0)
+    wide = jnp.broadcast_to(ids, (ROWS, BL))
+    hit = ((wide >> 2) == row_id) & ((wide & 3) == q)
+    return jnp.where(hit, 1.0, 0.0).astype(jnp.bfloat16)
+
+
+def pack_kernel(count_ref, blocks_ref, omega_ref, *out_refs):
+    for s in range(2):
+        for plane in range(2):
+            ids = live_ids(count_ref, blocks_ref, s, 1 - plane)
+            out_ref = out_refs[2 * s + plane]
+            total = jnp.zeros((BL, 3 * BL), jnp.float32)
+            for q in range(4):
+                chosen = chosen_rows(ids, q)
+                lanes = slice(q * BL, (q + 1) * BL)
+                x = jnp.concatenate([omega_ref[s, c, plane, :, lanes] for c in range(3)], axis=1)
+                for part in parts_of(x):
+                    total = total + lax.dot_general(
+                        chosen, part, (((0,), (0,)), ((), ())), preferred_element_type=jnp.float32
+                    )
+            out_ref[0:BL, :] = total
+            out_ref[BL : BL + 8, :] = jnp.zeros((8, 3 * BL), jnp.float32)
+            out_ref[BL : BL + 1, 0:BL] = ids.astype(jnp.float32)
+
+
+def packed_of(count, blocks, omega):
+    return pl.pallas_call(
+        pack_kernel,
+        out_shape=(jax.ShapeDtypeStruct((BL + 8, 3 * BL), jnp.float32),) * 4,
+        in_specs=[
+            pl.BlockSpec(memory_space=pltpu.SMEM),
+            pl.BlockSpec(memory_space=pltpu.VMEM),
+            pl.BlockSpec(memory_space=pltpu.VMEM),
+        ],
+        out_specs=(pl.BlockSpec(memory_space=pltpu.VMEM),) * 4,
+        compiler_params=pltpu.CompilerParams(vmem_limit_bytes=VMEM_LIMIT),
+        cost_estimate=pl.CostEstimate(flops=300_000_000, bytes_accessed=3_000_000, transcendentals=0),
+        name="pack",
+    )(count, blocks, omega)
 
 
 def deposit(own, own_code, other, other_code):
@@ -183,52 +240,74 @@
     return total
 
 
-def omega_kernel(own_ref, below_ref, above_ref, code_ref, cbelow_ref, cabove_ref, out_ref):
-    for plane, other_ref, cother_ref in ((0, below_ref, cbelow_ref), (1, above_ref, cabove_ref)):
+def omega_kernel(
+    s, own_ref, below_ref, above_ref, code0_ref, code1_ref, cbelow_ref, cabove_ref, out_ref, far_ref
+):
+    for plane, other_ref, code_ref, cother_ref in (
+        (0, below_ref, code0_ref, cbelow_ref),
+        (1, above_ref, code1_ref, cabove_ref),
+    ):
+        ids = other_ref[BL : BL + 1, 0:BL].astype(jnp.int32)
+        parts = parts_of(other_ref[0:BL, :])
+        for q in range(4):
+            chosen = chosen_rows(ids, q)
+            total = None
+            for part in parts:
+                term = jnp.dot(chosen, part, preferred_element_type=jnp.float32)
+                total = term if total is None else total + term
+            for c in range(3):
+                far_ref[c, :, q * BL : (q + 1) * BL] = total[:, c * BL : (c + 1) * BL]
 
         @pl.loop(0, ROWS // 8)
-        def _(step, plane=plane, other_ref=other_ref, cother_ref=cother_ref):
+        def _(step, plane=plane, code_ref=code_ref, cother_ref=cother_ref):
             rows = pl.ds(pl.multiple_of(step * 8, 8), 8)
-            own_code = code_ref[plane, rows, :]
+            own_code = code_ref[rows, :]
             other_code = cother_ref[rows, :]
             for c in range(3):
                 out_ref[c, plane, rows, :] = deposit(
-                    own_ref[c, plane, rows, :], own_code, other_ref[c, rows, :], other_code
+                    own_ref[s, c, plane, rows, :], own_code, far_ref[c, rows, :], other_code
                 )
 
 
-def omega_of(own, below, above, code, cbelow, cabove):
+def omega_of(s, *args):
+    def body(*refs):
+        omega_kernel(s, *refs)
+
     return pl.pallas_call(
-        omega_kernel,
+        body,
         out_shape=jax.ShapeDtypeStruct((3, 2, ROWS, N), jnp.float32),
-        in_specs=[pl.BlockSpec(memory_space=pltpu.VMEM)] * 6,
+        in_specs=[pl.BlockSpec(memory_space=pltpu.VMEM)] * 7,
         out_specs=pl.BlockSpec(memory_space=pltpu.VMEM),
+        scratch_shapes=[pltpu.VMEM((3, ROWS, N), jnp.float32)],
         compiler_params=pltpu.CompilerParams(vmem_limit_bytes=VMEM_LIMIT),
-        cost_estimate=pl.CostEstimate(flops=30_000_000, bytes_accessed=6_000_000, transcendentals=0),
+        cost_estimate=pl.CostEstimate(flops=300_000_000, bytes_accessed=6_000_000, transcendentals=0),
         name="omega",
-    )(own, below, above, code, cbelow, cabove)
+    )(*args)
 
 
 SUBLANE = (0, 4, 12)
 
 
 def first_kernel(
-    own_ref, below_ref, above_ref, code_ref, cbelow_ref, cabove_ref, forward_ref, r_ref,
-    lam_ref, u_ref, ends_ref, x_ref, h_ref,
+    own0_ref, own1_ref, below_ref, above_ref, code0_ref, code1_ref, cbelow_ref, cabove_ref,
+    forward_ref, table_ref, lam_ref, u_ref, ends_ref, x_ref, h_ref,
 ):
-    for plane, other, other_ref, cother_ref in (
-        (0, 0, below_ref, cbelow_ref),
-        (1, 3, above_ref, cabove_ref),
+    for plane, other, own_ref, other_ref, code_ref, cother_ref in (
+        (0, 0, own0_ref, below_ref, code0_ref, cbelow_ref),
+        (1, 3, own1_ref, above_ref, code1_ref, cabove_ref),
     ):
 
         @pl.loop(0, ROWS // 8)
-        def _(step, plane=plane, other=other, other_ref=other_ref, cother_ref=cother_ref):
+        def _(
+            step, plane=plane, other=other, own_ref=own_ref, other_ref=other_ref,
+            code_ref=code_ref, cother_ref=cother_ref,
+        ):
             start = pl.multiple_of(step * 8, 8)
             rows = pl.ds(start, 8)
-            own_code = code_ref[plane, rows, :]
+            own_code = code_ref[rows, :]
             other_code = cother_ref[rows, :]
             for c in range(3):
-                own = own_ref[c, plane, rows, :]
+                own = own_ref[c, rows, :]
                 far = other_ref[c, rows, :]
                 here = deposit(own, own_code, far, other_code)
                 there = deposit(far, other_code, own, own_code)
@@ -250,7 +329,7 @@
                         base : base + ROWS, part * BL : (part + 1) * BL
                     ]
 
-    r = [jnp.broadcast_to(r_ref[:, q * BL : (q + 1) * BL], (16, BL)) for q in range(4)]
+    r = [jnp.broadcast_to(table_ref[R_ROW, :, q * BL : (q + 1) * BL], (16, BL)) for q in range(4)]
     zero = jnp.zeros((16, BL), jnp.float32)
 
     def ahead(y, carry):
@@ -285,7 +364,7 @@
     ends_ref[24:25, 0:BL] = jnp.sum(jnp.where(used, sums, 0.0), axis=0, keepdims=True)
 
 
-def first_of(own, below, above, code, cbelow, cabove, forward, r):
+def first_of(*args):
     return pl.pallas_call(
         first_kernel,
         out_shape=(
@@ -293,7 +372,7 @@
             jax.ShapeDtypeStruct((4, ROWS * 16, BL), jnp.float32),
             jax.ShapeDtypeStruct((25, N), jnp.float32),
         ),
-        in_specs=[pl.BlockSpec(memory_space=pltpu.VMEM)] * 8,
+        in_specs=[pl.BlockSpec(memory_space=pltpu.VMEM)] * 10,
         out_specs=(pl.BlockSpec(memory_space=pltpu.VMEM),) * 3,
         scratch_shapes=[
             pltpu.VMEM((12 * ROWS, N), jnp.float32),
@@ -302,14 +381,16 @@
         compiler_params=pltpu.CompilerParams(vmem_limit_bytes=VMEM_LIMIT),
         cost_estimate=pl.CostEstimate(flops=3_000_000_000, bytes_accessed=8_000_000, transcendentals=0),
         name="first",
-    )(own, below, above, code, cbelow, cabove, forward, r)
+    )(*args)
 
 
 def second_kernel(
-    zero_u, zero_z,
-    me_ref, ends_ref, u_ref, lam_ref, omega_ref, cuu_ref, cww_ref, cwu_ref, rpow_ref, r_ref,
-    swap_ref, inverse_ref, out_ref, y_ref, field_ref,
+    zero_u, zero_z, last, me_ref, *refs
 ):
+    ends_refs = refs[:GROUPS]
+    u_ref, lam_ref, omega_ref, table_ref, inverse_ref = refs[GROUPS : GROUPS + 5]
+    out_refs = refs[GROUPS + 5 : -2]
+    y_ref, field_ref = refs[-2:]
     me = me_ref[0]
     u_in = [[jnp.zeros((8, BL), jnp.float32)] * 2 for _ in range(4)]
     w_in = [[jnp.zeros((8, BL), jnp.float32)] * 2 for _ in range(4)]
@@ -317,21 +398,22 @@
     w_sum = [jnp.zeros((8, BL), jnp.float32)] * 2
     z_row = jnp.zeros((1, BL), jnp.float32)
     for step in range(GROUPS):
-        who = (me + step) & (GROUPS - 1)
+        ends_ref = ends_refs[step]
+        who = (me ^ step) - me & (GROUPS - 1)
         for q in range(4):
             lanes = pl.ds(q * BL, BL)
-            uu = cuu_ref[step : step + 1, lanes]
-            ww = cww_ref[step : step + 1, lanes]
-            wu = cwu_ref[step : step + 1, lanes]
+            uu = table_ref[CUU_ROW + who, :, lanes]
+            ww = table_ref[CWW_ROW + who, :, lanes]
+            wu = table_ref[CWU_ROW + who, :, lanes]
             for g in range(2):
-                u = ends_ref[who, 4 * g : 4 * g + 8, lanes]
-                w = ends_ref[who, 12 + 4 * g : 20 + 4 * g, lanes]
+                u = ends_ref[4 * g : 4 * g + 8, lanes]
+                w = ends_ref[12 + 4 * g : 20 + 4 * g, lanes]
                 u_in[q][g] = u_in[q][g] + uu * u
                 w_in[q][g] = w_in[q][g] + (ww * w + wu * u)
                 if q == 0:
                     u_sum[g] = u_sum[g] + u
                     w_sum[g] = w_sum[g] + w
-        z_row = z_row + ends_ref[step, 24:25, 0:BL]
+        z_row = z_row + ends_ref[24:25, 0:BL]
     lane = lax.broadcasted_iota(jnp.int32, (8, BL), 1)
     sub = lax.broadcasted_iota(jnp.int32, (8, BL), 0)
     first_lane = lane == 0
@@ -343,8 +425,10 @@
         z_total = jnp.broadcast_to(jnp.sum(mine, axis=1, keepdims=True), (8, BL))
         w_in[0][g] = w_in[0][g] + jnp.where(first_lane, zero_z * z_total, 0.0)
 
-    r = [jnp.broadcast_to(r_ref[:, q * BL : (q + 1) * BL], (8, BL)) for q in range(4)]
-    swap = [jnp.broadcast_to(swap_ref[:, q * BL : (q + 1) * BL], (8, BL)) for q in range(4)]
+    r = [jnp.broadcast_to(table_ref[R_ROW, :, q * BL : (q + 1) * BL], (8, BL)) for q in range(4)]
+    swap = [
+        jnp.broadcast_to(table_ref[SWAP_ROW, :, q * BL : (q + 1) * BL], (8, BL)) for q in range(4)
+    ]
     upper = sub < 4
 
     def emit(y, after, here, before):
@@ -363,7 +447,7 @@
         after, here = carry[:8], carry[8:]
         new = []
         for q in range(4):
-            power = rpow_ref[y, :, q * BL : (q + 1) * BL]
+            power = table_ref[y, :, q * BL : (q + 1) * BL]
             for g in range(2):
                 at = pl.ds(pl.multiple_of(y * 16 + 8 * g, 8), 8)
                 value = u_ref[q, at, :] + power * u_in[q][g]
@@ -376,7 +460,7 @@
     edge = tuple(w_in[q][g] for q in range(4) for g in range(2))
     new = []
     for q in range(4):
-        power = rpow_ref[ROWS - 1, :, q * BL : (q + 1) * BL]
+        power = table_ref[ROWS - 1, :, q * BL : (q + 1) * BL]
         for g in range(2):
             value = u_ref[q, (ROWS - 1) * 16 + 8 * g : (ROWS - 1) * 16 + 8 * g + 8, :]
             value = value + power * u_in[q][g]
@@ -424,21 +508,27 @@
             )
             for c in range(3):
                 slope = 0.5 * (g[plane + 2][c] - g[plane][c])
-                out_ref[c, plane, rows, :] = lam_ref[c, plane, rows, :] + TIME_STEP * (
-                    cross[c] + w[0] * slope
-                )
-
-
-def second_of(t, me, ends, u, lam, omega, cuu, cww, cwu, rpow, r, swap, inverse):
+                new = lam_ref[c, plane, rows, :] + TIME_STEP * (cross[c] + w[0] * slope)
+                if last:
+                    out_refs[0][c, plane, rows, :] = new
+                else:
+                    out_refs[plane][c, rows, :] = new
+
+
+def second_of(t, last, *args):
     def body(*refs):
-        second_kernel(t["zero_u"], t["zero_z"], *refs)
-
+        second_kernel(t["zero_u"], t["zero_z"], last, *refs)
+
+    if last:
+        shapes = (jax.ShapeDtypeStruct((3, 2, ROWS, N), jnp.float32),)
+    else:
+        shapes = (jax.ShapeDtypeStruct((3, ROWS, N), jnp.float32),) * 2
     return pl.pallas_call(
         body,
-        out_shape=jax.ShapeDtypeStruct((3, 2, ROWS, N), jnp.float32),
+        out_shape=shapes,
         in_specs=[pl.BlockSpec(memory_space=pltpu.SMEM)]
-        + [pl.BlockSpec(memory_space=pltpu.VMEM)] * 11,
-        out_specs=pl.BlockSpec(memory_space=pltpu.VMEM),
+        + [pl.BlockSpec(memory_space=pltpu.VMEM)] * (GROUPS + 5),
+        out_specs=(pl.BlockSpec(memory_space=pltpu.VMEM),) * len(shapes),
         scratch_shapes=[
             pltpu.VMEM((ROWS * 16, N), jnp.float32),
             pltpu.VMEM((4, ROWS * 16, BL), jnp.float32),
@@ -446,7 +536,7 @@
         compiler_params=pltpu.CompilerParams(vmem_limit_bytes=VMEM_LIMIT),
         cost_estimate=pl.CostEstimate(flops=4_000_000_000, bytes_accessed=8_000_000, transcendentals=0),
         name="second",
-    )(me, ends, u, lam, omega, cuu, cww, cwu, rpow, r, swap, inverse)
+    )(*args)
 
 
 def shifted(value, axis, by):
@@ -458,34 +548,41 @@
     return shifted(upper_plane, "slab", 1), shifted(lower_plane, "slab", -1)
 
 
+def crossed(value, mask):
+    return lax.ppermute(value, "pencil", [(i, i ^ mask) for i in range(GROUPS)])
+
+
+def gathered(ends):
+    far = [ends] + [crossed(ends, 2 * d) for d in (1, 2, 3)]
+    out = []
+    for value in far:
+        out += [value, crossed(value, 1)]
+    return out
+
+
 def shards(adjoint_vort, omega_ckpt, cell_shift, move_count, move_blocks):
     t = tables()
     forward, inverse = halves(t["forward"]), halves(t["inverse"])
-    f32 = {k: jnp.asarray(t[k], jnp.float32) for k in ("cuu", "cww", "cwu", "rpow")}
-    r = jnp.asarray(t["r"], jnp.float32)[None]
-    swap = jnp.asarray(t["swap"], jnp.float32)[None]
+    rows = [t["rpow"], t["cuu"], t["cww"], t["cwu"], t["r"][None], t["swap"][None]]
+    table = jnp.asarray(np.concatenate(rows)[:, None], jnp.float32)
     me = lax.axis_index("pencil").astype(jnp.int32)[None]
 
-    lam = adjoint_vort
-    code = codes_of(move_count.reshape(4), move_blocks.reshape(4, BL), cell_shift)
-    below, above = neighbours(lam[:, 0], lam[:, 1])
-    far_code = [neighbours(code[s, 0], code[s, 1]) for s in range(2)]
-    omega = []
-    for s in range(2):
-        far = neighbours(omega_ckpt[s, :, 0], omega_ckpt[s, :, 1])
-        omega.append(omega_of(omega_ckpt[s], *far, code[s], *far_code[s]))
+    lam0, lam1 = adjoint_vort[:, 0], adjoint_vort[:, 1]
+    below, above = neighbours(lam0, lam1)
+    code = codes_of(move_count, move_blocks, cell_shift)
+    far_code = [neighbours(code[2 * s], code[2 * s + 1]) for s in range(2)]
+    packed = packed_of(move_count, move_blocks, omega_ckpt)
+    far_omega = [neighbours(packed[2 * s], packed[2 * s + 1]) for s in range(2)]
     for s in range(2):
         if s:
-            below, above = neighbours(lam[:, 0], lam[:, 1])
-        lam_r, u, ends = first_of(lam, below, above, code[s], *far_code[s], forward, r)
-        gathered = lax.all_to_all(
-            jnp.broadcast_to(ends[None], (GROUPS, 25, N)), "pencil", 0, 0, tiled=True
-        )
-        lam = second_of(
-            t, me, gathered, u, lam_r, omega[s], f32["cuu"], f32["cww"], f32["cwu"],
-            f32["rpow"][:, None], r, swap, inverse,
-        )
-    return lam
+            below, above = neighbours(lam0, lam1)
+        codes = (code[2 * s], code[2 * s + 1], *far_code[s])
+        omega = omega_of(s, omega_ckpt, *far_omega[s], *codes)
+        lam_r, u, ends = first_of(lam0, lam1, below, above, *codes, forward, table)
+        out = second_of(t, s == 1, me, *gathered(ends), u, lam_r, omega, table, inverse)
+        if s == 0:
+            lam0, lam1 = out
+    return out[0]
 
 
 def solution(mesh):

time: 184 us -> 123 us (0.67)
  waiting for transfers between devices: 90.5 us -> 19.8 us
  starting transfers between devices: 49.6 us -> 70.1 us
  local copies, waits for them, and re-layouts: 21.9 us -> 7.07 us
  Pallas kernels: 20.9 us -> 25.4 us
    ppermute x12, waiting for transfers between devices: 86.1 us -> 16.5 us  [shifted(): lax.ppermute(value, axis, [(i, (i + by) % count) for i in range(count)])]
    ppermute x0 -> x14, starting transfers between devices: none -> 21.1 us  [crossed(): return lax.ppermute(value, 'pencil', [(i, i ^ mask) for i in range(GROUPS)])]
    unnamed x71 -> x26, local copies, waits for them, and re-layouts: 15.2 us -> 5.79 us
    all_to_all x2 -> x0, starting transfers between devices: 7.97 us -> none  [shards(): lax.all_to_all(jnp.broadcast_to(ends[None], (GROUPS, 25, N)), 'pencil', 0...]
    ppermute x12, starting transfers between devices: 41.6 us -> 49 us  [shifted(): lax.ppermute(value, axis, [(i, (i + by) % count) for i in range(count)])]
    pallas_call x5 -> x6, Pallas kernels: 11.5 us -> 16 us  [the longest x2 7.85 us: second_of(): pl.pallas_call(body, out_shape=shapes, in_specs=[pl.BlockSpec(memory_spac...]
    all_to_all x2 -> x0, waiting for transfers between devices: 4.45 us -> none  [shards(): lax.all_to_all(jnp.broadcast_to(ends[None], (GROUPS, 25, N)), 'pencil', 0...]
    squeeze x6 -> x1, local copies, waits for them, and re-layouts: 4.8 us -> 1.29 us  [shards(): lam0, lam1 = (adjoint_vort[:, 0], adjoint_vort[:, 1])]
  transfers between devices with their start and end apart: 14 -> 26, of which waited for: 9 -> 5; matrix products, arithmetic and copies ran while one was open for 3% -> 0% of each run, Pallas kernels for 3% -> 14%
where the time goes in v2:
time: 123 us
  starting transfers between devices  70.1 us (57%)
  Pallas kernels  25.4 us (21%)
  waiting for transfers between devices  19.8 us (16%)
  local copies, waits for them, and re-layouts  7.07 us (6%)
    ppermute x12, starting transfers between devices, shifted(): lax.ppermute(value, axis, [(i, (i + by) % count) for i in range(count)])  49 us
    ppermute x14, starting transfers between devices, crossed(): return lax.ppermute(value, 'pencil', [(i, i ^ mask) for i in range(GROUPS)])  21.1 us
    ppermute x12, waiting for transfers between devices, shifted(): lax.ppermute(value, axis, [(i, (i + by) % count) for i in range(count)])  16.5 us
    pallas_call x2, Pallas kernels, first_of(): pl.pallas_call(first_kernel, out_shape=(jax.ShapeDtypeStruct((3, 2, ROWS,...  9.42 us
    pallas_call x2, Pallas kernels, second_of(): pl.pallas_call(body, out_shape=shapes, in_specs=[pl.BlockSpec(memory_spac...  7.85 us
    unnamed x26, local copies, waits for them, and re-layouts  5.79 us
    pallas_call x2, Pallas kernels, omega_of(): pl.pallas_call(body, out_shape=jax.ShapeDtypeStruct((3, 2, ROWS, N), jnp....  5.33 us
    ppermute x14, waiting for transfers between devices, crossed(): return lax.ppermute(value, 'pencil', [(i, i ^ mask) for i in range(GROUPS)])  3.38 us
  transfers between devices with their start and end apart: 26, of which 5 were waited for; matrix products, arithmetic and copies ran while one was open for 0% of the time, Pallas kernels for 14%

profile of v2, /device:TPU:1, one launch (start us, length us, event | category | flops | bytes accessed | tf_op | source)
XLA Modules:
  0.0 122.6 jit_solution(11698380567224336886)
XLA Ops:
  1.3 2.2 %collective-permute-start = (f32[3,64,512]{2,1,0:T(8,128)S(1)}, f32[3,64,512]{2,1,0:T(8,128)S(1)}, u32[]{:S(2)}, u32[]{:S(2)}) collective-permute-start(f32[3,64,512]{2,1,0:T(8,128)S(1)} %get-tuple-element.37.own1_ref), channel_id=1, source_target_pairs={{0,8},{8,16},{16,24},{24,32},{32,40},{40,48},{48,56},{56,64},{64,7... | collective-permute-start | bytes 1179656 | tf_op jit(solution)/shard_map/ppermute | solution.py:544
  3.5 10.3 %collective-permute-start.1 = (f32[3,64,512]{2,1,0:T(8,128)S(1)}, f32[3,64,512]{2,1,0:T(8,128)S(1)}, u32[]{:S(2)}, u32[]{:S(2)}) collective-permute-start(f32[3,64,512]{2,1,0:T(8,128)S(1)} %get-tuple-element.38.own0_ref), channel_id=1, source_target_pairs={{0,248},{8,0},{16,8},{24,16},{32,24},{40,32},{48,40},{56,48},{64,5... | collective-permute-start | bytes 1179656 | tf_op jit(solution)/shard_map/ppermute | solution.py:544
  17.2 9.6 %collective-permute-start.3 = (s32[64,512]{1,0:T(8,128)S(1)}, s32[64,512]{1,0:T(8,128)S(1)}, u32[]{:S(2)}, u32[]{:S(2)}) collective-permute-start(s32[64,512]{1,0:T(8,128)S(1)} %get-tuple-element.21.code0_ref.refs_3_), channel_id=1, source_target_pairs={{0,248},{8,0},{16,8},{24,16},{32,24},{40,32},{48,40},{56,48},{64,5... | collective-permute-start | bytes 393224 | tf_op jit(solution)/shard_map/ppermute | solution.py:544
  26.8 2.0 %pack.1 = (f32[136,384]{1,0:T(8,128)S(1)}, f32[136,384]{1,0:T(8,128)S(1)}, f32[136,384]{1,0:T(8,128)S(1)}, f32[136,384]{1,0:T(8,128)S(1)}) custom-call(s32[2,1,1,2]{3,2,1,0:T(1,128)S(1)} %copy-done.3, s32[2,1,1,2,128]{4,3,2,1,0:T(2,128)S(1)} %copy-done.2, f32[2,3,2,64,512]{4,3,2,1,0:T(8,128)S(1)} %copy-done), custom_call_target="tpu_custom_call" | custom-call | flops 300000000 | bytes 3000000 | tf_op jit(solution)/shard_map/pack/pallas_call | solution.py:216
  28.8 2.1 %collective-permute-done.2.cbelow_ref.refs_5_ = s32[64,512]{1,0:T(8,128)S(1)} collective-permute-done((s32[64,512]{1,0:T(8,128)S(1)}, s32[64,512]{1,0:T(8,128)S(1)}, u32[]{:S(2)}, u32[]{:S(2)}) %collective-permute-start.2) | collective-permute-done | bytes 131104 | tf_op jit(solution)/shard_map/ppermute | solution.py:544
  30.9 7.5 %collective-permute-start.12 = (f32[136,384]{1,0:T(8,128)S(1)}, f32[136,384]{1,0:T(8,128)S(1)}, u32[]{:S(2)}, u32[]{:S(2)}) collective-permute-start(f32[136,384]{1,0:T(8,128)S(1)} %get-tuple-element.27), channel_id=1, source_target_pairs={{0,248},{8,0},{16,8},{24,16},{32,24},{40,32},{48,40},{56,48},{64,5... | collective-permute-start | bytes 626696 | tf_op jit(solution)/shard_map/ppermute | solution.py:544
  38.5 4.7 %first.2 = (f32[3,2,64,512]{3,2,1,0:T(8,128)S(1)}, f32[4,1024,128]{2,1,0:T(8,128)S(1)}, f32[25,512]{1,0:T(8,128)S(1)}) custom-call(f32[3,64,512]{2,1,0:T(8,128)S(1)} %get-tuple-element.38.own0_ref, f32[3,64,512]{2,1,0:T(8,128)S(1)} %get-tuple-element.37.own1_ref, f32[3,64,512]{2,1,0:T(8,128)S(1)} %collective-permute-done.below_ref, ...), custom_call_target="tpu_custom_call" | custom-call | flops 3000000000 | bytes 8000000 | tf_op jit(solution)/shard_map/first/pallas_call | solution.py:368
  43.2 1.4 %copy-done.9 = f32[4,1024,128]{2,1,0:T(8,128)} copy-done((f32[4,1024,128]{2,1,0:T(8,128)}, f32[4,1024,128]{2,1,0:T(8,128)S(1)}, u32[]{:S(2)}) %copy-start.9) | copy-done | bytes 2097176
  45.4 2.3 %collective-permute-start.9 = (f32[25,512]{1,0:T(8,128)S(1)}, f32[25,512]{1,0:T(8,128)S(1)}, u32[]{:S(2)}, u32[]{:S(2)}) collective-permute-start(f32[25,512]{1,0:T(8,128)S(1)} %get-tuple-element.23.refs_1_), channel_id=1, source_target_pairs={{0,6},{1,7},{2,4},{3,5},{4,2},{5,3},{6,0},{7,1},{8,14},{9,15},{10,... | collective-permute-start | bytes 153608 | tf_op jit(solution)/shard_map/ppermute | solution.py:552
  49.0 2.9 %collective-permute-start.4 = (f32[25,512]{1,0:T(8,128)S(1)}, f32[25,512]{1,0:T(8,128)}, u32[]{:S(2)}, u32[]{:S(2)}) collective-permute-start(f32[25,512]{1,0:T(8,128)S(1)} %get-tuple-element.23.refs_1_), channel_id=1, source_target_pairs={{0,1},{1,0},{2,3},{3,2},{4,5},{5,4},{6,7},{7,6},{8,9},{9,8},{10,11... | collective-permute-start | bytes 153608 | tf_op jit(solution)/shard_map/ppermute | solution.py:552
  52.6 1.6 %collective-permute-start.10 = (f32[25,512]{1,0:T(8,128)S(1)}, f32[25,512]{1,0:T(8,128)}, u32[]{:S(2)}, u32[]{:S(2)}) collective-permute-start(f32[25,512]{1,0:T(8,128)S(1)} %collective-permute-done.9.refs_7_), channel_id=1, source_target_pairs={{0,1},{1,0},{2,3},{3,2},{4,5},{5,4},{6,7},{7,6},{8,9},{9,8},{10,11... | collective-permute-start | bytes 153608 | tf_op jit(solution)/shard_map/ppermute | solution.py:552
  54.9 2.6 %collective-permute-done.7.refs_5_ = f32[25,512]{1,0:T(8,128)} collective-permute-done((f32[25,512]{1,0:T(8,128)S(1)}, f32[25,512]{1,0:T(8,128)}, u32[]{:S(2)}, u32[]{:S(2)}) %collective-permute-start.7) | collective-permute-done | bytes 51232 | tf_op jit(solution)/shard_map/ppermute | solution.py:552
  58.0 2.7 %omega.2.refs_11_ = f32[3,2,64,512]{3,2,1,0:T(8,128)S(1)} custom-call(f32[2,3,2,64,512]{4,3,2,1,0:T(8,128)S(1)} %copy-done, f32[136,384]{1,0:T(8,128)S(1)} %collective-permute-done.11.refs_1_, f32[136,384]{1,0:T(8,128)S(1)} %collective-permute-done.12.refs_2_, s32[64,512]{1,0:T(8,128)S(1)} %get-tuple-element.21.code0_ref.refs_3_, ...), custom_call_target="tpu_custom_call" | custom-call | flops 300000000 | bytes 6000000 | tf_op jit(solution)/shard_map/omega/pallas_call | solution.py:276
  61.8 4.0 %second.2 = (f32[3,64,512]{2,1,0:T(8,128)S(1)}, f32[3,64,512]{2,1,0:T(8,128)S(1)}) custom-call(s32[1]{0:T(128)} %bitcast.refs_0_, f32[25,512]{1,0:T(8,128)S(1)} %get-tuple-element.23.refs_1_, f32[25,512]{1,0:T(8,128)} %collective-permute-done.4.refs_2_, f32[25,512]{1,0:T(8,128)} %collective-permute-done.5.refs_3_, f32[25,512]{1,0:T(8,128)} %collective-permute-done.6.refs_4_, ...), custom_call_target="tpu_custom_call" | custom-call | flops 4000000000 | bytes 8000000 | tf_op jit(solution)/shard_map/second/pallas_call | solution.py:526
  65.9 9.6 %collective-permute-start.14 = (f32[3,64,512]{2,1,0:T(8,128)S(1)}, f32[3,64,512]{2,1,0:T(8,128)S(1)}, u32[]{:S(2)}, u32[]{:S(2)}) collective-permute-start(f32[3,64,512]{2,1,0:T(8,128)S(1)} %get-tuple-element.28.own0_ref), channel_id=1, source_target_pairs={{0,248},{8,0},{16,8},{24,16},{32,24},{40,32},{48,40},{56,48},{64,5... | collective-permute-start | bytes 1179656 | tf_op jit(solution)/shard_map/ppermute | solution.py:544
  75.5 9.6 %collective-permute-start.16 = (s32[64,512]{1,0:T(8,128)S(1)}, s32[64,512]{1,0:T(8,128)S(1)}, u32[]{:S(2)}, u32[]{:S(2)}) collective-permute-start(s32[64,512]{1,0:T(8,128)S(1)} %get-tuple-element.30.code0_ref.refs_3_), channel_id=1, source_target_pairs={{0,248},{8,0},{16,8},{24,16},{32,24},{40,32},{48,40},{56,48},{64,5... | collective-permute-start | bytes 393224 | tf_op jit(solution)/shard_map/ppermute | solution.py:544
  85.1 13.8 %collective-permute-done.15.cbelow_ref.refs_5_ = s32[64,512]{1,0:T(8,128)S(1)} collective-permute-done((s32[64,512]{1,0:T(8,128)S(1)}, s32[64,512]{1,0:T(8,128)S(1)}, u32[]{:S(2)}, u32[]{:S(2)}) %collective-permute-start.15) | collective-permute-done | bytes 131104 | tf_op jit(solution)/shard_map/ppermute | solution.py:544
  98.9 4.7 %first.3 = (f32[3,2,64,512]{3,2,1,0:T(8,128)S(1)}, f32[4,1024,128]{2,1,0:T(8,128)S(1)}, f32[25,512]{1,0:T(8,128)S(1)}) custom-call(f32[3,64,512]{2,1,0:T(8,128)S(1)} %get-tuple-element.28.own0_ref, f32[3,64,512]{2,1,0:T(8,128)S(1)} %get-tuple-element.29.own1_ref, f32[3,64,512]{2,1,0:T(8,128)S(1)} %collective-permute-done.13.below_ref, ...), custom_call_target="tpu_custom_call" | custom-call | flops 3000000000 | bytes 8000000 | tf_op jit(solution)/shard_map/first/pallas_call | solution.py:368
  103.7 1.5 %collective-permute-start.20 = (f32[25,512]{1,0:T(8,128)S(1)}, f32[25,512]{1,0:T(8,128)S(1)}, u32[]{:S(2)}, u32[]{:S(2)}) collective-permute-start(f32[25,512]{1,0:T(8,128)S(1)} %get-tuple-element.32.refs_1_), channel_id=1, source_target_pairs={{0,4},{1,5},{2,6},{3,7},{4,0},{5,1},{6,2},{7,3},{8,12},{9,13},{10,... | collective-permute-start | bytes 153608 | tf_op jit(solution)/shard_map/ppermute | solution.py:552
  105.2 2.0 %collective-permute-start.22 = (f32[25,512]{1,0:T(8,128)S(1)}, f32[25,512]{1,0:T(8,128)S(1)}, u32[]{:S(2)}, u32[]{:S(2)}) collective-permute-start(f32[25,512]{1,0:T(8,128)S(1)} %get-tuple-element.32.refs_1_), channel_id=1, source_target_pairs={{0,6},{1,7},{2,4},{3,5},{4,2},{5,3},{6,0},{7,1},{8,14},{9,15},{10,... | collective-permute-start | bytes 153608 | tf_op jit(solution)/shard_map/ppermute | solution.py:552
  107.8 4.2 %collective-permute-start.17 = (f32[25,512]{1,0:T(8,128)S(1)}, f32[25,512]{1,0:T(8,128)S(1)}, u32[]{:S(2)}, u32[]{:S(2)}) collective-permute-start(f32[25,512]{1,0:T(8,128)S(1)} %get-tuple-element.32.refs_1_), channel_id=1, source_target_pairs={{0,1},{1,0},{2,3},{3,2},{4,5},{5,4},{6,7},{7,6},{8,9},{9,8},{10,11... | collective-permute-start | bytes 153608 | tf_op jit(solution)/shard_map/ppermute | solution.py:552
  112.7 3.4 %collective-permute-start.21 = (f32[25,512]{1,0:T(8,128)S(1)}, f32[25,512]{1,0:T(8,128)S(1)}, u32[]{:S(2)}, u32[]{:S(2)}) collective-permute-start(f32[25,512]{1,0:T(8,128)S(1)} %collective-permute-done.20.refs_5_), channel_id=1, source_target_pairs={{0,1},{1,0},{2,3},{3,2},{4,5},{5,4},{6,7},{7,6},{8,9},{9,8},{10,11... | collective-permute-start | bytes 153608 | tf_op jit(solution)/shard_map/ppermute | solution.py:552
  116.1 2.7 %omega.3.refs_11_ = f32[3,2,64,512]{3,2,1,0:T(8,128)S(1)} custom-call(f32[2,3,2,64,512]{4,3,2,1,0:T(8,128)S(1)} %copy-done, f32[136,384]{1,0:T(8,128)S(1)} %collective-permute-done.24.refs_1_, f32[136,384]{1,0:T(8,128)S(1)} %collective-permute-done.25.refs_2_, s32[64,512]{1,0:T(8,128)S(1)} %get-tuple-element.30.code0_ref.refs_3_, ...), custom_call_target="tpu_custom_call" | custom-call | flops 300000000 | bytes 6000000 | tf_op jit(solution)/shard_map/omega/pallas_call | solution.py:276
  118.8 3.8 %second.3 = f32[3,2,64,512]{3,2,1,0:T(8,128)} custom-call(s32[1]{0:T(128)} %bitcast.refs_0_, f32[25,512]{1,0:T(8,128)S(1)} %get-tuple-element.32.refs_1_, f32[25,512]{1,0:T(8,128)S(1)} %collective-permute-done.17.refs_2_, f32[25,512]{1,0:T(8,128)S(1)} %collective-permute-done.18.refs_3_, f32[25,512]{1,0:T(8,128)S(1)} %collective-permute-done.19.refs_4_, ...), custom_call_target="tpu_custom_call" | custom-call | flops 4000000000 | bytes 8000000 | tf_op jit(solution)/shard_map/second/pallas_call | solution.py:526
  (63 shorter events, 11.4 us)
Async XLA Ops:
  1.3 37.1 %collective-permute-start = (f32[3,64,512]{2,1,0:T(8,128)S(1)}, f32[3,64,512]{2,1,0:T(8,128)S(1)}, u32[]{:S(2)}, u32[]{:S(2)}) collective-permute-start(f32[3,64,512]{2,1,0:T(8,128)S(1)} %get-tuple-element.37.own1_ref), channel_id=1, source_target_pairs={{0,8},{8,16},{16,24},{24,32},{32,40},{40,48},{48,56},{56,64},{64,7... | collective-permute-start | bytes 1179656 | tf_op jit(solution)/shard_map/ppermute | solution.py:544
  3.5 34.9 %collective-permute-start.1 = (f32[3,64,512]{2,1,0:T(8,128)S(1)}, f32[3,64,512]{2,1,0:T(8,128)S(1)}, u32[]{:S(2)}, u32[]{:S(2)}) collective-permute-start(f32[3,64,512]{2,1,0:T(8,128)S(1)} %get-tuple-element.38.own0_ref), channel_id=1, source_target_pairs={{0,248},{8,0},{16,8},{24,16},{32,24},{40,32},{48,40},{56,48},{64,5... | collective-permute-start | bytes 1179656 | tf_op jit(solution)/shard_map/ppermute | solution.py:544
  17.1 13.8 %collective-permute-start.2 = (s32[64,512]{1,0:T(8,128)S(1)}, s32[64,512]{1,0:T(8,128)S(1)}, u32[]{:S(2)}, u32[]{:S(2)}) collective-permute-start(s32[64,512]{1,0:T(8,128)S(1)} %get-tuple-element.22.code1_ref.refs_4_), channel_id=1, source_target_pairs={{0,8},{8,16},{16,24},{24,32},{32,40},{40,48},{48,56},{56,64},{64,7... | collective-permute-start | bytes 393224 | tf_op jit(solution)/shard_map/ppermute | solution.py:544
  17.2 21.2 %collective-permute-start.3 = (s32[64,512]{1,0:T(8,128)S(1)}, s32[64,512]{1,0:T(8,128)S(1)}, u32[]{:S(2)}, u32[]{:S(2)}) collective-permute-start(s32[64,512]{1,0:T(8,128)S(1)} %get-tuple-element.21.code0_ref.refs_3_), channel_id=1, source_target_pairs={{0,248},{8,0},{16,8},{24,16},{32,24},{40,32},{48,40},{56,48},{64,5... | collective-permute-start | bytes 393224 | tf_op jit(solution)/shard_map/ppermute | solution.py:544
  28.7 20.2 %collective-permute-start.11 = (f32[136,384]{1,0:T(8,128)S(1)}, f32[136,384]{1,0:T(8,128)S(1)}, u32[]{:S(2)}, u32[]{:S(2)}) collective-permute-start(f32[136,384]{1,0:T(8,128)S(1)} %get-tuple-element.26), channel_id=1, source_target_pairs={{0,8},{8,16},{16,24},{24,32},{32,40},{40,48},{48,56},{56,64},{64,7... | collective-permute-start | bytes 626696 | tf_op jit(solution)/shard_map/ppermute | solution.py:544
  30.9 27.0 %collective-permute-start.12 = (f32[136,384]{1,0:T(8,128)S(1)}, f32[136,384]{1,0:T(8,128)S(1)}, u32[]{:S(2)}, u32[]{:S(2)}) collective-permute-start(f32[136,384]{1,0:T(8,128)S(1)} %get-tuple-element.27), channel_id=1, source_target_pairs={{0,248},{8,0},{16,8},{24,16},{32,24},{40,32},{48,40},{56,48},{64,5... | collective-permute-start | bytes 626696 | tf_op jit(solution)/shard_map/ppermute | solution.py:544
  45.4 7.2 %collective-permute-start.9 = (f32[25,512]{1,0:T(8,128)S(1)}, f32[25,512]{1,0:T(8,128)S(1)}, u32[]{:S(2)}, u32[]{:S(2)}) collective-permute-start(f32[25,512]{1,0:T(8,128)S(1)} %get-tuple-element.23.refs_1_), channel_id=1, source_target_pairs={{0,6},{1,7},{2,4},{3,5},{4,2},{5,3},{6,0},{7,1},{8,14},{9,15},{10,... | collective-permute-start | bytes 153608 | tf_op jit(solution)/shard_map/ppermute | solution.py:552
  47.7 6.5 %collective-permute-start.5 = (f32[25,512]{1,0:T(8,128)S(1)}, f32[25,512]{1,0:T(8,128)}, u32[]{:S(2)}, u32[]{:S(2)}) collective-permute-start(f32[25,512]{1,0:T(8,128)S(1)} %get-tuple-element.23.refs_1_), channel_id=1, source_target_pairs={{0,2},{1,3},{2,0},{3,1},{4,6},{5,7},{6,4},{7,5},{8,10},{9,11},{10,... | collective-permute-start | bytes 153608 | tf_op jit(solution)/shard_map/ppermute | solution.py:552
  47.7 9.7 %collective-permute-start.7 = (f32[25,512]{1,0:T(8,128)S(1)}, f32[25,512]{1,0:T(8,128)}, u32[]{:S(2)}, u32[]{:S(2)}) collective-permute-start(f32[25,512]{1,0:T(8,128)S(1)} %get-tuple-element.23.refs_1_), channel_id=1, source_target_pairs={{0,4},{1,5},{2,6},{3,7},{4,0},{5,1},{6,2},{7,3},{8,12},{9,13},{10,... | collective-permute-start | bytes 153608 | tf_op jit(solution)/shard_map/ppermute | solution.py:552
  49.0 11.7 %collective-permute-start.4 = (f32[25,512]{1,0:T(8,128)S(1)}, f32[25,512]{1,0:T(8,128)}, u32[]{:S(2)}, u32[]{:S(2)}) collective-permute-start(f32[25,512]{1,0:T(8,128)S(1)} %get-tuple-element.23.refs_1_), channel_id=1, source_target_pairs={{0,1},{1,0},{2,3},{3,2},{4,5},{5,4},{6,7},{7,6},{8,9},{9,8},{10,11... | collective-permute-start | bytes 153608 | tf_op jit(solution)/shard_map/ppermute | solution.py:552
  52.6 8.0 %collective-permute-start.10 = (f32[25,512]{1,0:T(8,128)S(1)}, f32[25,512]{1,0:T(8,128)}, u32[]{:S(2)}, u32[]{:S(2)}) collective-permute-start(f32[25,512]{1,0:T(8,128)S(1)} %collective-permute-done.9.refs_7_), channel_id=1, source_target_pairs={{0,1},{1,0},{2,3},{3,2},{4,5},{5,4},{6,7},{7,6},{8,9},{9,8},{10,11... | collective-permute-start | bytes 153608 | tf_op jit(solution)/shard_map/ppermute | solution.py:552
  54.2 6.4 %collective-permute-start.6 = (f32[25,512]{1,0:T(8,128)}, f32[25,512]{1,0:T(8,128)}, u32[]{:S(2)}, u32[]{:S(2)}) collective-permute-start(f32[25,512]{1,0:T(8,128)} %collective-permute-done.5.refs_3_), channel_id=1, source_target_pairs={{0,1},{1,0},{2,3},{3,2},{4,5},{5,4},{6,7},{7,6},{8,9},{9,8},{10,11... | collective-permute-start | bytes 153608 | tf_op jit(solution)/shard_map/ppermute | solution.py:552
  65.9 33.0 %collective-permute-start.13 = (f32[3,64,512]{2,1,0:T(8,128)S(1)}, f32[3,64,512]{2,1,0:T(8,128)S(1)}, u32[]{:S(2)}, u32[]{:S(2)}) collective-permute-start(f32[3,64,512]{2,1,0:T(8,128)S(1)} %get-tuple-element.29.own1_ref), channel_id=1, source_target_pairs={{0,8},{8,16},{16,24},{24,32},{32,40},{40,48},{48,56},{56,64},{64,7... | collective-permute-start | bytes 1179656 | tf_op jit(solution)/shard_map/ppermute | solution.py:544
  65.9 33.0 %collective-permute-start.14 = (f32[3,64,512]{2,1,0:T(8,128)S(1)}, f32[3,64,512]{2,1,0:T(8,128)S(1)}, u32[]{:S(2)}, u32[]{:S(2)}) collective-permute-start(f32[3,64,512]{2,1,0:T(8,128)S(1)} %get-tuple-element.28.own0_ref), channel_id=1, source_target_pairs={{0,248},{8,0},{16,8},{24,16},{32,24},{40,32},{48,40},{56,48},{64,5... | collective-permute-start | bytes 1179656 | tf_op jit(solution)/shard_map/ppermute | solution.py:544
  75.5 23.4 %collective-permute-start.15 = (s32[64,512]{1,0:T(8,128)S(1)}, s32[64,512]{1,0:T(8,128)S(1)}, u32[]{:S(2)}, u32[]{:S(2)}) collective-permute-start(s32[64,512]{1,0:T(8,128)S(1)} %get-tuple-element.31.code1_ref.refs_4_), channel_id=1, source_target_pairs={{0,8},{8,16},{16,24},{24,32},{32,40},{40,48},{48,56},{56,64},{64,7... | collective-permute-start | bytes 393224 | tf_op jit(solution)/shard_map/ppermute | solution.py:544
  75.5 23.4 %collective-permute-start.16 = (s32[64,512]{1,0:T(8,128)S(1)}, s32[64,512]{1,0:T(8,128)S(1)}, u32[]{:S(2)}, u32[]{:S(2)}) collective-permute-start(s32[64,512]{1,0:T(8,128)S(1)} %get-tuple-element.30.code0_ref.refs_3_), channel_id=1, source_target_pairs={{0,248},{8,0},{16,8},{24,16},{32,24},{40,32},{48,40},{56,48},{64,5... | collective-permute-start | bytes 393224 | tf_op jit(solution)/shard_map/ppermute | solution.py:544
  85.1 22.6 %collective-permute-start.24 = (f32[136,384]{1,0:T(8,128)S(1)}, f32[136,384]{1,0:T(8,128)S(1)}, u32[]{:S(2)}, u32[]{:S(2)}) collective-permute-start(f32[136,384]{1,0:T(8,128)S(1)} %get-tuple-element.35), channel_id=1, source_target_pairs={{0,8},{8,16},{16,24},{24,32},{32,40},{40,48},{48,56},{56,64},{64,7... | collective-permute-start | bytes 626696 | tf_op jit(solution)/shard_map/ppermute | solution.py:544
  98.9 17.2 %collective-permute-start.25 = (f32[136,384]{1,0:T(8,128)S(1)}, f32[136,384]{1,0:T(8,128)S(1)}, u32[]{:S(2)}, u32[]{:S(2)}) collective-permute-start(f32[136,384]{1,0:T(8,128)S(1)} %get-tuple-element.36), channel_id=1, source_target_pairs={{0,248},{8,0},{16,8},{24,16},{32,24},{40,32},{48,40},{56,48},{64,5... | collective-permute-start | bytes 626696 | tf_op jit(solution)/shard_map/ppermute | solution.py:544
  103.6 8.3 %collective-permute-start.18 = (f32[25,512]{1,0:T(8,128)S(1)}, f32[25,512]{1,0:T(8,128)S(1)}, u32[]{:S(2)}, u32[]{:S(2)}) collective-permute-start(f32[25,512]{1,0:T(8,128)S(1)} %get-tuple-element.32.refs_1_), channel_id=1, source_target_pairs={{0,2},{1,3},{2,0},{3,1},{4,6},{5,7},{6,4},{7,5},{8,10},{9,11},{10,... | collective-permute-start | bytes 153608 | tf_op jit(solution)/shard_map/ppermute | solution.py:552
  103.7 9.1 %collective-permute-start.20 = (f32[25,512]{1,0:T(8,128)S(1)}, f32[25,512]{1,0:T(8,128)S(1)}, u32[]{:S(2)}, u32[]{:S(2)}) collective-permute-start(f32[25,512]{1,0:T(8,128)S(1)} %get-tuple-element.32.refs_1_), channel_id=1, source_target_pairs={{0,4},{1,5},{2,6},{3,7},{4,0},{5,1},{6,2},{7,3},{8,12},{9,13},{10,... | collective-permute-start | bytes 153608 | tf_op jit(solution)/shard_map/ppermute | solution.py:552
  105.2 10.9 %collective-permute-start.22 = (f32[25,512]{1,0:T(8,128)S(1)}, f32[25,512]{1,0:T(8,128)S(1)}, u32[]{:S(2)}, u32[]{:S(2)}) collective-permute-start(f32[25,512]{1,0:T(8,128)S(1)} %get-tuple-element.32.refs_1_), channel_id=1, source_target_pairs={{0,6},{1,7},{2,4},{3,5},{4,2},{5,3},{6,0},{7,1},{8,14},{9,15},{10,... | collective-permute-start | bytes 153608 | tf_op jit(solution)/shard_map/ppermute | solution.py:552
  107.8 11.0 %collective-permute-start.17 = (f32[25,512]{1,0:T(8,128)S(1)}, f32[25,512]{1,0:T(8,128)S(1)}, u32[]{:S(2)}, u32[]{:S(2)}) collective-permute-start(f32[25,512]{1,0:T(8,128)S(1)} %get-tuple-element.32.refs_1_), channel_id=1, source_target_pairs={{0,1},{1,0},{2,3},{3,2},{4,5},{5,4},{6,7},{7,6},{8,9},{9,8},{10,11... | collective-permute-start | bytes 153608 | tf_op jit(solution)/shard_map/ppermute | solution.py:552
  111.9 6.8 %collective-permute-start.19 = (f32[25,512]{1,0:T(8,128)S(1)}, f32[25,512]{1,0:T(8,128)S(1)}, u32[]{:S(2)}, u32[]{:S(2)}) collective-permute-start(f32[25,512]{1,0:T(8,128)S(1)} %collective-permute-done.18.refs_3_), channel_id=1, source_target_pairs={{0,1},{1,0},{2,3},{3,2},{4,5},{5,4},{6,7},{7,6},{8,9},{9,8},{10,11... | collective-permute-start | bytes 153608 | tf_op jit(solution)/shard_map/ppermute | solution.py:552
  112.7 6.1 %collective-permute-start.21 = (f32[25,512]{1,0:T(8,128)S(1)}, f32[25,512]{1,0:T(8,128)S(1)}, u32[]{:S(2)}, u32[]{:S(2)}) collective-permute-start(f32[25,512]{1,0:T(8,128)S(1)} %collective-permute-done.20.refs_5_), channel_id=1, source_target_pairs={{0,1},{1,0},{2,3},{3,2},{4,5},{5,4},{6,7},{7,6},{8,9},{9,8},{10,11... | collective-permute-start | bytes 153608 | tf_op jit(solution)/shard_map/ppermute | solution.py:552
  (15 other events, 128.2 us)

commit v3 on v2

--- a/solution.py
+++ b/solution.py
@@ -146,37 +146,57 @@
     return jnp.where(slot < count_ref[s, 0, 0, direction], ids, -8)
 
 
-def code_kernel(count_ref, blocks_ref, shift_ref, *out_refs):
+def moved_of(ids):
     row_id = lax.broadcasted_iota(jnp.int32, (ROWS, BL), 0)
     lane_block = lax.broadcasted_iota(jnp.int32, (N, BL), 0) // BL
-    for s in range(2):
-        for plane in range(2):
-            ids = live_ids(count_ref, blocks_ref, s, 1 - plane)
-            rows = jnp.where(jnp.broadcast_to(ids >> 2, (ROWS, BL)) == row_id, 1.0, 0.0)
-            lanes = jnp.where(jnp.broadcast_to(ids & 3, (N, BL)) == lane_block, 1.0, 0.0)
-            moved = lax.dot_general(
-                rows.astype(jnp.bfloat16),
-                lanes.astype(jnp.bfloat16),
-                (((1,), (1,)), ((), ())),
-                preferred_element_type=jnp.float32,
-            )
-            out_refs[2 * s + plane][...] = shift_ref[s, plane] + 8 * moved.astype(jnp.int32)
-
-
-def codes_of(count, blocks, shifts):
+    rows = jnp.where(jnp.broadcast_to(ids >> 2, (ROWS, BL)) == row_id, 1.0, 0.0)
+    lanes = jnp.where(jnp.broadcast_to(ids & 3, (N, BL)) == lane_block, 1.0, 0.0)
+    return lax.dot_general(
+        rows.astype(jnp.bfloat16),
+        lanes.astype(jnp.bfloat16),
+        (((1,), (1,)), ((), ())),
+        preferred_element_type=jnp.float32,
+    )
+
+
+def early_kernel(count_hbm, blocks_hbm, shift_hbm, lam_hbm, low_ref, high_ref, count_ref, blocks_ref, shift_ref, sem):
+    copies = [
+        pltpu.make_async_copy(count_hbm, count_ref, sem.at[0]),
+        pltpu.make_async_copy(blocks_hbm.at[0], blocks_ref, sem.at[1]),
+        pltpu.make_async_copy(shift_hbm.at[0], shift_ref, sem.at[2]),
+        pltpu.make_async_copy(lam_hbm.at[:, 0], low_ref.at[pl.ds(0, 3)], sem.at[3]),
+        pltpu.make_async_copy(lam_hbm.at[:, 1], high_ref.at[pl.ds(0, 3)], sem.at[4]),
+    ]
+    for copy in copies:
+        copy.start()
+    for copy in copies[:3]:
+        copy.wait()
+    slot = lax.broadcasted_iota(jnp.int32, (1, BL), 1)
+    for plane, out_ref in ((0, low_ref), (1, high_ref)):
+        direction = 1 - plane
+        ids = blocks_ref[0, 0, direction : direction + 1, :]
+        ids = jnp.where(slot < count_ref[0, 0, 0, direction], ids, -8)
+        out_ref[3] = shift_ref[plane].astype(jnp.float32) + 8.0 * moved_of(ids)
+    for copy in copies[3:]:
+        copy.wait()
+
+
+def early_of(count, blocks, shifts, lam):
     return pl.pallas_call(
-        code_kernel,
-        out_shape=(jax.ShapeDtypeStruct((ROWS, N), jnp.int32),) * 4,
-        in_specs=[
-            pl.BlockSpec(memory_space=pltpu.SMEM),
-            pl.BlockSpec(memory_space=pltpu.VMEM),
-            pl.BlockSpec(memory_space=pltpu.VMEM),
+        early_kernel,
+        out_shape=(jax.ShapeDtypeStruct((4, ROWS, N), jnp.float32),) * 2,
+        in_specs=[pl.BlockSpec(memory_space=pltpu.HBM)] * 4,
+        out_specs=(pl.BlockSpec(memory_space=pltpu.VMEM),) * 2,
+        scratch_shapes=[
+            pltpu.SMEM(count.shape, jnp.int32),
+            pltpu.VMEM(blocks.shape[1:], jnp.int32),
+            pltpu.VMEM((2, ROWS, N), jnp.int32),
+            pltpu.SemaphoreType.DMA((5,)),
         ],
-        out_specs=(pl.BlockSpec(memory_space=pltpu.VMEM),) * 4,
         compiler_params=pltpu.CompilerParams(vmem_limit_bytes=VMEM_LIMIT),
         cost_estimate=pl.CostEstimate(flops=40_000_000, bytes_accessed=1_000_000, transcendentals=0),
-        name="codes",
-    )(count, blocks, shifts)
+        name="early",
+    )(count, blocks, shifts, lam)
 
 
 def parts_of(x):
@@ -193,11 +213,12 @@
     return jnp.where(hit, 1.0, 0.0).astype(jnp.bfloat16)
 
 
-def pack_kernel(count_ref, blocks_ref, omega_ref, *out_refs):
-    for s in range(2):
-        for plane in range(2):
+def pack_kernel(count_ref, blocks_ref, shift_ref, omega_ref, *out_refs):
+    for plane, out_ref in enumerate(out_refs):
+        out_ref[2 * BL :, :] = jnp.zeros((8, N), jnp.float32)
+        for s in range(2):
             ids = live_ids(count_ref, blocks_ref, s, 1 - plane)
-            out_ref = out_refs[2 * s + plane]
+            out_ref[2 * BL + s : 2 * BL + s + 1, 0:BL] = ids.astype(jnp.float32)
             total = jnp.zeros((BL, 3 * BL), jnp.float32)
             for q in range(4):
                 chosen = chosen_rows(ids, q)
@@ -207,32 +228,42 @@
                     total = total + lax.dot_general(
                         chosen, part, (((0,), (0,)), ((), ())), preferred_element_type=jnp.float32
                     )
-            out_ref[0:BL, :] = total
-            out_ref[BL : BL + 8, :] = jnp.zeros((8, 3 * BL), jnp.float32)
-            out_ref[BL : BL + 1, 0:BL] = ids.astype(jnp.float32)
-
-
-def packed_of(count, blocks, omega):
+            out_ref[s * BL : (s + 1) * BL, 0 : 3 * BL] = total
+        code = shift_ref[1, plane].astype(jnp.float32) + 8.0 * moved_of(ids)
+        for q in range(4):
+            out_ref[q * ROWS : (q + 1) * ROWS, 3 * BL :] = code[:, q * BL : (q + 1) * BL]
+
+
+def packed_of(count, blocks, shifts, omega):
     return pl.pallas_call(
         pack_kernel,
-        out_shape=(jax.ShapeDtypeStruct((BL + 8, 3 * BL), jnp.float32),) * 4,
+        out_shape=(jax.ShapeDtypeStruct((2 * BL + 8, N), jnp.float32),) * 2,
         in_specs=[
             pl.BlockSpec(memory_space=pltpu.SMEM),
             pl.BlockSpec(memory_space=pltpu.VMEM),
             pl.BlockSpec(memory_space=pltpu.VMEM),
+            pl.BlockSpec(memory_space=pltpu.VMEM),
         ],
-        out_specs=(pl.BlockSpec(memory_space=pltpu.VMEM),) * 4,
+        out_specs=(pl.BlockSpec(memory_space=pltpu.VMEM),) * 2,
         compiler_params=pltpu.CompilerParams(vmem_limit_bytes=VMEM_LIMIT),
         cost_estimate=pl.CostEstimate(flops=300_000_000, bytes_accessed=3_000_000, transcendentals=0),
         name="pack",
-    )(count, blocks, omega)
+    )(count, blocks, shifts, omega)
+
+
+def code_rows(s, early_ref, packed_ref, start):
+    if s == 0:
+        return early_ref[3, pl.ds(start, 8), :]
+    return jnp.concatenate(
+        [packed_ref[pl.ds(q * ROWS + start, 8), 3 * BL :] for q in range(4)], axis=1
+    )
 
 
 def deposit(own, own_code, other, other_code):
     total = None
     for amount in (0, 1, 2, -1, -2):
-        picked = jnp.where(own_code == amount, own, 0.0) + jnp.where(
-            other_code == amount + 8, other, 0.0
+        picked = jnp.where(own_code == float(amount), own, 0.0) + jnp.where(
+            other_code == float(amount + 8), other, 0.0
         )
         if amount:
             picked = pltpu.roll(picked, amount % N, 1)
@@ -240,15 +271,15 @@
     return total
 
 
-def omega_kernel(
-    s, own_ref, below_ref, above_ref, code0_ref, code1_ref, cbelow_ref, cabove_ref, out_ref, far_ref
-):
-    for plane, other_ref, code_ref, cother_ref in (
-        (0, below_ref, code0_ref, cbelow_ref),
-        (1, above_ref, code1_ref, cabove_ref),
-    ):
-        ids = other_ref[BL : BL + 1, 0:BL].astype(jnp.int32)
-        parts = parts_of(other_ref[0:BL, :])
+def omega_kernel(s, *refs):
+    own_ref = refs[0]
+    packed = refs[1:5]
+    early = refs[5:9] if s == 0 else (None,) * 4
+    out_ref, far_ref = refs[-2:]
+    for plane in range(2):
+        other_ref = packed[2 + plane]
+        ids = other_ref[2 * BL + s : 2 * BL + s + 1, 0:BL].astype(jnp.int32)
+        parts = parts_of(other_ref[s * BL : (s + 1) * BL, 0 : 3 * BL])
         for q in range(4):
             chosen = chosen_rows(ids, q)
             total = None
@@ -259,10 +290,11 @@
                 far_ref[c, :, q * BL : (q + 1) * BL] = total[:, c * BL : (c + 1) * BL]
 
         @pl.loop(0, ROWS // 8)
-        def _(step, plane=plane, code_ref=code_ref, cother_ref=cother_ref):
-            rows = pl.ds(pl.multiple_of(step * 8, 8), 8)
-            own_code = code_ref[rows, :]
-            other_code = cother_ref[rows, :]
+        def _(step, plane=plane):
+            start = pl.multiple_of(step * 8, 8)
+            rows = pl.ds(start, 8)
+            own_code = code_rows(s, early[plane], packed[plane], start)
+            other_code = code_rows(s, early[2 + plane], packed[2 + plane], start)
             for c in range(3):
                 out_ref[c, plane, rows, :] = deposit(
                     own_ref[s, c, plane, rows, :], own_code, far_ref[c, rows, :], other_code
@@ -276,7 +308,7 @@
     return pl.pallas_call(
         body,
         out_shape=jax.ShapeDtypeStruct((3, 2, ROWS, N), jnp.float32),
-        in_specs=[pl.BlockSpec(memory_space=pltpu.VMEM)] * 7,
+        in_specs=[pl.BlockSpec(memory_space=pltpu.VMEM)] * len(args),
         out_specs=pl.BlockSpec(memory_space=pltpu.VMEM),
         scratch_shapes=[pltpu.VMEM((3, ROWS, N), jnp.float32)],
         compiler_params=pltpu.CompilerParams(vmem_limit_bytes=VMEM_LIMIT),
@@ -288,24 +320,19 @@
 SUBLANE = (0, 4, 12)
 
 
-def first_kernel(
-    own0_ref, own1_ref, below_ref, above_ref, code0_ref, code1_ref, cbelow_ref, cabove_ref,
-    forward_ref, table_ref, lam_ref, u_ref, ends_ref, x_ref, h_ref,
-):
-    for plane, other, own_ref, other_ref, code_ref, cother_ref in (
-        (0, 0, own0_ref, below_ref, code0_ref, cbelow_ref),
-        (1, 3, own1_ref, above_ref, code1_ref, cabove_ref),
-    ):
+def first_kernel(s, *refs):
+    own_refs, far_refs = refs[0:2], refs[2:4]
+    packed = refs[4:8] if s else (None,) * 4
+    forward_ref, table_ref, lam_ref, u_ref, ends_ref, x_ref, h_ref = refs[-7:]
+    for plane, other in ((0, 0), (1, 3)):
+        own_ref, other_ref = own_refs[plane], far_refs[plane]
 
         @pl.loop(0, ROWS // 8)
-        def _(
-            step, plane=plane, other=other, own_ref=own_ref, other_ref=other_ref,
-            code_ref=code_ref, cother_ref=cother_ref,
-        ):
+        def _(step, plane=plane, other=other, own_ref=own_ref, other_ref=other_ref):
             start = pl.multiple_of(step * 8, 8)
             rows = pl.ds(start, 8)
-            own_code = code_ref[rows, :]
-            other_code = cother_ref[rows, :]
+            own_code = code_rows(s, own_ref, packed[plane], start)
+            other_code = code_rows(s, other_ref, packed[2 + plane], start)
             for c in range(3):
                 own = own_ref[c, rows, :]
                 far = other_ref[c, rows, :]
@@ -364,15 +391,18 @@
     ends_ref[24:25, 0:BL] = jnp.sum(jnp.where(used, sums, 0.0), axis=0, keepdims=True)
 
 
-def first_of(*args):
+def first_of(s, *args):
+    def body(*refs):
+        first_kernel(s, *refs)
+
     return pl.pallas_call(
-        first_kernel,
+        body,
         out_shape=(
             jax.ShapeDtypeStruct((3, 2, ROWS, N), jnp.float32),
             jax.ShapeDtypeStruct((4, ROWS * 16, BL), jnp.float32),
             jax.ShapeDtypeStruct((25, N), jnp.float32),
         ),
-        in_specs=[pl.BlockSpec(memory_space=pltpu.VMEM)] * 10,
+        in_specs=[pl.BlockSpec(memory_space=pltpu.VMEM)] * len(args),
         out_specs=(pl.BlockSpec(memory_space=pltpu.VMEM),) * 3,
         scratch_shapes=[
             pltpu.VMEM((12 * ROWS, N), jnp.float32),
@@ -385,13 +415,13 @@
 
 
 def second_kernel(
-    zero_u, zero_z, last, me_ref, *refs
+    zero_u, zero_z, last, *refs
 ):
     ends_refs = refs[:GROUPS]
     u_ref, lam_ref, omega_ref, table_ref, inverse_ref = refs[GROUPS : GROUPS + 5]
     out_refs = refs[GROUPS + 5 : -2]
     y_ref, field_ref = refs[-2:]
-    me = me_ref[0]
+    me = lax.axis_index("pencil")
     u_in = [[jnp.zeros((8, BL), jnp.float32)] * 2 for _ in range(4)]
     w_in = [[jnp.zeros((8, BL), jnp.float32)] * 2 for _ in range(4)]
     u_sum = [jnp.zeros((8, BL), jnp.float32)] * 2
@@ -526,8 +556,7 @@
     return pl.pallas_call(
         body,
         out_shape=shapes,
-        in_specs=[pl.BlockSpec(memory_space=pltpu.SMEM)]
-        + [pl.BlockSpec(memory_space=pltpu.VMEM)] * (GROUPS + 5),
+        in_specs=[pl.BlockSpec(memory_space=pltpu.VMEM)] * (GROUPS + 5),
         out_specs=(pl.BlockSpec(memory_space=pltpu.VMEM),) * len(shapes),
         scratch_shapes=[
             pltpu.VMEM((ROWS * 16, N), jnp.float32),
@@ -565,23 +594,23 @@
     forward, inverse = halves(t["forward"]), halves(t["inverse"])
     rows = [t["rpow"], t["cuu"], t["cww"], t["cwu"], t["r"][None], t["swap"][None]]
     table = jnp.asarray(np.concatenate(rows)[:, None], jnp.float32)
-    me = lax.axis_index("pencil").astype(jnp.int32)[None]
-
-    lam0, lam1 = adjoint_vort[:, 0], adjoint_vort[:, 1]
-    below, above = neighbours(lam0, lam1)
-    code = codes_of(move_count, move_blocks, cell_shift)
-    far_code = [neighbours(code[2 * s], code[2 * s + 1]) for s in range(2)]
-    packed = packed_of(move_count, move_blocks, omega_ckpt)
-    far_omega = [neighbours(packed[2 * s], packed[2 * s + 1]) for s in range(2)]
+
+    lows = early_of(move_count, move_blocks, cell_shift, adjoint_vort)
+    far = neighbours(*lows)
+    packed = packed_of(move_count, move_blocks, cell_shift, omega_ckpt)
+    far_packed = neighbours(*packed)
     for s in range(2):
+        extra = () if s == 0 else (*packed, *far_packed)
         if s:
-            below, above = neighbours(lam0, lam1)
-        codes = (code[2 * s], code[2 * s + 1], *far_code[s])
-        omega = omega_of(s, omega_ckpt, *far_omega[s], *codes)
-        lam_r, u, ends = first_of(lam0, lam1, below, above, *codes, forward, table)
-        out = second_of(t, s == 1, me, *gathered(ends), u, lam_r, omega, table, inverse)
+            far = neighbours(*lows)
+            omega = omega_of(s, omega_ckpt, *packed, *far_packed)
+            far, omega = lax.optimization_barrier((far, omega))
+        else:
+            omega = omega_of(s, omega_ckpt, *packed, *far_packed, *lows, *far)
+        lam_r, u, ends = first_of(s, *lows, *far, *extra, forward, table)
+        out = second_of(t, s == 1, *gathered(ends), u, lam_r, omega, table, inverse)
         if s == 0:
-            lam0, lam1 = out
+            lows = out
     return out[0]
 
 

time: 123 us -> 127 us (1.033); the launches traced: 123 us -> 125 us
  waiting for transfers between devices: 19.8 us -> 22.8 us
  starting transfers between devices: 70.1 us -> 73 us
  local copies, waits for them, and re-layouts: 7.07 us -> 4.96 us
    ppermute x14, starting transfers between devices: 21.1 us -> 49 us  [crossed(): return lax.ppermute(value, 'pencil', [(i, i ^ mask) for i in range(GROUPS)])]
    ppermute x12 -> x6, starting transfers between devices: 49 us -> 23.9 us  [shifted(): lax.ppermute(value, axis, [(i, (i + by) % count) for i in range(count)])]
    ppermute x14, waiting for transfers between devices: 3.38 us -> 7.45 us  [crossed(): return lax.ppermute(value, 'pencil', [(i, i ^ mask) for i in range(GROUPS)])]
    squeeze x1 -> x0, local copies, waits for them, and re-layouts: 1.29 us -> none  [shards(): lam0, lam1 = (adjoint_vort[:, 0], adjoint_vort[:, 1])]
    ppermute x12 -> x6, waiting for transfers between devices: 16.5 us -> 15.4 us  [shifted(): lax.ppermute(value, axis, [(i, (i + by) % count) for i in range(count)])]
    unnamed x26 -> x18, local copies, waits for them, and re-layouts: 5.79 us -> 4.96 us
  transfers between devices with their start and end apart: 26 -> 20, of which waited for: 5 -> 6; matrix products, arithmetic and copies ran while one was open for 0% -> 0% of each run, Pallas kernels for 14% -> 10%
where the time goes in v3:
time: 127 us; the launch traced here: 125 us
  starting transfers between devices  73 us (57%)
  Pallas kernels  24.5 us (19%)
  waiting for transfers between devices  22.8 us (18%)
  local copies, waits for them, and re-layouts  4.96 us (4%)
    ppermute x14, starting transfers between devices, crossed(): return lax.ppermute(value, 'pencil', [(i, i ^ mask) for i in range(GROUPS)])  49 us
    ppermute x6, starting transfers between devices, shifted(): lax.ppermute(value, axis, [(i, (i + by) % count) for i in range(count)])  23.9 us
    ppermute x6, waiting for transfers between devices, shifted(): lax.ppermute(value, axis, [(i, (i + by) % count) for i in range(count)])  15.4 us
    pallas_call x2, Pallas kernels, first_of(): pl.pallas_call(body, out_shape=(jax.ShapeDtypeStruct((3, 2, ROWS, N), jnp...  9.48 us
    ppermute x14, waiting for transfers between devices, crossed(): return lax.ppermute(value, 'pencil', [(i, i ^ mask) for i in range(GROUPS)])  7.45 us
    pallas_call x2, Pallas kernels, second_of(): pl.pallas_call(body, out_shape=shapes, in_specs=[pl.BlockSpec(memory_spac...  6.78 us
    pallas_call x2, Pallas kernels, omega_of(): pl.pallas_call(body, out_shape=jax.ShapeDtypeStruct((3, 2, ROWS, N), jnp....  5.34 us
    unnamed x18, local copies, waits for them, and re-layouts  4.96 us
  transfers between devices with their start and end apart: 20, of which 6 were waited for; matrix products, arithmetic and copies ran while one was open for 0% of the time, Pallas kernels for 10%

profile of v3, /device:TPU:1, one launch (start us, length us, event | category | flops | bytes accessed | tf_op | source)
XLA Modules:
  0.0 125.3 jit_solution(17514239523144881104)
XLA Ops:
  4.4 2.2 %collective-permute-start = (f32[4,64,512]{2,1,0:T(8,128)S(1)}, f32[4,64,512]{2,1,0:T(8,128)S(1)}, u32[]{:S(2)}, u32[]{:S(2)}) collective-permute-start(f32[4,64,512]{2,1,0:T(8,128)S(1)} %get-tuple-element.21.refs_1_.refs_6_), channel_id=1, source_target_pairs={{0,8},{8,16},{16,24},{24,32},{32,40},{40,48},{48,56},{56,64},{64,7... | collective-permute-start | bytes 1572872 | tf_op jit(solution)/shard_map/ppermute | solution.py:573
  6.6 10.3 %collective-permute-start.1 = (f32[4,64,512]{2,1,0:T(8,128)S(1)}, f32[4,64,512]{2,1,0:T(8,128)S(1)}, u32[]{:S(2)}, u32[]{:S(2)}) collective-permute-start(f32[4,64,512]{2,1,0:T(8,128)S(1)} %get-tuple-element.20.refs_0_.refs_5_), channel_id=1, source_target_pairs={{0,248},{8,0},{16,8},{24,16},{32,24},{40,32},{48,40},{56,48},{64,5... | collective-permute-start | bytes 1572872 | tf_op jit(solution)/shard_map/ppermute | solution.py:573
  16.9 1.4 %copy-done = f32[2,3,2,64,512]{4,3,2,1,0:T(8,128)S(1)} copy-done((f32[2,3,2,64,512]{4,3,2,1,0:T(8,128)S(1)}, f32[2,3,2,64,512]{4,3,2,1,0:T(8,128)}, u32[]{:S(2)}) %copy-start) | copy-done | bytes 1572888
  18.3 2.0 %pack.1 = (f32[264,512]{1,0:T(8,128)S(1)}, f32[264,512]{1,0:T(8,128)S(1)}) custom-call(s32[2,1,1,2]{3,2,1,0:T(1,128)S(1)} %copy-done.5, s32[2,1,1,2,128]{4,3,2,1,0:T(2,128)S(1)} %copy-done.4, s32[2,2,64,512]{3,2,1,0:T(8,128)S(1)} %copy-done.2, f32[2,3,2,64,512]{4,3,2,1,0:T(8,128)S(1)} %copy-done), custom_call_target="tpu_custom_call" | custom-call | flops 300000000 | bytes 3000000 | tf_op jit(solution)/shard_map/pack/pallas_call | solution.py:238
  20.4 1.5 %collective-permute-start.10 = (f32[264,512]{1,0:T(8,128)S(1)}, f32[264,512]{1,0:T(8,128)S(1)}, u32[]{:S(2)}, u32[]{:S(2)}) collective-permute-start(f32[264,512]{1,0:T(8,128)S(1)} %get-tuple-element.25.refs_1_.refs_4_), channel_id=1, source_target_pairs={{0,248},{8,0},{16,8},{24,16},{32,24},{40,32},{48,40},{56,48},{64,5... | collective-permute-start | bytes 1622024 | tf_op jit(solution)/shard_map/ppermute | solution.py:573
  21.9 9.2 %collective-permute-done.refs_2_.refs_7_ = f32[4,64,512]{2,1,0:T(8,128)S(1)} collective-permute-done((f32[4,64,512]{2,1,0:T(8,128)S(1)}, f32[4,64,512]{2,1,0:T(8,128)S(1)}, u32[]{:S(2)}, u32[]{:S(2)}) %collective-permute-start) | collective-permute-done | bytes 524320 | tf_op jit(solution)/shard_map/ppermute | solution.py:573
  31.1 4.7 %first.2 = (f32[3,2,64,512]{3,2,1,0:T(8,128)S(1)}, f32[4,1024,128]{2,1,0:T(8,128)S(1)}, f32[25,512]{1,0:T(8,128)S(1)}) custom-call(f32[4,64,512]{2,1,0:T(8,128)S(1)} %get-tuple-element.20.refs_0_.refs_5_, f32[4,64,512]{2,1,0:T(8,128)S(1)} %get-tuple-element.21.refs_1_.refs_6_, f32[4,64,512]{2,1,0:T(8,128)S(1)} %collective-permute-done.refs_2_.refs_7_, ...), custom_call_target="tpu_custom_call" | custom-call | flops 3000000000 | bytes 8000000 | tf_op jit(solution)/shard_map/first/pallas_call | solution.py:398
  35.8 13.7 %collective-permute-start.3 = (f32[25,512]{1,0:T(8,128)S(1)}, f32[25,512]{1,0:T(8,128)S(1)}, u32[]{:S(2)}, u32[]{:S(2)}) collective-permute-start(f32[25,512]{1,0:T(8,128)S(1)} %get-tuple-element.22.refs_0_), channel_id=1, source_target_pairs={{0,2},{1,3},{2,0},{3,1},{4,6},{5,7},{6,4},{7,5},{8,10},{9,11},{10,... | collective-permute-start | bytes 153608 | tf_op jit(solution)/shard_map/ppermute | solution.py:581
  49.5 6.4 %collective-permute-start.5 = (f32[25,512]{1,0:T(8,128)S(1)}, f32[25,512]{1,0:T(8,128)S(1)}, u32[]{:S(2)}, u32[]{:S(2)}) collective-permute-start(f32[25,512]{1,0:T(8,128)S(1)} %get-tuple-element.22.refs_0_), channel_id=1, source_target_pairs={{0,4},{1,5},{2,6},{3,7},{4,0},{5,1},{6,2},{7,3},{8,12},{9,13},{10,... | collective-permute-start | bytes 153608 | tf_op jit(solution)/shard_map/ppermute | solution.py:581
  57.0 4.4 %collective-permute-start.2 = (f32[25,512]{1,0:T(8,128)S(1)}, f32[25,512]{1,0:T(8,128)S(1)}, u32[]{:S(2)}, u32[]{:S(2)}) collective-permute-start(f32[25,512]{1,0:T(8,128)S(1)} %get-tuple-element.22.refs_0_), channel_id=1, source_target_pairs={{0,1},{1,0},{2,3},{3,2},{4,5},{5,4},{6,7},{7,6},{8,9},{9,8},{10,11... | collective-permute-start | bytes 153608 | tf_op jit(solution)/shard_map/ppermute | solution.py:581
  61.4 5.2 %collective-permute-done.3.refs_2_ = f32[25,512]{1,0:T(8,128)S(1)} collective-permute-done((f32[25,512]{1,0:T(8,128)S(1)}, f32[25,512]{1,0:T(8,128)S(1)}, u32[]{:S(2)}, u32[]{:S(2)}) %collective-permute-start.3) | collective-permute-done | bytes 51232 | tf_op jit(solution)/shard_map/ppermute | solution.py:581
  66.6 1.9 %collective-permute-start.4 = (f32[25,512]{1,0:T(8,128)S(1)}, f32[25,512]{1,0:T(8,128)S(1)}, u32[]{:S(2)}, u32[]{:S(2)}) collective-permute-start(f32[25,512]{1,0:T(8,128)S(1)} %collective-permute-done.3.refs_2_), channel_id=1, source_target_pairs={{0,1},{1,0},{2,3},{3,2},{4,5},{5,4},{6,7},{7,6},{8,9},{9,8},{10,11... | collective-permute-start | bytes 153608 | tf_op jit(solution)/shard_map/ppermute | solution.py:581
  68.5 3.1 %collective-permute-start.6 = (f32[25,512]{1,0:T(8,128)S(1)}, f32[25,512]{1,0:T(8,128)S(1)}, u32[]{:S(2)}, u32[]{:S(2)}) collective-permute-start(f32[25,512]{1,0:T(8,128)S(1)} %collective-permute-done.5.refs_4_), channel_id=1, source_target_pairs={{0,1},{1,0},{2,3},{3,2},{4,5},{5,4},{6,7},{7,6},{8,9},{9,8},{10,11... | collective-permute-start | bytes 153608 | tf_op jit(solution)/shard_map/ppermute | solution.py:581
  71.6 2.7 %omega.2.refs_10_ = f32[3,2,64,512]{3,2,1,0:T(8,128)S(1)} custom-call(f32[2,3,2,64,512]{4,3,2,1,0:T(8,128)S(1)} %copy-done.1, f32[264,512]{1,0:T(8,128)S(1)} %get-tuple-element.25.refs_1_.refs_4_, f32[264,512]{1,0:T(8,128)S(1)} %get-tuple-element.26.refs_2_.refs_5_, f32[264,512]{1,0:T(8,128)S(1)} %collective-permute-done.9.refs_3_.refs_6_, ...), custom_call_target="tpu_custom_call" | custom-call | flops 300000000 | bytes 6000000 | tf_op jit(solution)/shard_map/omega/pallas_call | solution.py:308
  74.3 3.0 %second.2 = (f32[3,64,512]{2,1,0:T(8,128)S(1)}, f32[3,64,512]{2,1,0:T(8,128)S(1)}) custom-call(f32[25,512]{1,0:T(8,128)S(1)} %get-tuple-element.22.refs_0_, f32[25,512]{1,0:T(8,128)S(1)} %collective-permute-done.2.refs_1_, f32[25,512]{1,0:T(8,128)S(1)} %collective-permute-done.3.refs_2_, f32[25,512]{1,0:T(8,128)S(1)} %collective-permute-done.4.refs_3_, ...), custom_call_target="tpu_custom_call" | custom-call | flops 4000000000 | bytes 8000000 | tf_op jit(solution)/shard_map/second/pallas_call | solution.py:556
  77.5 9.6 %collective-permute-start.12 = (f32[3,64,512]{2,1,0:T(8,128)S(1)}, f32[3,64,512]{2,1,0:T(8,128)S(1)}, u32[]{:S(2)}, u32[]{:S(2)}) collective-permute-start(f32[3,64,512]{2,1,0:T(8,128)S(1)} %get-tuple-element.27.refs_0_), channel_id=1, source_target_pairs={{0,248},{8,0},{16,8},{24,16},{32,24},{40,32},{48,40},{56,48},{64,5... | collective-permute-start | bytes 1179656 | tf_op jit(solution)/shard_map/ppermute | solution.py:573
  87.1 2.7 %omega.3.refs_10_ = f32[3,2,64,512]{3,2,1,0:T(8,128)S(1)} custom-call(f32[2,3,2,64,512]{4,3,2,1,0:T(8,128)S(1)} %copy-done.1, f32[264,512]{1,0:T(8,128)S(1)} %get-tuple-element.25.refs_1_.refs_4_, f32[264,512]{1,0:T(8,128)S(1)} %get-tuple-element.26.refs_2_.refs_5_, f32[264,512]{1,0:T(8,128)S(1)} %collective-permute-done.9.refs_3_.refs_6_, ...), custom_call_target="tpu_custom_call" | custom-call | flops 300000000 | bytes 6000000 | tf_op jit(solution)/shard_map/omega/pallas_call | solution.py:308
  89.8 6.2 %collective-permute-done.11.refs_2_ = f32[3,64,512]{2,1,0:T(8,128)S(1)} collective-permute-done((f32[3,64,512]{2,1,0:T(8,128)S(1)}, f32[3,64,512]{2,1,0:T(8,128)S(1)}, u32[]{:S(2)}, u32[]{:S(2)}) %collective-permute-start.11) | collective-permute-done | bytes 393248 | tf_op jit(solution)/shard_map/ppermute | solution.py:573
  96.0 4.8 %first.3 = (f32[3,2,64,512]{3,2,1,0:T(8,128)S(1)}, f32[4,1024,128]{2,1,0:T(8,128)S(1)}, f32[25,512]{1,0:T(8,128)S(1)}) custom-call(f32[3,64,512]{2,1,0:T(8,128)S(1)} %get-tuple-element.27.refs_0_, f32[3,64,512]{2,1,0:T(8,128)S(1)} %get-tuple-element.28.refs_1_, f32[3,64,512]{2,1,0:T(8,128)S(1)} %collective-permute-done.11.refs_2_, ...), custom_call_target="tpu_custom_call" | custom-call | flops 3000000000 | bytes 8000000 | tf_op jit(solution)/shard_map/first/pallas_call | solution.py:398
  100.8 10.5 %collective-permute-start.14 = (f32[25,512]{1,0:T(8,128)S(1)}, f32[25,512]{1,0:T(8,128)S(1)}, u32[]{:S(2)}, u32[]{:S(2)}) collective-permute-start(f32[25,512]{1,0:T(8,128)S(1)} %get-tuple-element.31.refs_0_), channel_id=1, source_target_pairs={{0,2},{1,3},{2,0},{3,1},{4,6},{5,7},{6,4},{7,5},{8,10},{9,11},{10,... | collective-permute-start | bytes 153608 | tf_op jit(solution)/shard_map/ppermute | solution.py:581
  112.2 1.3 %collective-permute-start.18 = (f32[25,512]{1,0:T(8,128)S(1)}, f32[25,512]{1,0:T(8,128)S(1)}, u32[]{:S(2)}, u32[]{:S(2)}) collective-permute-start(f32[25,512]{1,0:T(8,128)S(1)} %get-tuple-element.31.refs_0_), channel_id=1, source_target_pairs={{0,6},{1,7},{2,4},{3,5},{4,2},{5,3},{6,0},{7,1},{8,14},{9,15},{10,... | collective-permute-start | bytes 153608 | tf_op jit(solution)/shard_map/ppermute | solution.py:581
  113.5 1.4 %collective-permute-start.13 = (f32[25,512]{1,0:T(8,128)S(1)}, f32[25,512]{1,0:T(8,128)S(1)}, u32[]{:S(2)}, u32[]{:S(2)}) collective-permute-start(f32[25,512]{1,0:T(8,128)S(1)} %get-tuple-element.31.refs_0_), channel_id=1, source_target_pairs={{0,1},{1,0},{2,3},{3,2},{4,5},{5,4},{6,7},{7,6},{8,9},{9,8},{10,11... | collective-permute-start | bytes 153608 | tf_op jit(solution)/shard_map/ppermute | solution.py:581
  115.9 4.3 %collective-permute-start.17 = (f32[25,512]{1,0:T(8,128)S(1)}, f32[25,512]{1,0:T(8,128)S(1)}, u32[]{:S(2)}, u32[]{:S(2)}) collective-permute-start(f32[25,512]{1,0:T(8,128)S(1)} %collective-permute-done.16.refs_4_), channel_id=1, source_target_pairs={{0,1},{1,0},{2,3},{3,2},{4,5},{5,4},{6,7},{7,6},{8,9},{9,8},{10,11... | collective-permute-start | bytes 153608 | tf_op jit(solution)/shard_map/ppermute | solution.py:581
  121.5 3.8 %second.3 = f32[3,2,64,512]{3,2,1,0:T(8,128)} custom-call(f32[25,512]{1,0:T(8,128)S(1)} %get-tuple-element.31.refs_0_, f32[25,512]{1,0:T(8,128)S(1)} %collective-permute-done.13.refs_1_, f32[25,512]{1,0:T(8,128)S(1)} %collective-permute-done.14.refs_2_, f32[25,512]{1,0:T(8,128)S(1)} %collective-permute-done.15.refs_3_, ...), custom_call_target="tpu_custom_call" | custom-call | flops 4000000000 | bytes 8000000 | tf_op jit(solution)/shard_map/second/pallas_call | solution.py:556
  (42 shorter events, 9.0 us)
Async XLA Ops:
  3.5 27.5 %copy-start.7 = (bf16[2,2,256,256]{3,2,1,0:T(8,128)(2,1)S(1)}, bf16[2,2,256,256]{3,2,1,0:T(8,128)(2,1)}, u32[]{:S(2)}) copy-start(bf16[2,2,256,256]{3,2,1,0:T(8,128)(2,1)} %constant.6.clone.refs_4_.refs_8_) | copy-start | bytes 1572868
  3.5 27.5 %copy-start.8 = (f32[90,1,512]{2,1,0:T(1,128)S(1)}, f32[90,1,512]{2,1,0:T(1,128)}, u32[]{:S(2)}) copy-start(f32[90,1,512]{2,1,0:T(1,128)} %constant.8.clone.refs_5_.refs_11_.refs_9_) | copy-start | bytes 552964
  4.4 26.7 %collective-permute-start = (f32[4,64,512]{2,1,0:T(8,128)S(1)}, f32[4,64,512]{2,1,0:T(8,128)S(1)}, u32[]{:S(2)}, u32[]{:S(2)}) collective-permute-start(f32[4,64,512]{2,1,0:T(8,128)S(1)} %get-tuple-element.21.refs_1_.refs_6_), channel_id=1, source_target_pairs={{0,8},{8,16},{16,24},{24,32},{32,40},{40,48},{48,56},{56,64},{64,7... | collective-permute-start | bytes 1572872 | tf_op jit(solution)/shard_map/ppermute | solution.py:573
  6.6 24.5 %collective-permute-start.1 = (f32[4,64,512]{2,1,0:T(8,128)S(1)}, f32[4,64,512]{2,1,0:T(8,128)S(1)}, u32[]{:S(2)}, u32[]{:S(2)}) collective-permute-start(f32[4,64,512]{2,1,0:T(8,128)S(1)} %get-tuple-element.20.refs_0_.refs_5_), channel_id=1, source_target_pairs={{0,248},{8,0},{16,8},{24,16},{32,24},{40,32},{48,40},{56,48},{64,5... | collective-permute-start | bytes 1572872 | tf_op jit(solution)/shard_map/ppermute | solution.py:573
  20.4 36.6 %collective-permute-start.10 = (f32[264,512]{1,0:T(8,128)S(1)}, f32[264,512]{1,0:T(8,128)S(1)}, u32[]{:S(2)}, u32[]{:S(2)}) collective-permute-start(f32[264,512]{1,0:T(8,128)S(1)} %get-tuple-element.25.refs_1_.refs_4_), channel_id=1, source_target_pairs={{0,248},{8,0},{16,8},{24,16},{32,24},{40,32},{48,40},{56,48},{64,5... | collective-permute-start | bytes 1622024 | tf_op jit(solution)/shard_map/ppermute | solution.py:573
  21.8 49.8 %copy-start.1 = (f32[2,3,2,64,512]{4,3,2,1,0:T(8,128)S(1)}, f32[2,3,2,64,512]{4,3,2,1,0:T(8,128)}, u32[]{:S(2)}) copy-start(f32[2,3,2,64,512]{4,3,2,1,0:T(8,128)} %refs_0_.3) | copy-start | bytes 4718596
  21.8 49.8 %collective-permute-start.9 = (f32[264,512]{1,0:T(8,128)S(1)}, f32[264,512]{1,0:T(8,128)S(1)}, u32[]{:S(2)}, u32[]{:S(2)}) collective-permute-start(f32[264,512]{1,0:T(8,128)S(1)} %get-tuple-element.26.refs_2_.refs_5_), channel_id=1, source_target_pairs={{0,8},{8,16},{16,24},{24,32},{32,40},{40,48},{48,56},{56,64},{64,7... | collective-permute-start | bytes 1622024 | tf_op jit(solution)/shard_map/ppermute | solution.py:573
  35.8 38.5 %copy-start.6 = (bf16[2,2,256,256]{3,2,1,0:T(8,128)(2,1)S(1)}, bf16[2,2,256,256]{3,2,1,0:T(8,128)(2,1)}, u32[]{:S(2)}) copy-start(bf16[2,2,256,256]{3,2,1,0:T(8,128)(2,1)} %constant.7.clone.refs_12_) | copy-start | bytes 1572868
  35.8 30.8 %collective-permute-start.3 = (f32[25,512]{1,0:T(8,128)S(1)}, f32[25,512]{1,0:T(8,128)S(1)}, u32[]{:S(2)}, u32[]{:S(2)}) collective-permute-start(f32[25,512]{1,0:T(8,128)S(1)} %get-tuple-element.22.refs_0_), channel_id=1, source_target_pairs={{0,2},{1,3},{2,0},{3,1},{4,6},{5,7},{6,4},{7,5},{8,10},{9,11},{10,... | collective-permute-start | bytes 153608 | tf_op jit(solution)/shard_map/ppermute | solution.py:581
  49.5 19.0 %collective-permute-start.5 = (f32[25,512]{1,0:T(8,128)S(1)}, f32[25,512]{1,0:T(8,128)S(1)}, u32[]{:S(2)}, u32[]{:S(2)}) collective-permute-start(f32[25,512]{1,0:T(8,128)S(1)} %get-tuple-element.22.refs_0_), channel_id=1, source_target_pairs={{0,4},{1,5},{2,6},{3,7},{4,0},{5,1},{6,2},{7,3},{8,12},{9,13},{10,... | collective-permute-start | bytes 153608 | tf_op jit(solution)/shard_map/ppermute | solution.py:581
  55.9 15.7 %collective-permute-start.7 = (f32[25,512]{1,0:T(8,128)S(1)}, f32[25,512]{1,0:T(8,128)S(1)}, u32[]{:S(2)}, u32[]{:S(2)}) collective-permute-start(f32[25,512]{1,0:T(8,128)S(1)} %get-tuple-element.22.refs_0_), channel_id=1, source_target_pairs={{0,6},{1,7},{2,4},{3,5},{4,2},{5,3},{6,0},{7,1},{8,14},{9,15},{10,... | collective-permute-start | bytes 153608 | tf_op jit(solution)/shard_map/ppermute | solution.py:581
  57.0 17.3 %collective-permute-start.2 = (f32[25,512]{1,0:T(8,128)S(1)}, f32[25,512]{1,0:T(8,128)S(1)}, u32[]{:S(2)}, u32[]{:S(2)}) collective-permute-start(f32[25,512]{1,0:T(8,128)S(1)} %get-tuple-element.22.refs_0_), channel_id=1, source_target_pairs={{0,1},{1,0},{2,3},{3,2},{4,5},{5,4},{6,7},{7,6},{8,9},{9,8},{10,11... | collective-permute-start | bytes 153608 | tf_op jit(solution)/shard_map/ppermute | solution.py:581
  66.6 7.7 %collective-permute-start.4 = (f32[25,512]{1,0:T(8,128)S(1)}, f32[25,512]{1,0:T(8,128)S(1)}, u32[]{:S(2)}, u32[]{:S(2)}) collective-permute-start(f32[25,512]{1,0:T(8,128)S(1)} %collective-permute-done.3.refs_2_), channel_id=1, source_target_pairs={{0,1},{1,0},{2,3},{3,2},{4,5},{5,4},{6,7},{7,6},{8,9},{9,8},{10,11... | collective-permute-start | bytes 153608 | tf_op jit(solution)/shard_map/ppermute | solution.py:581
  68.5 5.8 %collective-permute-start.6 = (f32[25,512]{1,0:T(8,128)S(1)}, f32[25,512]{1,0:T(8,128)S(1)}, u32[]{:S(2)}, u32[]{:S(2)}) collective-permute-start(f32[25,512]{1,0:T(8,128)S(1)} %collective-permute-done.5.refs_4_), channel_id=1, source_target_pairs={{0,1},{1,0},{2,3},{3,2},{4,5},{5,4},{6,7},{7,6},{8,9},{9,8},{10,11... | collective-permute-start | bytes 153608 | tf_op jit(solution)/shard_map/ppermute | solution.py:581
  71.6 2.7 %collective-permute-start.8 = (f32[25,512]{1,0:T(8,128)S(1)}, f32[25,512]{1,0:T(8,128)S(1)}, u32[]{:S(2)}, u32[]{:S(2)}) collective-permute-start(f32[25,512]{1,0:T(8,128)S(1)} %collective-permute-done.7.refs_6_), channel_id=1, source_target_pairs={{0,1},{1,0},{2,3},{3,2},{4,5},{5,4},{6,7},{7,6},{8,9},{9,8},{10,11... | collective-permute-start | bytes 153608 | tf_op jit(solution)/shard_map/ppermute | solution.py:581
  77.3 18.7 %collective-permute-start.11 = (f32[3,64,512]{2,1,0:T(8,128)S(1)}, f32[3,64,512]{2,1,0:T(8,128)S(1)}, u32[]{:S(2)}, u32[]{:S(2)}) collective-permute-start(f32[3,64,512]{2,1,0:T(8,128)S(1)} %get-tuple-element.28.refs_1_), channel_id=1, source_target_pairs={{0,8},{8,16},{16,24},{24,32},{32,40},{40,48},{48,56},{56,64},{64,7... | collective-permute-start | bytes 1179656 | tf_op jit(solution)/shard_map/ppermute | solution.py:573
  77.5 18.4 %collective-permute-start.12 = (f32[3,64,512]{2,1,0:T(8,128)S(1)}, f32[3,64,512]{2,1,0:T(8,128)S(1)}, u32[]{:S(2)}, u32[]{:S(2)}) collective-permute-start(f32[3,64,512]{2,1,0:T(8,128)S(1)} %get-tuple-element.27.refs_0_), channel_id=1, source_target_pairs={{0,248},{8,0},{16,8},{24,16},{32,24},{40,32},{48,40},{56,48},{64,5... | collective-permute-start | bytes 1179656 | tf_op jit(solution)/shard_map/ppermute | solution.py:573
  100.8 14.2 %collective-permute-start.14 = (f32[25,512]{1,0:T(8,128)S(1)}, f32[25,512]{1,0:T(8,128)S(1)}, u32[]{:S(2)}, u32[]{:S(2)}) collective-permute-start(f32[25,512]{1,0:T(8,128)S(1)} %get-tuple-element.31.refs_0_), channel_id=1, source_target_pairs={{0,2},{1,3},{2,0},{3,1},{4,6},{5,7},{6,4},{7,5},{8,10},{9,11},{10,... | collective-permute-start | bytes 153608 | tf_op jit(solution)/shard_map/ppermute | solution.py:581
  111.3 4.6 %collective-permute-start.16 = (f32[25,512]{1,0:T(8,128)S(1)}, f32[25,512]{1,0:T(8,128)S(1)}, u32[]{:S(2)}, u32[]{:S(2)}) collective-permute-start(f32[25,512]{1,0:T(8,128)S(1)} %get-tuple-element.31.refs_0_), channel_id=1, source_target_pairs={{0,4},{1,5},{2,6},{3,7},{4,0},{5,1},{6,2},{7,3},{8,12},{9,13},{10,... | collective-permute-start | bytes 153608 | tf_op jit(solution)/shard_map/ppermute | solution.py:581
  112.2 8.1 %collective-permute-start.18 = (f32[25,512]{1,0:T(8,128)S(1)}, f32[25,512]{1,0:T(8,128)S(1)}, u32[]{:S(2)}, u32[]{:S(2)}) collective-permute-start(f32[25,512]{1,0:T(8,128)S(1)} %get-tuple-element.31.refs_0_), channel_id=1, source_target_pairs={{0,6},{1,7},{2,4},{3,5},{4,2},{5,3},{6,0},{7,1},{8,14},{9,15},{10,... | collective-permute-start | bytes 153608 | tf_op jit(solution)/shard_map/ppermute | solution.py:581
  113.5 6.7 %collective-permute-start.13 = (f32[25,512]{1,0:T(8,128)S(1)}, f32[25,512]{1,0:T(8,128)S(1)}, u32[]{:S(2)}, u32[]{:S(2)}) collective-permute-start(f32[25,512]{1,0:T(8,128)S(1)} %get-tuple-element.31.refs_0_), channel_id=1, source_target_pairs={{0,1},{1,0},{2,3},{3,2},{4,5},{5,4},{6,7},{7,6},{8,9},{9,8},{10,11... | collective-permute-start | bytes 153608 | tf_op jit(solution)/shard_map/ppermute | solution.py:581
  114.9 5.3 %collective-permute-start.15 = (f32[25,512]{1,0:T(8,128)S(1)}, f32[25,512]{1,0:T(8,128)S(1)}, u32[]{:S(2)}, u32[]{:S(2)}) collective-permute-start(f32[25,512]{1,0:T(8,128)S(1)} %collective-permute-done.14.refs_2_), channel_id=1, source_target_pairs={{0,1},{1,0},{2,3},{3,2},{4,5},{5,4},{6,7},{7,6},{8,9},{9,8},{10,11... | collective-permute-start | bytes 153608 | tf_op jit(solution)/shard_map/ppermute | solution.py:581
  115.9 5.2 %collective-permute-start.17 = (f32[25,512]{1,0:T(8,128)S(1)}, f32[25,512]{1,0:T(8,128)S(1)}, u32[]{:S(2)}, u32[]{:S(2)}) collective-permute-start(f32[25,512]{1,0:T(8,128)S(1)} %collective-permute-done.16.refs_4_), channel_id=1, source_target_pairs={{0,1},{1,0},{2,3},{3,2},{4,5},{5,4},{6,7},{7,6},{8,9},{9,8},{10,11... | collective-permute-start | bytes 153608 | tf_op jit(solution)/shard_map/ppermute | solution.py:581
  120.2 1.3 %collective-permute-start.19 = (f32[25,512]{1,0:T(8,128)S(1)}, f32[25,512]{1,0:T(8,128)S(1)}, u32[]{:S(2)}, u32[]{:S(2)}) collective-permute-start(f32[25,512]{1,0:T(8,128)S(1)} %collective-permute-done.18.refs_6_), channel_id=1, source_target_pairs={{0,1},{1,0},{2,3},{3,2},{4,5},{5,4},{6,7},{7,6},{8,9},{9,8},{10,11... | collective-permute-start | bytes 153608 | tf_op jit(solution)/shard_map/ppermute | solution.py:581
  (5 other events, 4.9 us)

commit v4 on v3

--- a/solution.py
+++ b/solution.py
@@ -1,5 +1,3 @@
-import math
-
 import jax
 import jax.numpy as jnp
 import numpy as np
@@ -8,6 +6,7 @@
 from jax.experimental.pallas import tpu as pltpu
 from jax.sharding import PartitionSpec as P
 
+
 N = 512
 H = 256
 ROWS = 64
@@ -15,6 +14,7 @@
 BL = 128
 TIME_STEP = 0.25
 VMEM_LIMIT = 16 * 1024 * 1024
+WIDE_LIMIT = 60 * 1024 * 1024
 CUU_ROW = ROWS
 CWW_ROW = CUU_ROW + GROUPS
 CWU_ROW = CWW_ROW + GROUPS
@@ -193,7 +193,7 @@
             pltpu.VMEM((2, ROWS, N), jnp.int32),
             pltpu.SemaphoreType.DMA((5,)),
         ],
-        compiler_params=pltpu.CompilerParams(vmem_limit_bytes=VMEM_LIMIT),
+        compiler_params=pltpu.CompilerParams(vmem_limit_bytes=WIDE_LIMIT),
         cost_estimate=pl.CostEstimate(flops=40_000_000, bytes_accessed=1_000_000, transcendentals=0),
         name="early",
     )(count, blocks, shifts, lam)
@@ -214,11 +214,12 @@
 
 
 def pack_kernel(count_ref, blocks_ref, shift_ref, omega_ref, *out_refs):
-    for plane, out_ref in enumerate(out_refs):
-        out_ref[2 * BL :, :] = jnp.zeros((8, N), jnp.float32)
-        for s in range(2):
+    for s in range(2):
+        for plane in range(2):
+            out_ref = out_refs[2 * s + plane]
+            out_ref[BL:, :] = jnp.zeros((8, out_ref.shape[1]), jnp.float32)
             ids = live_ids(count_ref, blocks_ref, s, 1 - plane)
-            out_ref[2 * BL + s : 2 * BL + s + 1, 0:BL] = ids.astype(jnp.float32)
+            out_ref[BL : BL + 1, 0:BL] = ids.astype(jnp.float32)
             total = jnp.zeros((BL, 3 * BL), jnp.float32)
             for q in range(4):
                 chosen = chosen_rows(ids, q)
@@ -228,35 +229,49 @@
                     total = total + lax.dot_general(
                         chosen, part, (((0,), (0,)), ((), ())), preferred_element_type=jnp.float32
                     )
-            out_ref[s * BL : (s + 1) * BL, 0 : 3 * BL] = total
-        code = shift_ref[1, plane].astype(jnp.float32) + 8.0 * moved_of(ids)
-        for q in range(4):
-            out_ref[q * ROWS : (q + 1) * ROWS, 3 * BL :] = code[:, q * BL : (q + 1) * BL]
+            out_ref[0:BL, 0 : 3 * BL] = total
+            if s == 1:
+                code = shift_ref[1, plane].astype(jnp.float32) + 8.0 * moved_of(ids)
+                for q in range(4):
+                    rows = slice((q % 2) * ROWS, (q % 2 + 1) * ROWS)
+                    lanes = slice((3 + q // 2) * BL, (4 + q // 2) * BL)
+                    out_ref[rows, lanes] = code[:, q * BL : (q + 1) * BL]
 
 
 def packed_of(count, blocks, shifts, omega):
-    return pl.pallas_call(
+    out = pl.pallas_call(
         pack_kernel,
-        out_shape=(jax.ShapeDtypeStruct((2 * BL + 8, N), jnp.float32),) * 2,
+        out_shape=(jax.ShapeDtypeStruct((BL + 8, 3 * BL), jnp.float32),) * 2
+        + (jax.ShapeDtypeStruct((BL + 8, 5 * BL), jnp.float32),) * 2,
         in_specs=[
             pl.BlockSpec(memory_space=pltpu.SMEM),
             pl.BlockSpec(memory_space=pltpu.VMEM),
             pl.BlockSpec(memory_space=pltpu.VMEM),
             pl.BlockSpec(memory_space=pltpu.VMEM),
         ],
-        out_specs=(pl.BlockSpec(memory_space=pltpu.VMEM),) * 2,
+        out_specs=(pl.BlockSpec(memory_space=pltpu.VMEM),) * 4,
         compiler_params=pltpu.CompilerParams(vmem_limit_bytes=VMEM_LIMIT),
         cost_estimate=pl.CostEstimate(flops=300_000_000, bytes_accessed=3_000_000, transcendentals=0),
         name="pack",
     )(count, blocks, shifts, omega)
-
-
-def code_rows(s, early_ref, packed_ref, start):
+    return out[:2], out[2:]
+
+
+def summed(refs, index):
+    value = refs[0][index]
+    for ref in refs[1:]:
+        value = value + ref[index]
+    return value
+
+
+def code_rows(s, refs, start):
     if s == 0:
-        return early_ref[3, pl.ds(start, 8), :]
-    return jnp.concatenate(
-        [packed_ref[pl.ds(q * ROWS + start, 8), 3 * BL :] for q in range(4)], axis=1
-    )
+        return summed(refs, (3, pl.ds(start, 8), slice(None)))
+    parts = []
+    for q in range(4):
+        rows = pl.ds((q % 2) * ROWS + start, 8)
+        parts.append(summed(refs, (rows, slice((3 + q // 2) * BL, (4 + q // 2) * BL))))
+    return jnp.concatenate(parts, axis=1)
 
 
 def deposit(own, own_code, other, other_code):
@@ -271,15 +286,11 @@
     return total
 
 
-def omega_kernel(s, *refs):
-    own_ref = refs[0]
-    packed = refs[1:5]
-    early = refs[5:9] if s == 0 else (None,) * 4
-    out_ref, far_ref = refs[-2:]
+def omega_kernel(s, own_ref, own_codes, far_codes, far_packed, out_ref, far_ref):
     for plane in range(2):
-        other_ref = packed[2 + plane]
-        ids = other_ref[2 * BL + s : 2 * BL + s + 1, 0:BL].astype(jnp.int32)
-        parts = parts_of(other_ref[s * BL : (s + 1) * BL, 0 : 3 * BL])
+        refs = far_packed[plane]
+        ids = summed(refs, (slice(BL, BL + 1), slice(0, BL))).astype(jnp.int32)
+        parts = parts_of(summed(refs, (slice(0, BL), slice(0, 3 * BL))))
         for q in range(4):
             chosen = chosen_rows(ids, q)
             total = None
@@ -293,17 +304,19 @@
         def _(step, plane=plane):
             start = pl.multiple_of(step * 8, 8)
             rows = pl.ds(start, 8)
-            own_code = code_rows(s, early[plane], packed[plane], start)
-            other_code = code_rows(s, early[2 + plane], packed[2 + plane], start)
+            own_code = code_rows(s, (own_codes[plane],), start)
+            other_code = code_rows(s, far_codes[plane], start)
             for c in range(3):
                 out_ref[c, plane, rows, :] = deposit(
                     own_ref[s, c, plane, rows, :], own_code, far_ref[c, rows, :], other_code
                 )
 
 
-def omega_of(s, *args):
+def omega_of(s, own, own_codes, far_codes, far_packed):
+    args, tree = jax.tree.flatten((own, own_codes, far_codes, far_packed))
+
     def body(*refs):
-        omega_kernel(s, *refs)
+        omega_kernel(s, *jax.tree.unflatten(tree, refs[: len(args)]), *refs[len(args) :])
 
     return pl.pallas_call(
         body,
@@ -320,10 +333,10 @@
 SUBLANE = (0, 4, 12)
 
 
-def first_kernel(s, *refs):
-    own_refs, far_refs = refs[0:2], refs[2:4]
-    packed = refs[4:8] if s else (None,) * 4
-    forward_ref, table_ref, lam_ref, u_ref, ends_ref, x_ref, h_ref = refs[-7:]
+def first_kernel(
+    s, own_refs, far_refs, own_codes, far_codes, forward_ref, table_ref,
+    lam_ref, u_ref, ends_ref, x_ref, h_ref,
+):
     for plane, other in ((0, 0), (1, 3)):
         own_ref, other_ref = own_refs[plane], far_refs[plane]
 
@@ -331,8 +344,8 @@
         def _(step, plane=plane, other=other, own_ref=own_ref, other_ref=other_ref):
             start = pl.multiple_of(step * 8, 8)
             rows = pl.ds(start, 8)
-            own_code = code_rows(s, own_ref, packed[plane], start)
-            other_code = code_rows(s, other_ref, packed[2 + plane], start)
+            own_code = code_rows(s, (own_codes[plane],), start)
+            other_code = code_rows(s, far_codes[plane], start)
             for c in range(3):
                 own = own_ref[c, rows, :]
                 far = other_ref[c, rows, :]
@@ -391,9 +404,11 @@
     ends_ref[24:25, 0:BL] = jnp.sum(jnp.where(used, sums, 0.0), axis=0, keepdims=True)
 
 
-def first_of(s, *args):
+def first_of(s, lows, far, own_codes, far_codes, forward, table):
+    args, tree = jax.tree.flatten((lows, far, own_codes, far_codes, forward, table))
+
     def body(*refs):
-        first_kernel(s, *refs)
+        first_kernel(s, *jax.tree.unflatten(tree, refs[: len(args)]), *refs[len(args) :])
 
     return pl.pallas_call(
         body,
@@ -574,7 +589,28 @@
 
 
 def neighbours(lower_plane, upper_plane):
-    return shifted(upper_plane, "slab", 1), shifted(lower_plane, "slab", -1)
+    below = shifted(upper_plane, "slab", 1)
+    above = shifted(lower_plane, "slab", -1)
+    return below, above
+
+
+FAR = ((15, 16), (31, 0))
+RELAY_UP = ({15: 3, 31: 19}, {3: 16, 19: 0})
+RELAY_DOWN = ({16: 28, 0: 12}, {28: 15, 12: 31})
+
+
+def relayed(lower_plane, upper_plane):
+    count = lax.axis_size("slab")
+    up = [(i, (i + 1) % count) for i in range(count)]
+    out = []
+    for value, near, relay in (
+        (upper_plane, [p for p in up if p not in FAR], RELAY_UP),
+        (lower_plane, [(b, a) for a, b in up if (a, b) not in FAR], RELAY_DOWN),
+    ):
+        hop = lax.ppermute(value, "slab", list(relay[0].items()))
+        direct = lax.ppermute(value, "slab", near)
+        out.append((direct, lax.ppermute(hop, "slab", list(relay[1].items()))))
+    return out
 
 
 def crossed(value, mask):
@@ -589,7 +625,7 @@
     return out
 
 
-def shards(adjoint_vort, omega_ckpt, cell_shift, move_count, move_blocks):
+def steps(adjoint_vort, omega_ckpt, cell_shift, move_count, move_blocks):
     t = tables()
     forward, inverse = halves(t["forward"]), halves(t["inverse"])
     rows = [t["rpow"], t["cuu"], t["cww"], t["cwu"], t["r"][None], t["swap"][None]]
@@ -598,16 +634,17 @@
     lows = early_of(move_count, move_blocks, cell_shift, adjoint_vort)
     far = neighbours(*lows)
     packed = packed_of(move_count, move_blocks, cell_shift, omega_ckpt)
-    far_packed = neighbours(*packed)
+    far_packed = [relayed(*pair) for pair in packed]
     for s in range(2):
-        extra = () if s == 0 else (*packed, *far_packed)
-        if s:
+        if s == 0:
+            own_codes, far_codes = lows, [(value,) for value in far]
+            omega = omega_of(s, omega_ckpt, own_codes, far_codes, far_packed[0])
+        else:
             far = neighbours(*lows)
-            omega = omega_of(s, omega_ckpt, *packed, *far_packed)
+            own_codes, far_codes = packed[1], far_packed[1]
+            omega = omega_of(s, omega_ckpt, own_codes, far_codes, far_packed[1])
             far, omega = lax.optimization_barrier((far, omega))
-        else:
-            omega = omega_of(s, omega_ckpt, *packed, *far_packed, *lows, *far)
-        lam_r, u, ends = first_of(s, *lows, *far, *extra, forward, table)
+        lam_r, u, ends = first_of(s, lows, far, own_codes, far_codes, forward, table)
         out = second_of(t, s == 1, *gathered(ends), u, lam_r, omega, table, inverse)
         if s == 0:
             lows = out
@@ -616,7 +653,7 @@
 
 def solution(mesh):
     return jax.shard_map(
-        shards,
+        steps,
         mesh=mesh,
         in_specs=(
             P(None, "slab", "pencil", None),

time: 127 us -> 127 us (level)
  waiting for transfers between devices: 22.8 us -> 28.5 us
  starting transfers between devices: 73 us -> 67.4 us
  Pallas kernels: 24.5 us -> 26.1 us
    ppermute x0 -> x12, waiting for transfers between devices: none -> 27.3 us  [the longest x4 12.3 us: relayed(): out.append((direct, lax.ppermute(hop, 'slab', list(relay[1].items()))))]
    ppermute x14, starting transfers between devices: 49 us -> 24.3 us  [crossed(): return lax.ppermute(value, 'pencil', [(i, i ^ mask) for i in range(GROUPS)])]
    ppermute x0 -> x12, starting transfers between devices: none -> 20.8 us  [the longest x4 9.03 us: relayed(): hop = lax.ppermute(value, 'slab', list(relay[0].items()))]
    ppermute x6 -> x4, waiting for transfers between devices: 15.4 us -> 0.01 us  [shifted(): lax.ppermute(value, axis, [(i, (i + by) % count) for i in range(count)])]
    ppermute x14, waiting for transfers between devices: 7.45 us -> 1.27 us  [crossed(): return lax.ppermute(value, 'pencil', [(i, i ^ mask) for i in range(GROUPS)])]
    ppermute x6 -> x4, starting transfers between devices: 23.9 us -> 22.2 us  [shifted(): lax.ppermute(value, axis, [(i, (i + by) % count) for i in range(count)])]
    pallas_call x1, Pallas kernels: 0.82 us -> 2.29 us  [early_of(): pl.pallas_call(early_kernel, out_shape=(jax.ShapeDtypeStruct((4, ROWS, N)...]
    unnamed x18 -> x20, local copies, waits for them, and re-layouts: 4.96 us -> 3.84 us
  transfers between devices with their start and end apart: 20 -> 30, of which waited for: 6 -> 6; matrix products, arithmetic and copies ran while one was open for 0% -> 0% of each run, Pallas kernels for 10% -> 12%
where the time goes in v4:
time: 127 us; the launch traced here: 126 us
  starting transfers between devices  67.4 us (53%)
  waiting for transfers between devices  28.5 us (22%)
  Pallas kernels  26.1 us (21%)
  local copies, waits for them, and re-layouts  3.84 us (3%)
    ppermute x14, starting transfers between devices, crossed(): return lax.ppermute(value, 'pencil', [(i, i ^ mask) for i in range(GROUPS)])  24.3 us
    ppermute x4, starting transfers between devices, shifted(): lax.ppermute(value, axis, [(i, (i + by) % count) for i in range(count)])  22.2 us
    ppermute x4, waiting for transfers between devices, relayed(): out.append((direct, lax.ppermute(hop, 'slab', list(relay[1].items()))))  12.3 us
    pallas_call x2, Pallas kernels, first_of(): pl.pallas_call(body, out_shape=(jax.ShapeDtypeStruct((3, 2, ROWS, N), jnp...  9.52 us
    ppermute x4, starting transfers between devices, relayed(): hop = lax.ppermute(value, 'slab', list(relay[0].items()))  9.03 us
    ppermute x4, waiting for transfers between devices, relayed(): hop = lax.ppermute(value, 'slab', list(relay[0].items()))  8.03 us
    ppermute x4, starting transfers between devices, relayed(): direct = lax.ppermute(value, 'slab', near)  7.88 us
    ppermute x4, waiting for transfers between devices, relayed(): direct = lax.ppermute(value, 'slab', near)  6.97 us
  transfers between devices with their start and end apart: 30, of which 6 were waited for; matrix products, arithmetic and copies ran while one was open for 0% of the time, Pallas kernels for 12%

profile of v4, /device:TPU:1, one launch (start us, length us, event | category | flops | bytes accessed | tf_op | source)
XLA Modules:
  0.0 126.1 jit_solution(3648307808199224357)
XLA Ops:
  0.0 2.3 %early.1 = (f32[4,64,512]{2,1,0:T(8,128)}, f32[4,64,512]{2,1,0:T(8,128)}) custom-call(s32[2,1,1,2]{3,2,1,0:T(1,128)} %count_ref.1, s32[2,1,1,2,128]{4,3,2,1,0:T(2,128)} %blocks_ref.1, s32[2,2,64,512]{3,2,1,0:T(8,128)} %shift_ref.1, f32[3,2,64,512]{3,2,1,0:T(8,128)} %lam_hbm.1), custom_call_target="tpu_custom_call" | custom-call | flops 40000000 | bytes 1000000 | tf_op jit(solution)/shard_map/early/pallas_call | solution.py:185
  2.3 2.2 %collective-permute-start = (f32[4,64,512]{2,1,0:T(8,128)}, f32[4,64,512]{2,1,0:T(8,128)S(1)}, u32[]{:S(2)}, u32[]{:S(2)}) collective-permute-start(f32[4,64,512]{2,1,0:T(8,128)} %get-tuple-element.23.refs_1_.refs_5_.refs_2_), channel_id=1, source_target_pairs={{0,8},{8,16},{16,24},{24,32},{32,40},{40,48},{48,56},{56,64},{64,7... | collective-permute-start | bytes 1572872 | tf_op jit(solution)/shard_map/ppermute | solution.py:588
  4.5 10.3 %collective-permute-start.1 = (f32[4,64,512]{2,1,0:T(8,128)}, f32[4,64,512]{2,1,0:T(8,128)S(1)}, u32[]{:S(2)}, u32[]{:S(2)}) collective-permute-start(f32[4,64,512]{2,1,0:T(8,128)} %get-tuple-element.22.refs_0_.refs_4_.refs_1_), channel_id=1, source_target_pairs={{0,248},{8,0},{16,8},{24,16},{32,24},{40,32},{48,40},{56,48},{64,5... | collective-permute-start | bytes 1572872 | tf_op jit(solution)/shard_map/ppermute | solution.py:588
  14.8 1.4 %copy-done = f32[2,3,2,64,512]{4,3,2,1,0:T(8,128)S(1)} copy-done((f32[2,3,2,64,512]{4,3,2,1,0:T(8,128)S(1)}, f32[2,3,2,64,512]{4,3,2,1,0:T(8,128)}, u32[]{:S(2)}) %copy-start) | copy-done | bytes 1572888
  18.7 2.0 %pack.1 = (f32[136,384]{1,0:T(8,128)S(1)}, f32[136,384]{1,0:T(8,128)S(1)}, f32[136,640]{1,0:T(8,128)S(1)}, f32[136,640]{1,0:T(8,128)S(1)}) custom-call(s32[2,1,1,2]{3,2,1,0:T(1,128)S(1)} %copy-done.6, s32[2,1,1,2,128]{4,3,2,1,0:T(2,128)S(1)} %copy-done.5, s32[2,2,64,512]{3,2,1,0:T(8,128)S(1)} %copy-done.2, f32[2,3,2,64,512]{4,3,2,1,0:T(8,128)S(1)} %copy-done), custom_call_target="tpu_custom_call" | custom-call | flops 300000000 | bytes 3000000 | tf_op jit(solution)/shard_map/pack/pallas_call | solution.py:242
  21.4 1.4 %collective-permute-start.13 = (f32[136,384]{1,0:T(8,128)S(1)}, f32[136,384]{1,0:T(8,128)S(1)}, u32[]{:S(2)}, u32[]{:S(2)}) collective-permute-start(f32[136,384]{1,0:T(8,128)S(1)} %get-tuple-element.28), channel_id=1, source_target_pairs={{128,224},{0,96},{129,225},{1,97},{130,226},{2,98},{131,227},{3,99... | collective-permute-start | bytes 626696 | tf_op jit(solution)/shard_map/ppermute | solution.py:610
  24.2 4.0 %collective-permute-start.9 = (f32[136,384]{1,0:T(8,128)S(1)}, f32[136,384]{1,0:T(8,128)S(1)}, u32[]{:S(2)}, u32[]{:S(2)}) collective-permute-start(f32[136,384]{1,0:T(8,128)S(1)} %get-tuple-element.27), channel_id=1, source_target_pairs={{0,8},{8,16},{16,24},{24,32},{32,40},{40,48},{48,56},{56,64},{64,7... | collective-permute-start | bytes 626696 | tf_op jit(solution)/shard_map/ppermute | solution.py:611
  28.2 8.0 %collective-permute-done.13 = f32[136,384]{1,0:T(8,128)S(1)} collective-permute-done((f32[136,384]{1,0:T(8,128)S(1)}, f32[136,384]{1,0:T(8,128)S(1)}, u32[]{:S(2)}, u32[]{:S(2)}) %collective-permute-start.13) | collective-permute-done | bytes 208928 | tf_op jit(solution)/shard_map/ppermute | solution.py:610
  38.2 4.7 %first.2 = (f32[3,2,64,512]{3,2,1,0:T(8,128)S(1)}, f32[4,1024,128]{2,1,0:T(8,128)S(1)}, f32[25,512]{1,0:T(8,128)S(1)}) custom-call(f32[4,64,512]{2,1,0:T(8,128)S(1)} %copy-done.3, f32[4,64,512]{2,1,0:T(8,128)S(1)} %copy-done.4, f32[4,64,512]{2,1,0:T(8,128)S(1)} %collective-permute-done.refs_2_.refs_6_.refs_3_, ...), custom_call_target="tpu_custom_call" | custom-call | flops 3000000000 | bytes 8000000 | tf_op jit(solution)/shard_map/first/pallas_call | solution.py:413
  44.5 2.0 %collective-permute-start.7 = (f32[25,512]{1,0:T(8,128)S(1)}, f32[25,512]{1,0:T(8,128)S(1)}, u32[]{:S(2)}, u32[]{:S(2)}) collective-permute-start(f32[25,512]{1,0:T(8,128)S(1)} %get-tuple-element.24.refs_0_), channel_id=1, source_target_pairs={{0,6},{1,7},{2,4},{3,5},{4,2},{5,3},{6,0},{7,1},{8,14},{9,15},{10,... | collective-permute-start | bytes 153608 | tf_op jit(solution)/shard_map/ppermute | solution.py:617
  46.5 4.2 %collective-permute-done.11.refs_6_ = f32[136,384]{1,0:T(8,128)S(1)} collective-permute-done((f32[136,384]{1,0:T(8,128)S(1)}, f32[136,384]{1,0:T(8,128)S(1)}, u32[]{:S(2)}, u32[]{:S(2)}) %collective-permute-start.11) | collective-permute-done | bytes 208928 | tf_op jit(solution)/shard_map/ppermute | solution.py:612
  53.8 2.7 %omega.2.refs_10_ = f32[3,2,64,512]{3,2,1,0:T(8,128)S(1)} custom-call(f32[2,3,2,64,512]{4,3,2,1,0:T(8,128)S(1)} %copy-done.1, f32[4,64,512]{2,1,0:T(8,128)S(1)} %copy-done.3, f32[4,64,512]{2,1,0:T(8,128)S(1)} %copy-done.4, f32[4,64,512]{2,1,0:T(8,128)S(1)} %collective-permute-done.refs_2_.refs_6_.refs_3_, ...), custom_call_target="tpu_custom_call" | custom-call | flops 300000000 | bytes 6000000 | tf_op jit(solution)/shard_map/omega/pallas_call | solution.py:321
  57.9 6.1 %collective-permute-start.21 = (f32[136,640]{1,0:T(8,128)S(1)}, f32[136,640]{1,0:T(8,128)S(1)}, u32[]{:S(2)}, u32[]{:S(2)}) collective-permute-start(f32[136,640]{1,0:T(8,128)S(1)} %get-tuple-element.31.refs_1_.refs_4_), channel_id=1, source_target_pairs={{128,224},{0,96},{129,225},{1,97},{130,226},{2,98},{131,227},{3,99... | collective-permute-start | bytes 1044488 | tf_op jit(solution)/shard_map/ppermute | solution.py:610
  64.0 2.9 %second.2 = (f32[3,64,512]{2,1,0:T(8,128)S(1)}, f32[3,64,512]{2,1,0:T(8,128)S(1)}) custom-call(f32[25,512]{1,0:T(8,128)S(1)} %get-tuple-element.24.refs_0_, f32[25,512]{1,0:T(8,128)S(1)} %collective-permute-done.2.refs_1_, f32[25,512]{1,0:T(8,128)S(1)} %collective-permute-done.3.refs_2_, f32[25,512]{1,0:T(8,128)S(1)} %collective-permute-done.4.refs_3_, ...), custom_call_target="tpu_custom_call" | custom-call | flops 4000000000 | bytes 8000000 | tf_op jit(solution)/shard_map/second/pallas_call | solution.py:571
  67.0 9.6 %collective-permute-start.16 = (f32[3,64,512]{2,1,0:T(8,128)S(1)}, f32[3,64,512]{2,1,0:T(8,128)S(1)}, u32[]{:S(2)}, u32[]{:S(2)}) collective-permute-start(f32[3,64,512]{2,1,0:T(8,128)S(1)} %get-tuple-element.29.refs_0_), channel_id=1, source_target_pairs={{0,248},{8,0},{16,8},{24,16},{32,24},{40,32},{48,40},{56,48},{64,5... | collective-permute-start | bytes 1179656 | tf_op jit(solution)/shard_map/ppermute | solution.py:588
  79.9 7.0 %collective-permute-done.20.refs_5_.refs_9_.refs_8_ = f32[136,640]{1,0:T(8,128)S(1)} collective-permute-done((f32[136,640]{1,0:T(8,128)S(1)}, f32[136,640]{1,0:T(8,128)S(1)}, u32[]{:S(2)}, u32[]{:S(2)}) %collective-permute-start.20) | collective-permute-done | bytes 348192 | tf_op jit(solution)/shard_map/ppermute | solution.py:611
  86.9 8.1 %collective-permute-done.19.refs_4_.refs_8_.refs_7_ = f32[136,640]{1,0:T(8,128)S(1)} collective-permute-done((f32[136,640]{1,0:T(8,128)S(1)}, f32[136,640]{1,0:T(8,128)S(1)}, u32[]{:S(2)}, u32[]{:S(2)}) %collective-permute-start.19) | collective-permute-done | bytes 348192 | tf_op jit(solution)/shard_map/ppermute | solution.py:612
  95.0 2.7 %omega.3.refs_10_ = f32[3,2,64,512]{3,2,1,0:T(8,128)S(1)} custom-call(f32[2,3,2,64,512]{4,3,2,1,0:T(8,128)S(1)} %copy-done.1, f32[136,640]{1,0:T(8,128)S(1)} %get-tuple-element.31.refs_1_.refs_4_, f32[136,640]{1,0:T(8,128)S(1)} %get-tuple-element.32.refs_2_.refs_5_, f32[136,640]{1,0:T(8,128)S(1)} %collective-permute-done.17.refs_3_.refs_7_.refs_6_, ...), custom_call_target="tpu_custom_call" | custom-call | flops 300000000 | bytes 6000000 | tf_op jit(solution)/shard_map/omega/pallas_call | solution.py:321
  97.8 4.8 %first.3 = (f32[3,2,64,512]{3,2,1,0:T(8,128)S(1)}, f32[4,1024,128]{2,1,0:T(8,128)S(1)}, f32[25,512]{1,0:T(8,128)S(1)}) custom-call(f32[3,64,512]{2,1,0:T(8,128)S(1)} %get-tuple-element.29.refs_0_, f32[3,64,512]{2,1,0:T(8,128)S(1)} %get-tuple-element.30.refs_1_, f32[3,64,512]{2,1,0:T(8,128)S(1)} %collective-permute-done.15.refs_2_, ...), custom_call_target="tpu_custom_call" | custom-call | flops 3000000000 | bytes 8000000 | tf_op jit(solution)/shard_map/first/pallas_call | solution.py:413
  102.6 8.4 %collective-permute-start.24 = (f32[25,512]{1,0:T(8,128)S(1)}, f32[25,512]{1,0:T(8,128)S(1)}, u32[]{:S(2)}, u32[]{:S(2)}) collective-permute-start(f32[25,512]{1,0:T(8,128)S(1)} %get-tuple-element.35.refs_0_), channel_id=1, source_target_pairs={{0,2},{1,3},{2,0},{3,1},{4,6},{5,7},{6,4},{7,5},{8,10},{9,11},{10,... | collective-permute-start | bytes 153608 | tf_op jit(solution)/shard_map/ppermute | solution.py:617
  110.9 2.2 %collective-permute-start.26 = (f32[25,512]{1,0:T(8,128)S(1)}, f32[25,512]{1,0:T(8,128)S(1)}, u32[]{:S(2)}, u32[]{:S(2)}) collective-permute-start(f32[25,512]{1,0:T(8,128)S(1)} %get-tuple-element.35.refs_0_), channel_id=1, source_target_pairs={{0,4},{1,5},{2,6},{3,7},{4,0},{5,1},{6,2},{7,3},{8,12},{9,13},{10,... | collective-permute-start | bytes 153608 | tf_op jit(solution)/shard_map/ppermute | solution.py:617
  114.3 1.3 %collective-permute-start.23 = (f32[25,512]{1,0:T(8,128)S(1)}, f32[25,512]{1,0:T(8,128)S(1)}, u32[]{:S(2)}, u32[]{:S(2)}) collective-permute-start(f32[25,512]{1,0:T(8,128)S(1)} %get-tuple-element.35.refs_0_), channel_id=1, source_target_pairs={{0,1},{1,0},{2,3},{3,2},{4,5},{5,4},{6,7},{7,6},{8,9},{9,8},{10,11... | collective-permute-start | bytes 153608 | tf_op jit(solution)/shard_map/ppermute | solution.py:617
  116.1 5.0 %collective-permute-start.27 = (f32[25,512]{1,0:T(8,128)S(1)}, f32[25,512]{1,0:T(8,128)S(1)}, u32[]{:S(2)}, u32[]{:S(2)}) collective-permute-start(f32[25,512]{1,0:T(8,128)S(1)} %collective-permute-done.26.refs_4_), channel_id=1, source_target_pairs={{0,1},{1,0},{2,3},{3,2},{4,5},{5,4},{6,7},{7,6},{8,9},{9,8},{10,11... | collective-permute-start | bytes 153608 | tf_op jit(solution)/shard_map/ppermute | solution.py:617
  122.3 3.8 %second.3 = f32[3,2,64,512]{3,2,1,0:T(8,128)} custom-call(f32[25,512]{1,0:T(8,128)S(1)} %get-tuple-element.35.refs_0_, f32[25,512]{1,0:T(8,128)S(1)} %collective-permute-done.23.refs_1_, f32[25,512]{1,0:T(8,128)S(1)} %collective-permute-done.24.refs_2_, f32[25,512]{1,0:T(8,128)S(1)} %collective-permute-done.25.refs_3_, ...), custom_call_target="tpu_custom_call" | custom-call | flops 4000000000 | bytes 8000000 | tf_op jit(solution)/shard_map/second/pallas_call | solution.py:571
  (64 shorter events, 18.5 us)
Async XLA Ops:
  2.3 35.2 %collective-permute-start = (f32[4,64,512]{2,1,0:T(8,128)}, f32[4,64,512]{2,1,0:T(8,128)S(1)}, u32[]{:S(2)}, u32[]{:S(2)}) collective-permute-start(f32[4,64,512]{2,1,0:T(8,128)} %get-tuple-element.23.refs_1_.refs_5_.refs_2_), channel_id=1, source_target_pairs={{0,8},{8,16},{16,24},{24,32},{32,40},{40,48},{48,56},{56,64},{64,7... | collective-permute-start | bytes 1572872 | tf_op jit(solution)/shard_map/ppermute | solution.py:588
  4.5 33.7 %collective-permute-start.1 = (f32[4,64,512]{2,1,0:T(8,128)}, f32[4,64,512]{2,1,0:T(8,128)S(1)}, u32[]{:S(2)}, u32[]{:S(2)}) collective-permute-start(f32[4,64,512]{2,1,0:T(8,128)} %get-tuple-element.22.refs_0_.refs_4_.refs_1_), channel_id=1, source_target_pairs={{0,248},{8,0},{16,8},{24,16},{32,24},{40,32},{48,40},{56,48},{64,5... | collective-permute-start | bytes 1572872 | tf_op jit(solution)/shard_map/ppermute | solution.py:588
  21.4 14.8 %collective-permute-start.13 = (f32[136,384]{1,0:T(8,128)S(1)}, f32[136,384]{1,0:T(8,128)S(1)}, u32[]{:S(2)}, u32[]{:S(2)}) collective-permute-start(f32[136,384]{1,0:T(8,128)S(1)} %get-tuple-element.28), channel_id=1, source_target_pairs={{128,224},{0,96},{129,225},{1,97},{130,226},{2,98},{131,227},{3,99... | collective-permute-start | bytes 626696 | tf_op jit(solution)/shard_map/ppermute | solution.py:610
  22.9 21.2 %collective-permute-start.12 = (f32[136,384]{1,0:T(8,128)S(1)}, f32[136,384]{1,0:T(8,128)S(1)}, u32[]{:S(2)}, u32[]{:S(2)}) collective-permute-start(f32[136,384]{1,0:T(8,128)S(1)} %get-tuple-element.28), channel_id=1, source_target_pairs={{8,0},{16,8},{24,16},{32,24},{40,32},{48,40},{56,48},{64,56},{72,6... | collective-permute-start | bytes 626696 | tf_op jit(solution)/shard_map/ppermute | solution.py:611
  24.2 20.3 %collective-permute-start.9 = (f32[136,384]{1,0:T(8,128)S(1)}, f32[136,384]{1,0:T(8,128)S(1)}, u32[]{:S(2)}, u32[]{:S(2)}) collective-permute-start(f32[136,384]{1,0:T(8,128)S(1)} %get-tuple-element.27), channel_id=1, source_target_pairs={{0,8},{8,16},{16,24},{24,32},{32,40},{40,48},{48,56},{56,64},{64,7... | collective-permute-start | bytes 626696 | tf_op jit(solution)/shard_map/ppermute | solution.py:611
  36.2 14.5 %collective-permute-start.11 = (f32[136,384]{1,0:T(8,128)S(1)}, f32[136,384]{1,0:T(8,128)S(1)}, u32[]{:S(2)}, u32[]{:S(2)}) collective-permute-start(f32[136,384]{1,0:T(8,128)S(1)} %collective-permute-done.10), channel_id=1, source_target_pairs={{24,128},{152,0},{25,129},{153,1},{26,130},{154,2},{27,131},{155,3... | collective-permute-start | bytes 626696 | tf_op jit(solution)/shard_map/ppermute | solution.py:612
  37.5 15.5 %collective-permute-start.14 = (f32[136,384]{1,0:T(8,128)S(1)}, f32[136,384]{1,0:T(8,128)S(1)}, u32[]{:S(2)}, u32[]{:S(2)}) collective-permute-start(f32[136,384]{1,0:T(8,128)S(1)} %collective-permute-done.13), channel_id=1, source_target_pairs={{224,120},{96,248},{225,121},{97,249},{226,122},{98,250},{227,123}... | collective-permute-start | bytes 626696 | tf_op jit(solution)/shard_map/ppermute | solution.py:612
  42.9 9.0 %collective-permute-start.3 = (f32[25,512]{1,0:T(8,128)S(1)}, f32[25,512]{1,0:T(8,128)S(1)}, u32[]{:S(2)}, u32[]{:S(2)}) collective-permute-start(f32[25,512]{1,0:T(8,128)S(1)} %get-tuple-element.24.refs_0_), channel_id=1, source_target_pairs={{0,2},{1,3},{2,0},{3,1},{4,6},{5,7},{6,4},{7,5},{8,10},{9,11},{10,... | collective-permute-start | bytes 153608 | tf_op jit(solution)/shard_map/ppermute | solution.py:617
  44.0 7.9 %collective-permute-start.5 = (f32[25,512]{1,0:T(8,128)S(1)}, f32[25,512]{1,0:T(8,128)S(1)}, u32[]{:S(2)}, u32[]{:S(2)}) collective-permute-start(f32[25,512]{1,0:T(8,128)S(1)} %get-tuple-element.24.refs_0_), channel_id=1, source_target_pairs={{0,4},{1,5},{2,6},{3,7},{4,0},{5,1},{6,2},{7,3},{8,12},{9,13},{10,... | collective-permute-start | bytes 153608 | tf_op jit(solution)/shard_map/ppermute | solution.py:617
  44.5 8.5 %collective-permute-start.7 = (f32[25,512]{1,0:T(8,128)S(1)}, f32[25,512]{1,0:T(8,128)S(1)}, u32[]{:S(2)}, u32[]{:S(2)}) collective-permute-start(f32[25,512]{1,0:T(8,128)S(1)} %get-tuple-element.24.refs_0_), channel_id=1, source_target_pairs={{0,6},{1,7},{2,4},{3,5},{4,2},{5,3},{6,0},{7,1},{8,14},{9,15},{10,... | collective-permute-start | bytes 153608 | tf_op jit(solution)/shard_map/ppermute | solution.py:617
  51.9 5.9 %collective-permute-start.4 = (f32[25,512]{1,0:T(8,128)S(1)}, f32[25,512]{1,0:T(8,128)S(1)}, u32[]{:S(2)}, u32[]{:S(2)}) collective-permute-start(f32[25,512]{1,0:T(8,128)S(1)} %collective-permute-done.3.refs_2_), channel_id=1, source_target_pairs={{0,1},{1,0},{2,3},{3,2},{4,5},{5,4},{6,7},{7,6},{8,9},{9,8},{10,11... | collective-permute-start | bytes 153608 | tf_op jit(solution)/shard_map/ppermute | solution.py:617
  52.0 12.0 %collective-permute-start.6 = (f32[25,512]{1,0:T(8,128)S(1)}, f32[25,512]{1,0:T(8,128)S(1)}, u32[]{:S(2)}, u32[]{:S(2)}) collective-permute-start(f32[25,512]{1,0:T(8,128)S(1)} %collective-permute-done.5.refs_4_), channel_id=1, source_target_pairs={{0,1},{1,0},{2,3},{3,2},{4,5},{5,4},{6,7},{7,6},{8,9},{9,8},{10,11... | collective-permute-start | bytes 153608 | tf_op jit(solution)/shard_map/ppermute | solution.py:617
  52.9 11.0 %collective-permute-start.8 = (f32[25,512]{1,0:T(8,128)S(1)}, f32[25,512]{1,0:T(8,128)S(1)}, u32[]{:S(2)}, u32[]{:S(2)}) collective-permute-start(f32[25,512]{1,0:T(8,128)S(1)} %collective-permute-done.7.refs_6_), channel_id=1, source_target_pairs={{0,1},{1,0},{2,3},{3,2},{4,5},{5,4},{6,7},{7,6},{8,9},{9,8},{10,11... | collective-permute-start | bytes 153608 | tf_op jit(solution)/shard_map/ppermute | solution.py:617
  53.0 23.7 %collective-permute-start.18 = (f32[136,640]{1,0:T(8,128)S(1)}, f32[136,640]{1,0:T(8,128)S(1)}, u32[]{:S(2)}, u32[]{:S(2)}) collective-permute-start(f32[136,640]{1,0:T(8,128)S(1)} %get-tuple-element.32.refs_2_.refs_5_), channel_id=1, source_target_pairs={{120,24},{248,152},{121,25},{249,153},{122,26},{250,154},{123,27},... | collective-permute-start | bytes 1044488 | tf_op jit(solution)/shard_map/ppermute | solution.py:610
  56.5 22.7 %collective-permute-start.17 = (f32[136,640]{1,0:T(8,128)S(1)}, f32[136,640]{1,0:T(8,128)S(1)}, u32[]{:S(2)}, u32[]{:S(2)}) collective-permute-start(f32[136,640]{1,0:T(8,128)S(1)} %get-tuple-element.32.refs_2_.refs_5_), channel_id=1, source_target_pairs={{0,8},{8,16},{16,24},{24,32},{32,40},{40,48},{48,56},{56,64},{64,7... | collective-permute-start | bytes 1044488 | tf_op jit(solution)/shard_map/ppermute | solution.py:611
  57.9 20.1 %collective-permute-start.21 = (f32[136,640]{1,0:T(8,128)S(1)}, f32[136,640]{1,0:T(8,128)S(1)}, u32[]{:S(2)}, u32[]{:S(2)}) collective-permute-start(f32[136,640]{1,0:T(8,128)S(1)} %get-tuple-element.31.refs_1_.refs_4_), channel_id=1, source_target_pairs={{128,224},{0,96},{129,225},{1,97},{130,226},{2,98},{131,227},{3,99... | collective-permute-start | bytes 1044488 | tf_op jit(solution)/shard_map/ppermute | solution.py:610
  67.0 30.8 %collective-permute-start.15 = (f32[3,64,512]{2,1,0:T(8,128)S(1)}, f32[3,64,512]{2,1,0:T(8,128)S(1)}, u32[]{:S(2)}, u32[]{:S(2)}) collective-permute-start(f32[3,64,512]{2,1,0:T(8,128)S(1)} %get-tuple-element.30.refs_1_), channel_id=1, source_target_pairs={{0,8},{8,16},{16,24},{24,32},{32,40},{40,48},{48,56},{56,64},{64,7... | collective-permute-start | bytes 1179656 | tf_op jit(solution)/shard_map/ppermute | solution.py:588
  67.0 30.7 %collective-permute-start.16 = (f32[3,64,512]{2,1,0:T(8,128)S(1)}, f32[3,64,512]{2,1,0:T(8,128)S(1)}, u32[]{:S(2)}, u32[]{:S(2)}) collective-permute-start(f32[3,64,512]{2,1,0:T(8,128)S(1)} %get-tuple-element.29.refs_0_), channel_id=1, source_target_pairs={{0,248},{8,0},{16,8},{24,16},{32,24},{40,32},{48,40},{56,48},{64,5... | collective-permute-start | bytes 1179656 | tf_op jit(solution)/shard_map/ppermute | solution.py:588
  76.6 10.3 %collective-permute-start.20 = (f32[136,640]{1,0:T(8,128)S(1)}, f32[136,640]{1,0:T(8,128)S(1)}, u32[]{:S(2)}, u32[]{:S(2)}) collective-permute-start(f32[136,640]{1,0:T(8,128)S(1)} %get-tuple-element.31.refs_1_.refs_4_), channel_id=1, source_target_pairs={{8,0},{16,8},{24,16},{32,24},{40,32},{48,40},{56,48},{64,56},{72,6... | collective-permute-start | bytes 1044488 | tf_op jit(solution)/shard_map/ppermute | solution.py:611
  77.9 17.1 %collective-permute-start.19 = (f32[136,640]{1,0:T(8,128)S(1)}, f32[136,640]{1,0:T(8,128)S(1)}, u32[]{:S(2)}, u32[]{:S(2)}) collective-permute-start(f32[136,640]{1,0:T(8,128)S(1)} %collective-permute-done.18), channel_id=1, source_target_pairs={{24,128},{152,0},{25,129},{153,1},{26,130},{154,2},{27,131},{155,3... | collective-permute-start | bytes 1044488 | tf_op jit(solution)/shard_map/ppermute | solution.py:612
  79.2 15.7 %collective-permute-start.22 = (f32[136,640]{1,0:T(8,128)S(1)}, f32[136,640]{1,0:T(8,128)S(1)}, u32[]{:S(2)}, u32[]{:S(2)}) collective-permute-start(f32[136,640]{1,0:T(8,128)S(1)} %collective-permute-done.21), channel_id=1, source_target_pairs={{224,120},{96,248},{225,121},{97,249},{226,122},{98,250},{227,123}... | collective-permute-start | bytes 1044488 | tf_op jit(solution)/shard_map/ppermute | solution.py:612
  102.6 13.0 %collective-permute-start.24 = (f32[25,512]{1,0:T(8,128)S(1)}, f32[25,512]{1,0:T(8,128)S(1)}, u32[]{:S(2)}, u32[]{:S(2)}) collective-permute-start(f32[25,512]{1,0:T(8,128)S(1)} %get-tuple-element.35.refs_0_), channel_id=1, source_target_pairs={{0,2},{1,3},{2,0},{3,1},{4,6},{5,7},{6,4},{7,5},{8,10},{9,11},{10,... | collective-permute-start | bytes 153608 | tf_op jit(solution)/shard_map/ppermute | solution.py:617
  113.2 7.9 %collective-permute-start.28 = (f32[25,512]{1,0:T(8,128)S(1)}, f32[25,512]{1,0:T(8,128)S(1)}, u32[]{:S(2)}, u32[]{:S(2)}) collective-permute-start(f32[25,512]{1,0:T(8,128)S(1)} %get-tuple-element.35.refs_0_), channel_id=1, source_target_pairs={{0,6},{1,7},{2,4},{3,5},{4,2},{5,3},{6,0},{7,1},{8,14},{9,15},{10,... | collective-permute-start | bytes 153608 | tf_op jit(solution)/shard_map/ppermute | solution.py:617
  114.3 6.8 %collective-permute-start.23 = (f32[25,512]{1,0:T(8,128)S(1)}, f32[25,512]{1,0:T(8,128)S(1)}, u32[]{:S(2)}, u32[]{:S(2)}) collective-permute-start(f32[25,512]{1,0:T(8,128)S(1)} %get-tuple-element.35.refs_0_), channel_id=1, source_target_pairs={{0,1},{1,0},{2,3},{3,2},{4,5},{5,4},{6,7},{7,6},{8,9},{9,8},{10,11... | collective-permute-start | bytes 153608 | tf_op jit(solution)/shard_map/ppermute | solution.py:617
  (16 other events, 189.8 us)

commit v5 on v4

--- a/solution.py
+++ b/solution.py
@@ -213,13 +213,27 @@
     return jnp.where(hit, 1.0, 0.0).astype(jnp.bfloat16)
 
 
-def pack_kernel(count_ref, blocks_ref, shift_ref, omega_ref, *out_refs):
+WIDTHS = (3 * BL, 5 * BL)
+STARTS = (0, 3 * BL)
+
+
+def pack_kernel(count_hbm, blocks_hbm, shift_hbm, omega_hbm, *refs):
+    out_refs = refs[:6]
+    count_ref, blocks_ref, shift_ref, omega_ref, sem = refs[6:]
+    copies = [
+        pltpu.make_async_copy(count_hbm, count_ref, sem.at[0]),
+        pltpu.make_async_copy(blocks_hbm, blocks_ref, sem.at[1]),
+        pltpu.make_async_copy(omega_hbm.at[0], omega_ref.at[0], sem.at[2]),
+        pltpu.make_async_copy(omega_hbm.at[1], omega_ref.at[1], sem.at[3]),
+        pltpu.make_async_copy(shift_hbm.at[1], shift_ref, sem.at[4]),
+    ]
+    for copy in copies:
+        copy.start()
     for s in range(2):
+        for copy in copies[:3] if s == 0 else copies[3:]:
+            copy.wait()
         for plane in range(2):
-            out_ref = out_refs[2 * s + plane]
-            out_ref[BL:, :] = jnp.zeros((8, out_ref.shape[1]), jnp.float32)
             ids = live_ids(count_ref, blocks_ref, s, 1 - plane)
-            out_ref[BL : BL + 1, 0:BL] = ids.astype(jnp.float32)
             total = jnp.zeros((BL, 3 * BL), jnp.float32)
             for q in range(4):
                 chosen = chosen_rows(ids, q)
@@ -229,32 +243,42 @@
                     total = total + lax.dot_general(
                         chosen, part, (((0,), (0,)), ((), ())), preferred_element_type=jnp.float32
                     )
-            out_ref[0:BL, 0 : 3 * BL] = total
+            pieces = [total]
             if s == 1:
-                code = shift_ref[1, plane].astype(jnp.float32) + 8.0 * moved_of(ids)
-                for q in range(4):
-                    rows = slice((q % 2) * ROWS, (q % 2 + 1) * ROWS)
-                    lanes = slice((3 + q // 2) * BL, (4 + q // 2) * BL)
-                    out_ref[rows, lanes] = code[:, q * BL : (q + 1) * BL]
+                code = shift_ref[plane].astype(jnp.float32) + 8.0 * moved_of(ids)
+                part = [code[:, q * BL : (q + 1) * BL] for q in range(4)]
+                pieces += [jnp.concatenate(part[0:2], axis=0), jnp.concatenate(part[2:4], axis=0)]
+            message = jnp.concatenate(pieces, axis=1)
+            for out_ref in (
+                out_refs[plane].at[:, STARTS[s] : STARTS[s] + WIDTHS[s]],
+                out_refs[2 + 2 * s + plane],
+            ):
+                out_ref[0:BL, :] = message
+                out_ref[BL:, :] = jnp.zeros((8, WIDTHS[s]), jnp.float32)
+                out_ref[BL : BL + 1, 0:BL] = ids.astype(jnp.float32)
 
 
 def packed_of(count, blocks, shifts, omega):
     out = pl.pallas_call(
         pack_kernel,
-        out_shape=(jax.ShapeDtypeStruct((BL + 8, 3 * BL), jnp.float32),) * 2
-        + (jax.ShapeDtypeStruct((BL + 8, 5 * BL), jnp.float32),) * 2,
-        in_specs=[
-            pl.BlockSpec(memory_space=pltpu.SMEM),
-            pl.BlockSpec(memory_space=pltpu.VMEM),
-            pl.BlockSpec(memory_space=pltpu.VMEM),
-            pl.BlockSpec(memory_space=pltpu.VMEM),
+        out_shape=tuple(
+            jax.ShapeDtypeStruct((BL + 8, width), jnp.float32)
+            for width in (8 * BL, 8 * BL, WIDTHS[0], WIDTHS[0], WIDTHS[1], WIDTHS[1])
+        ),
+        in_specs=[pl.BlockSpec(memory_space=pltpu.HBM)] * 4,
+        out_specs=(pl.BlockSpec(memory_space=pltpu.VMEM),) * 6,
+        scratch_shapes=[
+            pltpu.SMEM(count.shape, jnp.int32),
+            pltpu.VMEM(blocks.shape, jnp.int32),
+            pltpu.VMEM((2, ROWS, N), jnp.int32),
+            pltpu.VMEM(omega.shape, jnp.float32),
+            pltpu.SemaphoreType.DMA((5,)),
         ],
-        out_specs=(pl.BlockSpec(memory_space=pltpu.VMEM),) * 4,
-        compiler_params=pltpu.CompilerParams(vmem_limit_bytes=VMEM_LIMIT),
+        compiler_params=pltpu.CompilerParams(vmem_limit_bytes=WIDE_LIMIT),
         cost_estimate=pl.CostEstimate(flops=300_000_000, bytes_accessed=3_000_000, transcendentals=0),
         name="pack",
     )(count, blocks, shifts, omega)
-    return out[:2], out[2:]
+    return out[0:2], out[2:4], out[4:6]
 
 
 def summed(refs, index):
@@ -264,9 +288,14 @@
     return value
 
 
+def seen(s, refs):
+    return (refs[0].at[:, STARTS[s] : STARTS[s] + WIDTHS[s]], *refs[1:])
+
+
 def code_rows(s, refs, start):
     if s == 0:
         return summed(refs, (3, pl.ds(start, 8), slice(None)))
+    refs = seen(s, refs)
     parts = []
     for q in range(4):
         rows = pl.ds((q % 2) * ROWS + start, 8)
@@ -288,7 +317,7 @@
 
 def omega_kernel(s, own_ref, own_codes, far_codes, far_packed, out_ref, far_ref):
     for plane in range(2):
-        refs = far_packed[plane]
+        refs = seen(s, far_packed[plane])
         ids = summed(refs, (slice(BL, BL + 1), slice(0, BL))).astype(jnp.int32)
         parts = parts_of(summed(refs, (slice(0, BL), slice(0, 3 * BL))))
         for q in range(4):
@@ -595,21 +624,23 @@
 
 
 FAR = ((15, 16), (31, 0))
-RELAY_UP = ({15: 3, 31: 19}, {3: 16, 19: 0})
-RELAY_DOWN = ({16: 28, 0: 12}, {28: 15, 12: 31})
-
-
-def relayed(lower_plane, upper_plane):
+RELAY_UP = ({15: 12, 31: 28}, {12: 16, 28: 0})
+RELAY_DOWN = ({16: 19, 0: 3}, {19: 15, 3: 31})
+
+
+def relayed(both, singles):
     count = lax.axis_size("slab")
     up = [(i, (i + 1) % count) for i in range(count)]
-    out = []
-    for value, near, relay in (
-        (upper_plane, [p for p in up if p not in FAR], RELAY_UP),
-        (lower_plane, [(b, a) for a, b in up if (a, b) not in FAR], RELAY_DOWN),
-    ):
-        hop = lax.ppermute(value, "slab", list(relay[0].items()))
-        direct = lax.ppermute(value, "slab", near)
-        out.append((direct, lax.ppermute(hop, "slab", list(relay[1].items()))))
+    sides = (
+        (1, [p for p in up if p not in FAR], RELAY_UP),
+        (0, [(b, a) for a, b in up if (a, b) not in FAR], RELAY_DOWN),
+    )
+    out = [[], []]
+    for plane, near, relay in sides:
+        direct = lax.ppermute(both[plane], "slab", near)
+        for s in range(2):
+            hop = lax.ppermute(singles[s][plane], "slab", list(relay[0].items()))
+            out[s].append((direct, lax.ppermute(hop, "slab", list(relay[1].items()))))
     return out
 
 
@@ -634,14 +665,14 @@
     lows = early_of(move_count, move_blocks, cell_shift, adjoint_vort)
     far = neighbours(*lows)
     packed = packed_of(move_count, move_blocks, cell_shift, omega_ckpt)
-    far_packed = [relayed(*pair) for pair in packed]
+    far_packed = relayed(packed[0], packed[1:])
     for s in range(2):
         if s == 0:
             own_codes, far_codes = lows, [(value,) for value in far]
             omega = omega_of(s, omega_ckpt, own_codes, far_codes, far_packed[0])
         else:
             far = neighbours(*lows)
-            own_codes, far_codes = packed[1], far_packed[1]
+            own_codes, far_codes = packed[0], far_packed[1]
             omega = omega_of(s, omega_ckpt, own_codes, far_codes, far_packed[1])
             far, omega = lax.optimization_barrier((far, omega))
         lam_r, u, ends = first_of(s, lows, far, own_codes, far_codes, forward, table)

time: 127 us -> 130 us (1.024)
  waiting for transfers between devices: 28.5 us -> 35.9 us
  local copies, waits for them, and re-layouts: 3.84 us -> 0.04 us
  starting transfers between devices: 67.4 us -> 64.5 us
  Pallas kernels: 26.1 us -> 28.2 us
    ppermute x12 -> x10, starting transfers between devices: 20.8 us -> 12.8 us  [the longest x2 4.82 us: relayed(): direct = lax.ppermute(both[plane], 'slab', near)]
    ppermute x12 -> x10, waiting for transfers between devices: 27.3 us -> 33 us  [the longest x4 20.6 us: relayed(): out[s].append((direct, lax.ppermute(hop, 'slab', list(relay[1].items()))))]
    ppermute x14, starting transfers between devices: 24.3 us -> 29.4 us  [crossed(): return lax.ppermute(value, 'pencil', [(i, i ^ mask) for i in range(GROUPS)])]
    unnamed x20, local copies, waits for them, and re-layouts: 3.84 us -> 0.04 us
    pallas_call x1, Pallas kernels: 2.05 us -> 4.1 us  [packed_of(): pl.pallas_call(pack_kernel, out_shape=tuple((jax.ShapeDtypeStruct((BL + 8...]
    ppermute x14, waiting for transfers between devices: 1.27 us -> 2.85 us  [crossed(): return lax.ppermute(value, 'pencil', [(i, i ^ mask) for i in range(GROUPS)])]
  transfers between devices with their start and end apart: 30 -> 28, of which waited for: 6 -> 8; matrix products, arithmetic and copies ran while one was open for 0% -> 0% of each run, Pallas kernels for 12% -> 13%
where the time goes in v5:
time: 130 us; the launch traced here: 129 us
  starting transfers between devices  64.5 us (50%)
  waiting for transfers between devices  35.9 us (28%)
  Pallas kernels  28.2 us (22%)
    ppermute x14, starting transfers between devices, crossed(): return lax.ppermute(value, 'pencil', [(i, i ^ mask) for i in range(GROUPS)])  29.4 us
    ppermute x4, starting transfers between devices, shifted(): lax.ppermute(value, axis, [(i, (i + by) % count) for i in range(count)])  22.2 us
    ppermute x4, waiting for transfers between devices, relayed(): out[s].append((direct, lax.ppermute(hop, 'slab', list(relay[1].items()))))  20.6 us
    ppermute x4, waiting for transfers between devices, relayed(): hop = lax.ppermute(singles[s][plane], 'slab', list(relay[0].items()))  12.4 us
    pallas_call x2, Pallas kernels, first_of(): pl.pallas_call(body, out_shape=(jax.ShapeDtypeStruct((3, 2, ROWS, N), jnp...  9.54 us
    pallas_call x2, Pallas kernels, second_of(): pl.pallas_call(body, out_shape=shapes, in_specs=[pl.BlockSpec(memory_spac...  6.78 us
    pallas_call x2, Pallas kernels, omega_of(): pl.pallas_call(body, out_shape=jax.ShapeDtypeStruct((3, 2, ROWS, N), jnp....  5.45 us
    ppermute x2, starting transfers between devices, relayed(): direct = lax.ppermute(both[plane], 'slab', near)  4.82 us
  transfers between devices with their start and end apart: 28, of which 8 were waited for; matrix products, arithmetic and copies ran while one was open for 0% of the time, Pallas kernels for 13%

profile of v5, /device:TPU:1, one launch (start us, length us, event | category | flops | bytes accessed | tf_op | source)
XLA Modules:
  0.0 128.9 jit_solution(15318861510964013754)
XLA Ops:
  0.0 2.3 %early.1 = (f32[4,64,512]{2,1,0:T(8,128)}, f32[4,64,512]{2,1,0:T(8,128)}) custom-call(s32[2,1,1,2]{3,2,1,0:T(1,128)} %count_hbm.3, s32[2,1,1,2,128]{4,3,2,1,0:T(2,128)} %blocks_hbm.3, s32[2,2,64,512]{3,2,1,0:T(8,128)} %shift_hbm.3, f32[3,2,64,512]{3,2,1,0:T(8,128)} %lam_hbm.1), custom_call_target="tpu_custom_call" | custom-call | flops 40000000 | bytes 1000000 | tf_op jit(solution)/shard_map/early/pallas_call | solution.py:185
  2.4 2.2 %collective-permute-start = (f32[4,64,512]{2,1,0:T(8,128)}, f32[4,64,512]{2,1,0:T(8,128)S(1)}, u32[]{:S(2)}, u32[]{:S(2)}) collective-permute-start(f32[4,64,512]{2,1,0:T(8,128)} %get-tuple-element.25.refs_1_.refs_5_.refs_2_), channel_id=1, source_target_pairs={{0,8},{8,16},{16,24},{24,32},{32,40},{40,48},{48,56},{56,64},{64,7... | collective-permute-start | bytes 1572872 | tf_op jit(solution)/shard_map/ppermute | solution.py:617
  4.5 10.3 %collective-permute-start.1 = (f32[4,64,512]{2,1,0:T(8,128)}, f32[4,64,512]{2,1,0:T(8,128)S(1)}, u32[]{:S(2)}, u32[]{:S(2)}) collective-permute-start(f32[4,64,512]{2,1,0:T(8,128)} %get-tuple-element.24.refs_0_.refs_4_.refs_1_), channel_id=1, source_target_pairs={{0,248},{8,0},{16,8},{24,16},{32,24},{40,32},{48,40},{56,48},{64,5... | collective-permute-start | bytes 1572872 | tf_op jit(solution)/shard_map/ppermute | solution.py:617
  14.9 4.1 %pack.1 = (f32[136,1024]{1,0:T(8,128)}, f32[136,1024]{1,0:T(8,128)}, f32[136,384]{1,0:T(8,128)}, f32[136,384]{1,0:T(8,128)}, f32[136,640]{1,0:T(8,128)}, /*index=5*/f32[136,640]{1,0:T(8,128)}) custom-call(s32[2,1,1,2]{3,2,1,0:T(1,128)} %count_hbm.3, s32[2,1,1,2,128]{4,3,2,1,0:T(2,128)} %blocks_hbm.3, s32[2,2,64,512]{3,2,1,0:T(8,128)} %shift_hbm.3, ...), custom_call_target="tpu_custom_call" | custom-call | flops 300000000 | bytes 3000000 | tf_op jit(solution)/shard_map/pack/pallas_call | solution.py:262
  22.3 3.5 %collective-permute-start.9 = (f32[136,1024]{1,0:T(8,128)}, f32[136,1024]{1,0:T(8,128)S(1)}, u32[]{:S(2)}, u32[]{:S(2)}) collective-permute-start(f32[136,1024]{1,0:T(8,128)} %get-tuple-element.29.refs_2_.refs_5_), channel_id=1, source_target_pairs={{0,8},{8,16},{16,24},{24,32},{32,40},{40,48},{48,56},{56,64},{64,7... | collective-permute-start | bytes 1671176 | tf_op jit(solution)/shard_map/ppermute | solution.py:640
  25.9 10.3 %collective-permute-done.13 = f32[136,384]{1,0:T(8,128)S(1)} collective-permute-done((f32[136,384]{1,0:T(8,128)}, f32[136,384]{1,0:T(8,128)S(1)}, u32[]{:S(2)}, u32[]{:S(2)}) %collective-permute-start.13) | collective-permute-done | bytes 208928 | tf_op jit(solution)/shard_map/ppermute | solution.py:642
  38.2 4.7 %first.2 = (f32[3,2,64,512]{3,2,1,0:T(8,128)S(1)}, f32[4,1024,128]{2,1,0:T(8,128)S(1)}, f32[25,512]{1,0:T(8,128)S(1)}) custom-call(f32[4,64,512]{2,1,0:T(8,128)S(1)} %copy-done.3, f32[4,64,512]{2,1,0:T(8,128)S(1)} %copy-done.4, f32[4,64,512]{2,1,0:T(8,128)S(1)} %collective-permute-done.refs_2_.refs_6_.refs_3_, ...), custom_call_target="tpu_custom_call" | custom-call | flops 3000000000 | bytes 8000000 | tf_op jit(solution)/shard_map/first/pallas_call | solution.py:442
  42.9 1.7 %collective-permute-start.3 = (f32[25,512]{1,0:T(8,128)S(1)}, f32[25,512]{1,0:T(8,128)S(1)}, u32[]{:S(2)}, u32[]{:S(2)}) collective-permute-start(f32[25,512]{1,0:T(8,128)S(1)} %get-tuple-element.26.refs_0_), channel_id=1, source_target_pairs={{0,2},{1,3},{2,0},{3,1},{4,6},{5,7},{6,4},{7,5},{8,10},{9,11},{10,... | collective-permute-start | bytes 153608 | tf_op jit(solution)/shard_map/ppermute | solution.py:648
  44.5 5.7 %collective-permute-done.11.refs_6_ = f32[136,384]{1,0:T(8,128)S(1)} collective-permute-done((f32[136,384]{1,0:T(8,128)S(1)}, f32[136,384]{1,0:T(8,128)S(1)}, u32[]{:S(2)}, u32[]{:S(2)}) %collective-permute-start.11) | collective-permute-done | bytes 208928 | tf_op jit(solution)/shard_map/ppermute | solution.py:643
  50.3 7.4 %collective-permute-start.5 = (f32[25,512]{1,0:T(8,128)S(1)}, f32[25,512]{1,0:T(8,128)S(1)}, u32[]{:S(2)}, u32[]{:S(2)}) collective-permute-start(f32[25,512]{1,0:T(8,128)S(1)} %get-tuple-element.26.refs_0_), channel_id=1, source_target_pairs={{0,4},{1,5},{2,6},{3,7},{4,0},{5,1},{6,2},{7,3},{8,12},{9,13},{10,... | collective-permute-start | bytes 153608 | tf_op jit(solution)/shard_map/ppermute | solution.py:648
  57.7 2.9 %collective-permute-start.2 = (f32[25,512]{1,0:T(8,128)S(1)}, f32[25,512]{1,0:T(8,128)S(1)}, u32[]{:S(2)}, u32[]{:S(2)}) collective-permute-start(f32[25,512]{1,0:T(8,128)S(1)} %get-tuple-element.26.refs_0_), channel_id=1, source_target_pairs={{0,1},{1,0},{2,3},{3,2},{4,5},{5,4},{6,7},{7,6},{8,9},{9,8},{10,11... | collective-permute-start | bytes 153608 | tf_op jit(solution)/shard_map/ppermute | solution.py:648
  61.5 1.4 %collective-permute-done.7.refs_6_ = f32[25,512]{1,0:T(8,128)S(1)} collective-permute-done((f32[25,512]{1,0:T(8,128)S(1)}, f32[25,512]{1,0:T(8,128)S(1)}, u32[]{:S(2)}, u32[]{:S(2)}) %collective-permute-start.7) | collective-permute-done | bytes 51232 | tf_op jit(solution)/shard_map/ppermute | solution.py:648
  62.9 1.7 %collective-permute-start.8 = (f32[25,512]{1,0:T(8,128)S(1)}, f32[25,512]{1,0:T(8,128)S(1)}, u32[]{:S(2)}, u32[]{:S(2)}) collective-permute-start(f32[25,512]{1,0:T(8,128)S(1)} %collective-permute-done.7.refs_6_), channel_id=1, source_target_pairs={{0,1},{1,0},{2,3},{3,2},{4,5},{5,4},{6,7},{7,6},{8,9},{9,8},{10,11... | collective-permute-start | bytes 153608 | tf_op jit(solution)/shard_map/ppermute | solution.py:648
  65.5 2.7 %omega.2.refs_10_ = f32[3,2,64,512]{3,2,1,0:T(8,128)S(1)} custom-call(f32[2,3,2,64,512]{4,3,2,1,0:T(8,128)S(1)} %copy-done, f32[4,64,512]{2,1,0:T(8,128)S(1)} %copy-done.3, f32[4,64,512]{2,1,0:T(8,128)S(1)} %copy-done.4, f32[4,64,512]{2,1,0:T(8,128)S(1)} %collective-permute-done.refs_2_.refs_6_.refs_3_, ...), custom_call_target="tpu_custom_call" | custom-call | flops 300000000 | bytes 6000000 | tf_op jit(solution)/shard_map/omega/pallas_call | solution.py:350
  69.6 3.0 %second.2 = (f32[3,64,512]{2,1,0:T(8,128)S(1)}, f32[3,64,512]{2,1,0:T(8,128)S(1)}) custom-call(f32[25,512]{1,0:T(8,128)S(1)} %get-tuple-element.26.refs_0_, f32[25,512]{1,0:T(8,128)S(1)} %collective-permute-done.2.refs_1_, f32[25,512]{1,0:T(8,128)S(1)} %collective-permute-done.3.refs_2_, f32[25,512]{1,0:T(8,128)S(1)} %collective-permute-done.4.refs_3_, ...), custom_call_target="tpu_custom_call" | custom-call | flops 4000000000 | bytes 8000000 | tf_op jit(solution)/shard_map/second/pallas_call | solution.py:600
  72.7 9.6 %collective-permute-start.16 = (f32[3,64,512]{2,1,0:T(8,128)S(1)}, f32[3,64,512]{2,1,0:T(8,128)S(1)}, u32[]{:S(2)}, u32[]{:S(2)}) collective-permute-start(f32[3,64,512]{2,1,0:T(8,128)S(1)} %get-tuple-element.33.refs_0_), channel_id=1, source_target_pairs={{0,248},{8,0},{16,8},{24,16},{32,24},{40,32},{48,40},{56,48},{64,5... | collective-permute-start | bytes 1179656 | tf_op jit(solution)/shard_map/ppermute | solution.py:617
  83.6 2.1 %collective-permute-done.19 = f32[136,640]{1,0:T(8,128)S(1)} collective-permute-done((f32[136,640]{1,0:T(8,128)S(1)}, f32[136,640]{1,0:T(8,128)S(1)}, u32[]{:S(2)}, u32[]{:S(2)}) %collective-permute-start.19) | collective-permute-done | bytes 348192 | tf_op jit(solution)/shard_map/ppermute | solution.py:642
  86.4 14.9 %collective-permute-done.18.refs_4_.refs_8_.refs_7_ = f32[136,640]{1,0:T(8,128)S(1)} collective-permute-done((f32[136,640]{1,0:T(8,128)S(1)}, f32[136,640]{1,0:T(8,128)S(1)}, u32[]{:S(2)}, u32[]{:S(2)}) %collective-permute-start.18) | collective-permute-done | bytes 348192 | tf_op jit(solution)/shard_map/ppermute | solution.py:643
  101.3 2.7 %omega.3.refs_10_ = f32[3,2,64,512]{3,2,1,0:T(8,128)S(1)} custom-call(f32[2,3,2,64,512]{4,3,2,1,0:T(8,128)S(1)} %copy-done, f32[136,1024]{1,0:T(8,128)S(1)} %copy-done.1, f32[136,1024]{1,0:T(8,128)S(1)} %copy-done.2, f32[136,1024]{1,0:T(8,128)S(1)} %collective-permute-done.9.refs_5_.refs_3_.refs_7_.refs_6_, ...), custom_call_target="tpu_custom_call" | custom-call | flops 300000000 | bytes 6000000 | tf_op jit(solution)/shard_map/omega/pallas_call | solution.py:350
  104.0 4.8 %first.3 = (f32[3,2,64,512]{3,2,1,0:T(8,128)S(1)}, f32[4,1024,128]{2,1,0:T(8,128)S(1)}, f32[25,512]{1,0:T(8,128)S(1)}) custom-call(f32[3,64,512]{2,1,0:T(8,128)S(1)} %get-tuple-element.33.refs_0_, f32[3,64,512]{2,1,0:T(8,128)S(1)} %get-tuple-element.34.refs_1_, f32[3,64,512]{2,1,0:T(8,128)S(1)} %collective-permute-done.15.refs_2_, ...), custom_call_target="tpu_custom_call" | custom-call | flops 3000000000 | bytes 8000000 | tf_op jit(solution)/shard_map/first/pallas_call | solution.py:442
  108.9 6.1 %collective-permute-start.22 = (f32[25,512]{1,0:T(8,128)S(1)}, f32[25,512]{1,0:T(8,128)S(1)}, u32[]{:S(2)}, u32[]{:S(2)}) collective-permute-start(f32[25,512]{1,0:T(8,128)S(1)} %get-tuple-element.39.refs_0_), channel_id=1, source_target_pairs={{0,2},{1,3},{2,0},{3,1},{4,6},{5,7},{6,4},{7,5},{8,10},{9,11},{10,... | collective-permute-start | bytes 153608 | tf_op jit(solution)/shard_map/ppermute | solution.py:648
  117.1 2.2 %collective-permute-start.21 = (f32[25,512]{1,0:T(8,128)S(1)}, f32[25,512]{1,0:T(8,128)S(1)}, u32[]{:S(2)}, u32[]{:S(2)}) collective-permute-start(f32[25,512]{1,0:T(8,128)S(1)} %get-tuple-element.39.refs_0_), channel_id=1, source_target_pairs={{0,1},{1,0},{2,3},{3,2},{4,5},{5,4},{6,7},{7,6},{8,9},{9,8},{10,11... | collective-permute-start | bytes 153608 | tf_op jit(solution)/shard_map/ppermute | solution.py:648
  119.7 4.2 %collective-permute-start.25 = (f32[25,512]{1,0:T(8,128)S(1)}, f32[25,512]{1,0:T(8,128)S(1)}, u32[]{:S(2)}, u32[]{:S(2)}) collective-permute-start(f32[25,512]{1,0:T(8,128)S(1)} %collective-permute-done.24.refs_4_), channel_id=1, source_target_pairs={{0,1},{1,0},{2,3},{3,2},{4,5},{5,4},{6,7},{7,6},{8,9},{9,8},{10,11... | collective-permute-start | bytes 153608 | tf_op jit(solution)/shard_map/ppermute | solution.py:648
  125.1 3.8 %second.3 = f32[3,2,64,512]{3,2,1,0:T(8,128)} custom-call(f32[25,512]{1,0:T(8,128)S(1)} %get-tuple-element.39.refs_0_, f32[25,512]{1,0:T(8,128)S(1)} %collective-permute-done.21.refs_1_, f32[25,512]{1,0:T(8,128)S(1)} %collective-permute-done.22.refs_2_, f32[25,512]{1,0:T(8,128)S(1)} %collective-permute-done.23.refs_3_, ...), custom_call_target="tpu_custom_call" | custom-call | flops 4000000000 | bytes 8000000 | tf_op jit(solution)/shard_map/second/pallas_call | solution.py:600
  (60 shorter events, 14.2 us)
Async XLA Ops:
  2.4 35.1 %collective-permute-start = (f32[4,64,512]{2,1,0:T(8,128)}, f32[4,64,512]{2,1,0:T(8,128)S(1)}, u32[]{:S(2)}, u32[]{:S(2)}) collective-permute-start(f32[4,64,512]{2,1,0:T(8,128)} %get-tuple-element.25.refs_1_.refs_5_.refs_2_), channel_id=1, source_target_pairs={{0,8},{8,16},{16,24},{24,32},{32,40},{40,48},{48,56},{56,64},{64,7... | collective-permute-start | bytes 1572872 | tf_op jit(solution)/shard_map/ppermute | solution.py:617
  4.5 33.6 %collective-permute-start.1 = (f32[4,64,512]{2,1,0:T(8,128)}, f32[4,64,512]{2,1,0:T(8,128)S(1)}, u32[]{:S(2)}, u32[]{:S(2)}) collective-permute-start(f32[4,64,512]{2,1,0:T(8,128)} %get-tuple-element.24.refs_0_.refs_4_.refs_1_), channel_id=1, source_target_pairs={{0,248},{8,0},{16,8},{24,16},{32,24},{40,32},{48,40},{56,48},{64,5... | collective-permute-start | bytes 1572872 | tf_op jit(solution)/shard_map/ppermute | solution.py:617
  19.7 38.0 %collective-permute-start.12 = (f32[136,1024]{1,0:T(8,128)}, f32[136,1024]{1,0:T(8,128)S(1)}, u32[]{:S(2)}, u32[]{:S(2)}) collective-permute-start(f32[136,1024]{1,0:T(8,128)} %get-tuple-element.31.refs_1_.refs_4_), channel_id=1, source_target_pairs={{8,0},{16,8},{24,16},{32,24},{40,32},{48,40},{56,48},{64,56},{72,6... | collective-permute-start | bytes 1671176 | tf_op jit(solution)/shard_map/ppermute | solution.py:640
  21.0 15.1 %collective-permute-start.13 = (f32[136,384]{1,0:T(8,128)}, f32[136,384]{1,0:T(8,128)S(1)}, u32[]{:S(2)}, u32[]{:S(2)}) collective-permute-start(f32[136,384]{1,0:T(8,128)} %get-tuple-element.32), channel_id=1, source_target_pairs={{128,152},{0,24},{129,153},{1,25},{130,154},{2,26},{131,155},{3,27... | collective-permute-start | bytes 626696 | tf_op jit(solution)/shard_map/ppermute | solution.py:642
  22.3 42.3 %collective-permute-start.9 = (f32[136,1024]{1,0:T(8,128)}, f32[136,1024]{1,0:T(8,128)S(1)}, u32[]{:S(2)}, u32[]{:S(2)}) collective-permute-start(f32[136,1024]{1,0:T(8,128)} %get-tuple-element.29.refs_2_.refs_5_), channel_id=1, source_target_pairs={{0,8},{8,16},{16,24},{24,32},{32,40},{40,48},{48,56},{56,64},{64,7... | collective-permute-start | bytes 1671176 | tf_op jit(solution)/shard_map/ppermute | solution.py:640
  36.1 14.1 %collective-permute-start.11 = (f32[136,384]{1,0:T(8,128)S(1)}, f32[136,384]{1,0:T(8,128)S(1)}, u32[]{:S(2)}, u32[]{:S(2)}) collective-permute-start(f32[136,384]{1,0:T(8,128)S(1)} %collective-permute-done.10), channel_id=1, source_target_pairs={{96,128},{224,0},{97,129},{225,1},{98,130},{226,2},{99,131},{227,3... | collective-permute-start | bytes 626696 | tf_op jit(solution)/shard_map/ppermute | solution.py:643
  37.4 20.3 %collective-permute-start.14 = (f32[136,384]{1,0:T(8,128)S(1)}, f32[136,384]{1,0:T(8,128)S(1)}, u32[]{:S(2)}, u32[]{:S(2)}) collective-permute-start(f32[136,384]{1,0:T(8,128)S(1)} %collective-permute-done.13), channel_id=1, source_target_pairs={{152,120},{24,248},{153,121},{25,249},{154,122},{26,250},{155,123}... | collective-permute-start | bytes 626696 | tf_op jit(solution)/shard_map/ppermute | solution.py:643
  42.9 17.7 %collective-permute-start.3 = (f32[25,512]{1,0:T(8,128)S(1)}, f32[25,512]{1,0:T(8,128)S(1)}, u32[]{:S(2)}, u32[]{:S(2)}) collective-permute-start(f32[25,512]{1,0:T(8,128)S(1)} %get-tuple-element.26.refs_0_), channel_id=1, source_target_pairs={{0,2},{1,3},{2,0},{3,1},{4,6},{5,7},{6,4},{7,5},{8,10},{9,11},{10,... | collective-permute-start | bytes 153608 | tf_op jit(solution)/shard_map/ppermute | solution.py:648
  50.3 10.4 %collective-permute-start.5 = (f32[25,512]{1,0:T(8,128)S(1)}, f32[25,512]{1,0:T(8,128)S(1)}, u32[]{:S(2)}, u32[]{:S(2)}) collective-permute-start(f32[25,512]{1,0:T(8,128)S(1)} %get-tuple-element.26.refs_0_), channel_id=1, source_target_pairs={{0,4},{1,5},{2,6},{3,7},{4,0},{5,1},{6,2},{7,3},{8,12},{9,13},{10,... | collective-permute-start | bytes 153608 | tf_op jit(solution)/shard_map/ppermute | solution.py:648
  57.7 5.2 %collective-permute-start.7 = (f32[25,512]{1,0:T(8,128)S(1)}, f32[25,512]{1,0:T(8,128)S(1)}, u32[]{:S(2)}, u32[]{:S(2)}) collective-permute-start(f32[25,512]{1,0:T(8,128)S(1)} %get-tuple-element.26.refs_0_), channel_id=1, source_target_pairs={{0,6},{1,7},{2,4},{3,5},{4,2},{5,3},{6,0},{7,1},{8,14},{9,15},{10,... | collective-permute-start | bytes 153608 | tf_op jit(solution)/shard_map/ppermute | solution.py:648
  57.7 10.5 %collective-permute-start.2 = (f32[25,512]{1,0:T(8,128)S(1)}, f32[25,512]{1,0:T(8,128)S(1)}, u32[]{:S(2)}, u32[]{:S(2)}) collective-permute-start(f32[25,512]{1,0:T(8,128)S(1)} %get-tuple-element.26.refs_0_), channel_id=1, source_target_pairs={{0,1},{1,0},{2,3},{3,2},{4,5},{5,4},{6,7},{7,6},{8,9},{9,8},{10,11... | collective-permute-start | bytes 153608 | tf_op jit(solution)/shard_map/ppermute | solution.py:648
  60.6 9.0 %collective-permute-start.4 = (f32[25,512]{1,0:T(8,128)S(1)}, f32[25,512]{1,0:T(8,128)S(1)}, u32[]{:S(2)}, u32[]{:S(2)}) collective-permute-start(f32[25,512]{1,0:T(8,128)S(1)} %collective-permute-done.3.refs_2_), channel_id=1, source_target_pairs={{0,1},{1,0},{2,3},{3,2},{4,5},{5,4},{6,7},{7,6},{8,9},{9,8},{10,11... | collective-permute-start | bytes 153608 | tf_op jit(solution)/shard_map/ppermute | solution.py:648
  60.7 8.9 %collective-permute-start.6 = (f32[25,512]{1,0:T(8,128)S(1)}, f32[25,512]{1,0:T(8,128)S(1)}, u32[]{:S(2)}, u32[]{:S(2)}) collective-permute-start(f32[25,512]{1,0:T(8,128)S(1)} %collective-permute-done.5.refs_4_), channel_id=1, source_target_pairs={{0,1},{1,0},{2,3},{3,2},{4,5},{5,4},{6,7},{7,6},{8,9},{9,8},{10,11... | collective-permute-start | bytes 153608 | tf_op jit(solution)/shard_map/ppermute | solution.py:648
  62.9 6.7 %collective-permute-start.8 = (f32[25,512]{1,0:T(8,128)S(1)}, f32[25,512]{1,0:T(8,128)S(1)}, u32[]{:S(2)}, u32[]{:S(2)}) collective-permute-start(f32[25,512]{1,0:T(8,128)S(1)} %collective-permute-done.7.refs_6_), channel_id=1, source_target_pairs={{0,1},{1,0},{2,3},{3,2},{4,5},{5,4},{6,7},{7,6},{8,9},{9,8},{10,11... | collective-permute-start | bytes 153608 | tf_op jit(solution)/shard_map/ppermute | solution.py:648
  64.7 17.6 %collective-permute-start.17 = (f32[136,640]{1,0:T(8,128)S(1)}, f32[136,640]{1,0:T(8,128)S(1)}, u32[]{:S(2)}, u32[]{:S(2)}) collective-permute-start(f32[136,640]{1,0:T(8,128)S(1)} %copy-done.9), channel_id=1, source_target_pairs={{120,96},{248,224},{121,97},{249,225},{122,98},{250,226},{123,99},... | collective-permute-start | bytes 1044488 | tf_op jit(solution)/shard_map/ppermute | solution.py:642
  68.2 17.5 %collective-permute-start.19 = (f32[136,640]{1,0:T(8,128)S(1)}, f32[136,640]{1,0:T(8,128)S(1)}, u32[]{:S(2)}, u32[]{:S(2)}) collective-permute-start(f32[136,640]{1,0:T(8,128)S(1)} %copy-done.8), channel_id=1, source_target_pairs={{128,152},{0,24},{129,153},{1,25},{130,154},{2,26},{131,155},{3,27... | collective-permute-start | bytes 1044488 | tf_op jit(solution)/shard_map/ppermute | solution.py:642
  72.6 31.4 %collective-permute-start.15 = (f32[3,64,512]{2,1,0:T(8,128)S(1)}, f32[3,64,512]{2,1,0:T(8,128)S(1)}, u32[]{:S(2)}, u32[]{:S(2)}) collective-permute-start(f32[3,64,512]{2,1,0:T(8,128)S(1)} %get-tuple-element.34.refs_1_), channel_id=1, source_target_pairs={{0,8},{8,16},{16,24},{24,32},{32,40},{40,48},{48,56},{56,64},{64,7... | collective-permute-start | bytes 1179656 | tf_op jit(solution)/shard_map/ppermute | solution.py:617
  72.7 31.4 %collective-permute-start.16 = (f32[3,64,512]{2,1,0:T(8,128)S(1)}, f32[3,64,512]{2,1,0:T(8,128)S(1)}, u32[]{:S(2)}, u32[]{:S(2)}) collective-permute-start(f32[3,64,512]{2,1,0:T(8,128)S(1)} %get-tuple-element.33.refs_0_), channel_id=1, source_target_pairs={{0,248},{8,0},{16,8},{24,16},{32,24},{40,32},{48,40},{56,48},{64,5... | collective-permute-start | bytes 1179656 | tf_op jit(solution)/shard_map/ppermute | solution.py:617
  82.3 19.0 %collective-permute-start.18 = (f32[136,640]{1,0:T(8,128)S(1)}, f32[136,640]{1,0:T(8,128)S(1)}, u32[]{:S(2)}, u32[]{:S(2)}) collective-permute-start(f32[136,640]{1,0:T(8,128)S(1)} %collective-permute-done.17), channel_id=1, source_target_pairs={{96,128},{224,0},{97,129},{225,1},{98,130},{226,2},{99,131},{227,3... | collective-permute-start | bytes 1044488 | tf_op jit(solution)/shard_map/ppermute | solution.py:643
  85.7 15.6 %collective-permute-start.20 = (f32[136,640]{1,0:T(8,128)S(1)}, f32[136,640]{1,0:T(8,128)S(1)}, u32[]{:S(2)}, u32[]{:S(2)}) collective-permute-start(f32[136,640]{1,0:T(8,128)S(1)} %collective-permute-done.19), channel_id=1, source_target_pairs={{152,120},{24,248},{153,121},{25,249},{154,122},{26,250},{155,123}... | collective-permute-start | bytes 1044488 | tf_op jit(solution)/shard_map/ppermute | solution.py:643
  108.9 10.4 %collective-permute-start.22 = (f32[25,512]{1,0:T(8,128)S(1)}, f32[25,512]{1,0:T(8,128)S(1)}, u32[]{:S(2)}, u32[]{:S(2)}) collective-permute-start(f32[25,512]{1,0:T(8,128)S(1)} %get-tuple-element.39.refs_0_), channel_id=1, source_target_pairs={{0,2},{1,3},{2,0},{3,1},{4,6},{5,7},{6,4},{7,5},{8,10},{9,11},{10,... | collective-permute-start | bytes 153608 | tf_op jit(solution)/shard_map/ppermute | solution.py:648
  115.8 8.1 %collective-permute-start.26 = (f32[25,512]{1,0:T(8,128)S(1)}, f32[25,512]{1,0:T(8,128)S(1)}, u32[]{:S(2)}, u32[]{:S(2)}) collective-permute-start(f32[25,512]{1,0:T(8,128)S(1)} %get-tuple-element.39.refs_0_), channel_id=1, source_target_pairs={{0,6},{1,7},{2,4},{3,5},{4,2},{5,3},{6,0},{7,1},{8,14},{9,15},{10,... | collective-permute-start | bytes 153608 | tf_op jit(solution)/shard_map/ppermute | solution.py:648
  117.1 6.7 %collective-permute-start.21 = (f32[25,512]{1,0:T(8,128)S(1)}, f32[25,512]{1,0:T(8,128)S(1)}, u32[]{:S(2)}, u32[]{:S(2)}) collective-permute-start(f32[25,512]{1,0:T(8,128)S(1)} %get-tuple-element.39.refs_0_), channel_id=1, source_target_pairs={{0,1},{1,0},{2,3},{3,2},{4,5},{5,4},{6,7},{7,6},{8,9},{9,8},{10,11... | collective-permute-start | bytes 153608 | tf_op jit(solution)/shard_map/ppermute | solution.py:648
  119.7 5.1 %collective-permute-start.25 = (f32[25,512]{1,0:T(8,128)S(1)}, f32[25,512]{1,0:T(8,128)S(1)}, u32[]{:S(2)}, u32[]{:S(2)}) collective-permute-start(f32[25,512]{1,0:T(8,128)S(1)} %collective-permute-done.24.refs_4_), channel_id=1, source_target_pairs={{0,1},{1,0},{2,3},{3,2},{4,5},{5,4},{6,7},{7,6},{8,9},{9,8},{10,11... | collective-permute-start | bytes 153608 | tf_op jit(solution)/shard_map/ppermute | solution.py:648
  (14 other events, 319.1 us)
